TPU v7x, 128 devices: a whole 4x4x4 slice. The times are simulated.
128 devices in a mesh: ap: 32 (over y, x_hi, z), rg: 4 (over x_lo, core).
Axes of the slice: x: 4 (x_hi: 2, x_lo: 2; x = x_hi * 2 + x_lo), y: 4, z: 4, core: 2. Of those that a mesh axis runs over, the one named last changes fastest.
Arguments:
- raw_echoes: bfloat16 [2, 8192, 4096], P(None, 'ap', 'rg'), may hold values from -6 to 6
- chirp: float32 [2, 128], replicated, may hold values from -0.375 to 0.375
- range_offsets: int32 [8, 2, 4096], P(None, None, 'rg'), may hold values from 0 to 7
- phases: float32 [8, 2, 4096], P(None, None, 'rg'), may hold values from -3.140625 to 3.140625
- tile_table: int32 [1024, 16], replicated, may hold values from 0 to 16383, as said below
Outputs:
- image: float32 [2, 8192, 4096], P(None, 'ap', 'rg')
Inputs may be any that keep to these rules, and one draw needn't show every extreme that they name: `tile_table`: all entries differ (a permutation of tile indices). The tiles that lie in one device's block of the image (256 pulses by 1024 range bins) go to tiles of distinct devices' blocks, one to each device. The same holds for each set of tiles whose tile rows u share one value of u mod (32) and whose columns lie in one device's range bins.
All inputs are finite; a program needn't handle non-finite values.
Results may differ from a plain program's by a relative error of at most 0.0029.
Values may be sent and summed in bfloat16 or wider, within the bound.
No kernel may reach another device: no remote copies, remote signals or barrier semaphores. Data moves between devices by JAX's collectives and lax.ppermute only.
A program may use at most 64 MiB of HBM per device.

v0:
```python
import functools
import math

import jax
import jax.numpy as jnp
from jax import lax
from jax.experimental import pallas as pl
from jax.experimental.pallas import tpu as pltpu
from jax.sharding import PartitionSpec as P

ROOT_HALF = 0.7071067811865476
LANES = 128
STEP = 8
LEAD = 64
VMEM = pltpu.VMEM
BF16 = jnp.bfloat16
F32 = jnp.float32


def whole(count):
    return [pl.BlockSpec(memory_space=VMEM)] * count


def split_three(values):
    high = values.astype(BF16)
    rest = values - high.astype(F32)
    middle = rest.astype(BF16)
    low = (rest - middle.astype(F32)).astype(BF16)
    return high, middle, low


def rim_kernel(raw_ref, offset_ref, phase_ref, left_ref, right_ref):
    pulses, width = raw_ref.shape[1], raw_ref.shape[2]
    rows = offset_ref.shape[0]
    for out_ref, start in ((left_ref, 0), (right_ref, width - LANES)):
        cut = slice(start, start + LANES)
        out_ref[:pulses] = raw_ref[0, :, cut]
        out_ref[pulses : 2 * pulses] = raw_ref[1, :, cut]
        at = 2 * pulses
        out_ref[at : at + rows] = offset_ref[:, cut].astype(F32).astype(BF16)
        for part in split_three(phase_ref[:, cut]):
            at += rows
            out_ref[at : at + rows] = part


def toeplitz_kernel(chirp_ref, table_ref):
    taps = chirp_ref[...].astype(BF16).astype(F32)
    zeros = jnp.zeros((1, LANES), F32)
    rolled = []
    for part in range(2):
        row = jnp.concatenate([taps[part : part + 1], zeros], axis=1)
        spread = jnp.broadcast_to(row, (LANES, 2 * LANES))
        rolled.append(pltpu.roll(spread, 0, 1, stride=1, stride_axis=0))
    real, imag = rolled
    table_ref[0] = jnp.concatenate([real, -imag], axis=0).astype(BF16)
    table_ref[1] = jnp.concatenate([imag, real], axis=0).astype(BF16)


def steering_kernel(total, offset_ref, phase_ref, left_ref, right_ref, trig_ref, index_ref):
    rows, width = offset_ref.shape
    columns = index_ref.shape[1]
    base = left_ref.shape[0] - 4 * rows
    start = lax.axis_index("rg") * width - LANES

    def rim(ref):
        parts = [
            ref[base + k * rows : base + (k + 1) * rows, :].astype(F32) for k in range(4)
        ]
        return parts[0].astype(jnp.int32), parts[1] + parts[2] + parts[3]

    left_offset, left_phase = rim(left_ref)
    right_offset, right_phase = rim(right_ref)
    offsets = jnp.concatenate([left_offset, offset_ref[...], right_offset], axis=1)
    angles = jnp.concatenate([left_phase, phase_ref[...], right_phase], axis=1)
    padded = width + 2 * LANES
    bins = start + lax.broadcasted_iota(jnp.int32, (rows, padded), 1)
    inside = (bins >= 0) & (bins < total)
    cosine = jnp.where(inside, jnp.cos(angles) * ROOT_HALF, 0.0)
    sine = jnp.where(inside, jnp.sin(angles) * ROOT_HALF, 0.0)
    lane = lax.broadcasted_iota(jnp.int32, (2, columns), 1) % LANES
    for level in range(rows // 2):
        shift = padded - (LANES - LEAD + STEP * (level + 1))
        pick = slice(2 * level, 2 * level + 2)

        def moved(values):
            return pltpu.roll(values, shift, 1)[pick, :columns]

        trig_ref[0, pick] = moved(cosine)
        trig_ref[1, pick] = moved(sine)
        index_ref[pick] = lane + (STEP - 4) + moved(offsets)


def row_of(ref, lead, row, lanes, rows):
    return jnp.broadcast_to(ref[lead + (slice(row, row + 1), lanes)], (rows, LANES))


def steering(trig_ref, index_ref, level, lanes, rows):
    sides = []
    for side in range(2):
        row = 2 * level + side
        index = row_of(index_ref, (), row, lanes, rows)
        sides.append(
            (
                index & (LANES - 1),
                index >= LANES,
                row_of(trig_ref, (0,), row, lanes, rows),
                row_of(trig_ref, (1,), row, lanes, rows),
            )
        )
    return sides


def gathered(values, index):
    return jnp.take_along_axis(values, index, axis=1, mode="promise_in_bounds")


def term_of(here, following, side):
    index, beyond, cosine, sine = side
    real, imag = (
        jnp.where(beyond, gathered(b, index), gathered(a, index))
        for a, b in zip(here, following)
    )
    return real * cosine - imag * sine, real * sine + imag * cosine


def first_merges_kernel(
    levels, total, raw_ref, left_ref, right_ref, table_ref, trig_ref, index_ref, out_ref, field_ref
):
    pulses, width = raw_ref.shape[1], raw_ref.shape[2]
    blocks = out_ref.shape[2] // LANES
    start = lax.axis_index("rg") * width - LEAD
    dims = (((1,), (1,)), ((), ()))
    for block in range(blocks):
        parts = []
        for part in range(2):
            tiles = []
            for tile in (block, block + 1):
                if tile == 0:
                    tiles.append(left_ref[part * pulses : (part + 1) * pulses, :])
                elif tile == blocks:
                    tiles.append(right_ref[part * pulses : (part + 1) * pulses, :])
                else:
                    tiles.append(raw_ref[part, :, (tile - 1) * LANES : tile * LANES])
            parts.append(
                lax.dot_general(
                    jnp.concatenate(tiles, axis=1),
                    table_ref[part],
                    dims,
                    preferred_element_type=F32,
                )
            )
        both = parts[0] + parts[1]
        if block in (0, blocks - 1):
            bins = start + block * LANES + (
                lax.broadcasted_iota(jnp.int32, both.shape, 1) % LANES
            )
            both = jnp.where((bins >= 0) & (bins < total), both, 0.0)
        lanes = slice(block * LANES, (block + 1) * LANES)
        field_ref[0, :, lanes] = both[:, :LANES]
        field_ref[1, :, lanes] = both[:, LANES:]
    for part in range(2):
        field_ref[part, :, blocks * LANES :] = jnp.zeros((pulses, LANES), F32)

    chunk = 16
    for level in range(levels):
        distance = (pulses >> levels) << level
        last = level == levels - 1

        def merge_block(block, carry, level=level, distance=distance, last=last):
            at = pl.multiple_of(block * LANES, LANES)
            lanes = pl.ds(at, LANES)
            beyond = pl.ds(pl.multiple_of(at + LANES, LANES), LANES)
            sides = steering(trig_ref, index_ref, level, lanes, chunk)
            for first in range(0, pulses, chunk):
                if first & distance:
                    continue
                terms = []
                for side in range(2):
                    rows = pl.ds(first + side * distance, chunk)
                    here = [field_ref[part, rows, lanes] for part in range(2)]
                    following = [field_ref[part, rows, beyond] for part in range(2)]
                    terms.append(term_of(here, following, sides[side]))
                for side in range(2):
                    row = first + side * distance
                    merged = [
                        terms[0][part] + terms[1][part]
                        if side == 0
                        else terms[0][part] - terms[1][part]
                        for part in range(2)
                    ]
                    if last:
                        for tile in range(chunk // 8):
                            cut = slice(tile * 8, tile * 8 + 8)
                            out_ref[row // 8 + tile, :, lanes] = jnp.concatenate(
                                [merged[0][cut], merged[1][cut]], axis=0
                            ).astype(BF16)
                    else:
                        for part in range(2):
                            field_ref[part, pl.ds(row, chunk), lanes] = merged[part]
            return carry

        lax.fori_loop(0, blocks, merge_block, 0)


def last_merges_kernel(
    skipped, target_ref, moved_ref, trig_ref, index_ref, out_ref, field_ref
):
    holders, _, columns = moved_ref.shape
    blocks = columns // LANES
    out_blocks = out_ref.shape[0] // holders * out_ref.shape[2] // LANES
    per_tile = out_ref.shape[2] // LANES
    tiles_across = out_blocks // per_tile
    levels = holders.bit_length() - 1
    for holder in range(holders):
        field_ref[holder, :, blocks * LANES :] = jnp.zeros((16, LANES), F32)
        for block in range(blocks):
            lanes = slice(block * LANES, (block + 1) * LANES)
            field_ref[holder, :, lanes] = moved_ref[holder, :, lanes].astype(F32)

    for level in range(levels):
        distance = 1 << level
        last = level == levels - 1

        def merge_block(block, carry, level=level, distance=distance, last=last):
            at = pl.multiple_of(block * LANES, LANES)
            lanes = pl.ds(at, LANES)
            beyond = pl.ds(pl.multiple_of(at + LANES, LANES), LANES)
            sides = steering(trig_ref, index_ref, skipped + level, lanes, 8)
            for first in range(holders):
                if first & distance:
                    continue
                terms = []
                for side in range(2):
                    holder = first + side * distance
                    here = [field_ref[holder, 8 * part : 8 * part + 8, lanes] for part in range(2)]
                    following = [
                        field_ref[holder, 8 * part : 8 * part + 8, beyond] for part in range(2)
                    ]
                    terms.append(term_of(here, following, sides[side]))
                for side in range(2):
                    holder = first + side * distance
                    merged = jnp.concatenate(
                        [
                            terms[0][part] + terms[1][part]
                            if side == 0
                            else terms[0][part] - terms[1][part]
                            for part in range(2)
                        ],
                        axis=0,
                    )
                    if last:
                        to = target_ref[holder * tiles_across + block // per_tile]
                        inner = pl.multiple_of(block % per_tile * LANES, LANES)
                        out_ref[to, :, pl.ds(inner, LANES)] = merged.astype(BF16)
                    else:
                        field_ref[holder, :, lanes] = merged
            return carry

        lax.fori_loop(0, out_blocks if last else blocks, merge_block, 0)


def place_kernel(source_ref, incoming_ref, out_ref):
    rows = out_ref.shape[1]
    tile_bins = incoming_ref.shape[2]
    across = out_ref.shape[2] // tile_bins
    base = pl.program_id(0) * (rows // 8) * across
    for row in range(rows // 8):
        for column in range(across):
            tile = incoming_ref[source_ref[base + row * across + column]].astype(F32)
            for part in range(2):
                out_ref[
                    part, row * 8 : row * 8 + 8, column * tile_bins : (column + 1) * tile_bins
                ] = tile[8 * part : 8 * part + 8]


def per_device(raw_echoes, chirp, range_offsets, phases, tile_table):
    ap_count, rg_count = lax.axis_size("ap"), lax.axis_size("rg")
    devices = ap_count * rg_count
    _, pulses, width = raw_echoes.shape
    level_count = range_offsets.shape[0]
    total = width * rg_count
    outer_levels = ap_count.bit_length() - 1
    inner_levels = level_count - outer_levels
    padded = width + 2 * LANES
    columns = width + LANES
    tile_rows = pulses // ap_count
    tile_bins = width // rg_count
    offset_rows = range_offsets.reshape(2 * level_count, width)
    phase_rows = phases.reshape(2 * level_count, width)
    rim_rows = 2 * pulses + 8 * level_count
    shape = jax.ShapeDtypeStruct

    to_left, to_right = pl.pallas_call(
        rim_kernel,
        out_shape=[shape((rim_rows, LANES), BF16)] * 2,
        in_specs=whole(3),
        out_specs=whole(2),
    )(raw_echoes, offset_rows, phase_rows)
    ends = rg_count - 1
    from_left = lax.ppermute(to_right, "rg", [(i, i + 1) for i in range(ends)])
    from_right = lax.ppermute(to_left, "rg", [(i + 1, i) for i in range(ends)])
    table = pl.pallas_call(
        toeplitz_kernel,
        out_shape=shape((2, 2 * LANES, 2 * LANES), BF16),
        in_specs=whole(1),
        out_specs=whole(1)[0],
    )(chirp)
    trig, index = pl.pallas_call(
        functools.partial(steering_kernel, total),
        out_shape=[
            shape((2, 2 * level_count, columns), F32),
            shape((2 * level_count, columns), jnp.int32),
        ],
        in_specs=whole(4),
        out_specs=whole(2),
    )(offset_rows, phase_rows, from_left, from_right)
    merged = pl.pallas_call(
        functools.partial(first_merges_kernel, inner_levels, total),
        out_shape=shape((ap_count, 2 * tile_rows, columns), BF16),
        in_specs=whole(6),
        out_specs=whole(1)[0],
        scratch_shapes=[VMEM((2, pulses, padded), F32)],
    )(raw_echoes, from_left, from_right, table, trig, index)
    moved = lax.all_to_all(merged, "ap", split_axis=0, concat_axis=0, tiled=True)

    ap_here, rg_here = lax.axis_index("ap"), lax.axis_index("rg")
    slot_row = tile_table // (rg_count * rg_count)
    slot_col = tile_table % (rg_count * rg_count)
    target = slot_row // ap_count * rg_count + slot_col // rg_count
    shaped = (ap_count, ap_count, rg_count, rg_count)
    target = target.reshape(shaped)
    local_slot = (slot_row % ap_count * rg_count + slot_col % rg_count).reshape(shaped)
    mine = target == ap_here * rg_count + rg_here
    slot_from = jnp.sum(jnp.where(mine, local_slot, 0), axis=(0, 3)).reshape(devices)
    ids = jnp.arange(devices, dtype=jnp.int32)
    source = jnp.sum(
        jnp.where(slot_from[None, :] == ids[:, None], ids[None, :], 0), axis=1
    )
    send_to = lax.dynamic_slice(
        target, (0, ap_here, rg_here, 0), (ap_count, 1, 1, rg_count)
    ).reshape(devices)

    outgoing = pl.pallas_call(
        functools.partial(last_merges_kernel, inner_levels),
        out_shape=shape((devices, 2 * tile_rows, tile_bins), BF16),
        grid_spec=pltpu.PrefetchScalarGridSpec(
            num_scalar_prefetch=1,
            in_specs=whole(3),
            out_specs=whole(1)[0],
            scratch_shapes=[VMEM((ap_count, 2 * tile_rows, padded), F32)],
        ),
    )(send_to, moved, trig, index)
    incoming = lax.all_to_all(outgoing, ("ap", "rg"), split_axis=0, concat_axis=0, tiled=True)
    steps = 8
    return pl.pallas_call(
        place_kernel,
        out_shape=shape((2, pulses, width), F32),
        grid_spec=pltpu.PrefetchScalarGridSpec(
            num_scalar_prefetch=1,
            grid=(steps,),
            in_specs=whole(1),
            out_specs=pl.BlockSpec((2, pulses // steps, width), lambda i, s: (0, i, 0)),
        ),
    )(source, incoming)


def solution(mesh):
    placed = (P(None, "ap", "rg"), P(), P(None, None, "rg"), P(None, None, "rg"), P())
    return jax.shard_map(
        per_device, mesh=mesh, in_specs=placed, out_specs=P(None, "ap", "rg"), check_vma=False
    )
```

profile of v0, /device:TPU:1, one launch (start us, length us, event | category | flops | bytes accessed | tf_op | source)
XLA Modules:
  0.0 148.6 jit_solution(16318222393703940610)
XLA Ops:
  0.0 1.5 %reshape.19.offset_ref = s32[16,1024]{1,0:T(8,128)} reshape(s32[8,2,1024]{2,1,0:T(2,128)} %param.7) | data formatting | bytes 131072 | tf_op jit(solution)/shard_map/reshape | solution.py:288
  1.5 1.5 %reshape.20.phase_ref = f32[16,1024]{1,0:T(8,128)} reshape(f32[8,2,1024]{2,1,0:T(2,128)} %param.8) | data formatting | bytes 131072 | tf_op jit(solution)/shard_map/reshape | solution.py:289
  3.0 2.0 %shard_map.55 = (bf16[576,128]{1,0:T(8,128)(2,1)}, bf16[576,128]{1,0:T(8,128)(2,1)}) custom-call(bf16[2,256,1024]{2,1,0:T(8,128)(2,1)} %raw_ref.3, s32[16,1024]{1,0:T(8,128)} %reshape.19.offset_ref, f32[16,1024]{1,0:T(8,128)} %reshape.20.phase_ref), custom_call_target="tpu_custom_call" | custom-call | tf_op jit(solution)/shard_map/pallas_call | solution.py:293
  5.0 4.5 %collective-permute-start = (bf16[576,128]{1,0:T(8,128)(2,1)}, bf16[576,128]{1,0:T(8,128)(2,1)S(1)}, u32[]{:S(2)}, u32[]{:S(2)}) collective-permute-start(bf16[576,128]{1,0:T(8,128)(2,1)} %get-tuple-element.9), channel_id=1, source_target_pairs={{0,1},{1,2},{2,3},{4,5},{5,6},{6,7},{8,9},{9,10},{10,11},{12,13},{... | collective-permute-start | bytes 442376 | tf_op jit(solution)/shard_map/ppermute | solution.py:300
  9.5 1.9 %collective-permute-start.1 = (bf16[576,128]{1,0:T(8,128)(2,1)}, bf16[576,128]{1,0:T(8,128)(2,1)S(1)}, u32[]{:S(2)}, u32[]{:S(2)}) collective-permute-start(bf16[576,128]{1,0:T(8,128)(2,1)} %get-tuple-element.10), channel_id=1, source_target_pairs={{1,0},{2,1},{3,2},{5,4},{6,5},{7,6},{9,8},{10,9},{11,10},{13,12},{... | collective-permute-start | bytes 442376 | tf_op jit(solution)/shard_map/ppermute | solution.py:301
  11.4 1.5 %shard_map.56.table_ref = bf16[2,256,256]{2,1,0:T(8,128)(2,1)} custom-call(f32[2,128]{1,0:T(2,128)} %chirp_ref.1), custom_call_target="tpu_custom_call" | custom-call | tf_op jit(solution)/shard_map/pallas_call | solution.py:302
  12.9 0.0 collective-permute-done.left_ref
  12.9 0.0 copy-start.2
  12.9 3.2 %collective-permute-done.1.right_ref = bf16[576,128]{1,0:T(8,128)(2,1)S(1)} collective-permute-done((bf16[576,128]{1,0:T(8,128)(2,1)}, bf16[576,128]{1,0:T(8,128)(2,1)S(1)}, u32[]{:S(2)}, u32[]{:S(2)}) %collective-permute-start.1) | collective-permute-done | bytes 147488 | tf_op jit(solution)/shard_map/ppermute | solution.py:301
  16.2 0.0 copy-done.2
  16.2 0.0 copy-start.3
  16.2 0.7 copy-done.3
  16.8 2.2 %shard_map.57 = (f32[2,16,1152]{2,1,0:T(8,128)}, s32[16,1152]{1,0:T(8,128)}) custom-call(s32[16,1024]{1,0:T(8,128)} %reshape.19.offset_ref, f32[16,1024]{1,0:T(8,128)} %reshape.20.phase_ref, bf16[576,128]{1,0:T(8,128)(2,1)} %copy-done.2, bf16[576,128]{1,0:T(8,128)(2,1)} %copy-done.3), custom_call_target="tpu_custom_call" | custom-call | tf_op jit(solution)/shard_map/pallas_call | solution.py:308
  19.1 18.2 %shard_map.58 = bf16[32,16,1152]{2,1,0:T(8,128)(2,1)} custom-call(bf16[2,256,1024]{2,1,0:T(8,128)(2,1)} %raw_ref.3, bf16[576,128]{1,0:T(8,128)(2,1)} %copy-done.2, bf16[576,128]{1,0:T(8,128)(2,1)} %copy-done.3, bf16[2,256,256]{2,1,0:T(8,128)(2,1)} %shard_map.56.table_ref, f32[2,16,1152]{2,1,0:T(8,128)} %get-tuple-element.11.trig_ref, ...), custom_call_target="tpu_custom_call" | custom-call | tf_op jit(solution)/shard_map/pallas_call | solution.py:317
  37.3 0.0 copy-start.4
  37.3 10.3 %all-to-all-start = ((bf16[32,16,1152]{2,1,0:T(8,128)(2,1)}), bf16[32,16,1152]{2,1,0:T(8,128)(2,1)S(1)}, u32[]{:S(2)}, u32[]{:S(2)}) async-start(bf16[32,16,1152]{2,1,0:T(8,128)(2,1)} %shard_map.58), calls=%async_computation | async-start | bytes 2359296 | tf_op jit(solution)/shard_map/all_to_all | solution.py:324
  47.7 0.0 copy-done.4
  47.7 0.2 fusion.1
  47.9 0.1 reshape.16
  48.0 0.1 constant_dynamic-slice_fusion
  48.1 0.3 copy.12
  48.4 0.7 reshape.18.target_ref
  49.1 15.7 %all-to-all-done.moved_ref = bf16[32,16,1152]{2,1,0:T(8,128)(2,1)S(1)} async-done(((bf16[32,16,1152]{2,1,0:T(8,128)(2,1)}), bf16[32,16,1152]{2,1,0:T(8,128)(2,1)S(1)}, u32[]{:S(2)}, u32[]{:S(2)}) %all-to-all-start) | async-done | bytes 1179680 | tf_op jit(solution)/shard_map/all_to_all | solution.py:324
  64.7 0.0 copy-start
  64.7 1.0 copy-done
  65.7 53.4 %shard_map.59 = bf16[128,16,256]{2,1,0:T(8,128)(2,1)} custom-call(s32[128]{0:T(128)} %reshape.18.target_ref, bf16[32,16,1152]{2,1,0:T(8,128)(2,1)} %copy-done, f32[2,16,1152]{2,1,0:T(8,128)} %get-tuple-element.11.trig_ref, s32[16,1152]{1,0:T(8,128)} %get-tuple-element.12.index_ref), custom_call_target="tpu_custom_call" | custom-call | tf_op jit(solution)/shard_map/pallas_call | solution.py:343
  119.1 4.3 %all-to-all-start.1 = ((bf16[128,16,256]{2,1,0:T(8,128)(2,1)}), bf16[128,16,256]{2,1,0:T(8,128)(2,1)S(1)}, u32[]{:S(2)}, u32[]{:S(2)}) async-start(bf16[128,16,256]{2,1,0:T(8,128)(2,1)} %shard_map.59), calls=%async_computation.1 | async-start | bytes 2097152 | tf_op jit(solution)/shard_map/all_to_all | solution.py:353
  123.4 0.1 reshape.17
  123.5 0.1 select_reduce_fusion
  123.6 0.1 copy.10
  123.7 0.1 eq.27
  123.8 0.6 select_reduce_fusion.1.source_ref
  124.4 18.3 %all-to-all-done.1.incoming_ref = bf16[128,16,256]{2,1,0:T(8,128)(2,1)S(1)} async-done(((bf16[128,16,256]{2,1,0:T(8,128)(2,1)}), bf16[128,16,256]{2,1,0:T(8,128)(2,1)S(1)}, u32[]{:S(2)}, u32[]{:S(2)}) %all-to-all-start.1) | async-done | bytes 1048608 | tf_op jit(solution)/shard_map/all_to_all | solution.py:353
  142.8 0.0 copy-start.1
  142.8 1.0 copy-done.1
  143.7 4.9 %shard_map.60 = f32[2,256,1024]{2,1,0:T(8,128)} custom-call(s32[128]{0:T(128)} %select_reduce_fusion.1.source_ref, bf16[128,16,256]{2,1,0:T(8,128)(2,1)} %copy-done.1), custom_call_target="tpu_custom_call" | custom-call | tf_op jit(solution)/shard_map/pallas_call | solution.py:355
Async XLA Ops:
  5.0 7.9 %collective-permute-start = (bf16[576,128]{1,0:T(8,128)(2,1)}, bf16[576,128]{1,0:T(8,128)(2,1)S(1)}, u32[]{:S(2)}, u32[]{:S(2)}) collective-permute-start(bf16[576,128]{1,0:T(8,128)(2,1)} %get-tuple-element.9), channel_id=1, source_target_pairs={{0,1},{1,2},{2,3},{4,5},{5,6},{6,7},{8,9},{9,10},{10,11},{12,13},{... | collective-permute-start | bytes 442376 | tf_op jit(solution)/shard_map/ppermute | solution.py:300
  9.5 6.7 %collective-permute-start.1 = (bf16[576,128]{1,0:T(8,128)(2,1)}, bf16[576,128]{1,0:T(8,128)(2,1)S(1)}, u32[]{:S(2)}, u32[]{:S(2)}) collective-permute-start(bf16[576,128]{1,0:T(8,128)(2,1)} %get-tuple-element.10), channel_id=1, source_target_pairs={{1,0},{2,1},{3,2},{5,4},{6,5},{7,6},{9,8},{10,9},{11,10},{13,12},{... | collective-permute-start | bytes 442376 | tf_op jit(solution)/shard_map/ppermute | solution.py:301
  12.9 3.2 %copy-start.2 = (bf16[576,128]{1,0:T(8,128)(2,1)}, bf16[576,128]{1,0:T(8,128)(2,1)S(1)}, u32[]{:S(2)}) copy-start(bf16[576,128]{1,0:T(8,128)(2,1)S(1)} %collective-permute-done.left_ref) | copy-start | bytes 442372
  16.2 0.7 copy-start.3
  37.3 10.4 %copy-start.4 = (s32[1024,16]{0,1:T(8,128)S(1)}, s32[1024,16]{0,1:T(8,128)}, u32[]{:S(2)}) copy-start(s32[1024,16]{0,1:T(8,128)} %param.9) | copy-start | bytes 196612
  37.3 27.4 %all-to-all-start = ((bf16[32,16,1152]{2,1,0:T(8,128)(2,1)}), bf16[32,16,1152]{2,1,0:T(8,128)(2,1)S(1)}, u32[]{:S(2)}, u32[]{:S(2)}) async-start(bf16[32,16,1152]{2,1,0:T(8,128)(2,1)} %shard_map.58), calls=%async_computation | async-start | bytes 2359296 | tf_op jit(solution)/shard_map/all_to_all | solution.py:324
  64.7 1.0 copy-start
  119.1 23.7 %all-to-all-start.1 = ((bf16[128,16,256]{2,1,0:T(8,128)(2,1)}), bf16[128,16,256]{2,1,0:T(8,128)(2,1)S(1)}, u32[]{:S(2)}, u32[]{:S(2)}) async-start(bf16[128,16,256]{2,1,0:T(8,128)(2,1)} %shard_map.59), calls=%async_computation.1 | async-start | bytes 2097152 | tf_op jit(solution)/shard_map/all_to_all | solution.py:353
  142.8 1.0 copy-start.1
where the time goes:
time: 149 us
  Pallas kernels  82.2 us (55%)
  waiting for transfers between devices  37.2 us (25%)
  starting transfers between devices  21.1 us (14%)
  local copies, waits for them, and re-layouts  7.14 us (5%)
    pallas_call x1, Pallas kernels, per_device(): pl.pallas_call(functools.partial(last_merges_kernel, inner_levels), out_s...  53.4 us
    all_to_all x1, waiting for transfers between devices, per_device(): lax.all_to_all(outgoing, ('ap', 'rg'), split_axis=0, concat_axis=0, tiled...  18.3 us
    pallas_call x1, Pallas kernels, per_device(): pl.pallas_call(functools.partial(first_merges_kernel, inner_levels, total...  18.2 us
    all_to_all x1, waiting for transfers between devices, per_device(): lax.all_to_all(merged, 'ap', split_axis=0, concat_axis=0, tiled=True)  15.7 us
    all_to_all x1, starting transfers between devices, per_device(): lax.all_to_all(merged, 'ap', split_axis=0, concat_axis=0, tiled=True)  10.3 us
    pallas_call x1, Pallas kernels, per_device(): pl.pallas_call(place_kernel, out_shape=shape((2, pulses, width), F32), gr...  4.88 us
    ppermute x1, starting transfers between devices, per_device(): from_left = lax.ppermute(to_right, 'rg', [(i, i + 1) for i in range(ends)])  4.49 us
    all_to_all x1, starting transfers between devices, per_device(): lax.all_to_all(outgoing, ('ap', 'rg'), split_axis=0, concat_axis=0, tiled...  4.3 us
  transfers between devices with their start and end apart: 4, of which 3 were waited for; matrix products, arithmetic and copies ran while one was open for 2% of the time, Pallas kernels for 1%

commit v1 on v0

v1 whole, which is shorter than its diff:
```python
import functools
import math

import jax
import jax.numpy as jnp
from jax import lax
from jax.experimental import pallas as pl
from jax.experimental.pallas import tpu as pltpu
from jax.sharding import PartitionSpec as P

ROOT_HALF = 0.7071067811865476
LANES = 128
STEP = 8
LEAD = 64
VMEM = pltpu.VMEM
BF16 = jnp.bfloat16
F32 = jnp.float32


def whole(count):
    return [pl.BlockSpec(memory_space=VMEM)] * count


def at_block(block):
    return pl.ds(pl.multiple_of(block * LANES, LANES), LANES)


def split_three(values):
    high = values.astype(BF16)
    rest = values - high.astype(F32)
    middle = rest.astype(BF16)
    low = (rest - middle.astype(F32)).astype(BF16)
    return high, middle, low


def rim_kernel(head_ref, tail_ref, offset_ref, phase_ref, left_ref, right_ref):
    pulses = head_ref.shape[1]
    levels, _, width = offset_ref.shape
    rows = 2 * levels
    for edge_ref, out_ref, start in ((head_ref, left_ref, 0), (tail_ref, right_ref, width - LANES)):
        cut = slice(start, start + LANES)
        out_ref[:pulses] = edge_ref[0]
        out_ref[pulses : 2 * pulses] = edge_ref[1]
        at = 2 * pulses
        offsets = jnp.concatenate([offset_ref[l, :, cut] for l in range(levels)], axis=0)
        angles = jnp.concatenate([phase_ref[l, :, cut] for l in range(levels)], axis=0)
        out_ref[at : at + rows] = offsets.astype(F32).astype(BF16)
        for part in split_three(angles):
            at += rows
            out_ref[at : at + rows] = part


def toeplitz_kernel(chirp_ref, table_ref):
    taps = chirp_ref[...].astype(BF16).astype(F32)
    zeros = jnp.zeros((1, LANES), F32)
    rolled = []
    for part in range(2):
        row = jnp.concatenate([taps[part : part + 1], zeros], axis=1)
        spread = jnp.broadcast_to(row, (LANES, 2 * LANES))
        rolled.append(pltpu.roll(spread, 0, 1, stride=1, stride_axis=0))
    real, imag = rolled
    table_ref[0] = jnp.concatenate([real, -imag], axis=0).astype(BF16)
    table_ref[1] = jnp.concatenate([imag, real], axis=0).astype(BF16)


def gathered(values, index):
    return jnp.take_along_axis(values, index, axis=1, mode="promise_in_bounds")


def picked(here, following, index, beyond):
    return jnp.where(beyond, gathered(following, index), gathered(here, index))


def steer(levels, total, offset_ref, phase_ref, left_ref, right_ref, rows_ref, pair_refs, index_ref, trig_ref):
    all_levels, _, width = offset_ref.shape
    columns = rows_ref.shape[2]
    blocks = columns // LANES
    rim_rows = 2 * all_levels
    base = left_ref.shape[0] - 4 * rim_rows
    first, count = levels[0], 2 * len(levels)
    start = lax.axis_index("rg") * width - LANES

    def rim(ref):
        aligned = first * 2 // 16 * 16
        parts = [
            ref[base + k * rim_rows + aligned : base + (k + 1) * rim_rows, :].astype(F32)[
                2 * first - aligned : 2 * first - aligned + count
            ]
            for k in range(4)
        ]
        return parts[0], parts[1] + parts[2] + parts[3]

    left_offset, left_phase = rim(left_ref)
    right_offset, right_phase = rim(right_ref)
    middle_offset = jnp.concatenate([offset_ref[l] for l in levels], axis=0).astype(F32)
    middle_phase = jnp.concatenate([phase_ref[l] for l in levels], axis=0)
    offsets = jnp.concatenate([left_offset, middle_offset, right_offset], axis=1)
    angles = jnp.concatenate([left_phase, middle_phase, right_phase], axis=1)
    padded = width + 2 * LANES
    bins = start + lax.broadcasted_iota(jnp.int32, (count, padded), 1)
    inside = (bins >= 0) & (bins < total)
    cosine = jnp.where(inside, jnp.cos(angles) * ROOT_HALF, 0.0)
    sine = jnp.where(inside, jnp.sin(angles) * ROOT_HALF, 0.0)
    for at, level in enumerate(levels):
        shift = padded - (LANES - LEAD + STEP * (level + 1))
        pick = slice(2 * at, 2 * at + 2)
        for part, values in enumerate((offsets + (STEP - 4.0), cosine, sine)):
            rows_ref[part, pick] = pltpu.roll(values, shift, 1)[pick, :columns]

    lane = lax.broadcasted_iota(jnp.int32, (8, LANES), 1)
    for at in range(1, len(levels)):
        inner = 1 << at
        group = max(inner, 8)
        source, target = pair_refs[(at + 1) % 2], pair_refs[at % 2]
        last = at == len(levels) - 1
        for block in range(index_ref.shape[1] // LANES if last else blocks):
            lanes = slice(block * LANES, (block + 1) * LANES)
            ahead = min(block + 1, blocks - 1)
            beyond_lanes = slice(ahead * LANES, (ahead + 1) * LANES)

            def load(part, where):
                if at == 1:
                    return jnp.broadcast_to(
                        jnp.concatenate([rows_ref[part, 0:2, where]] * 4, axis=0), (8, LANES)
                    )
                return source[part, :group, where]

            for side in range(2):
                row = 2 * at + side
                step = jnp.broadcast_to(rows_ref[0, row : row + 1, lanes], (8, LANES))
                cos_out = jnp.broadcast_to(rows_ref[1, row : row + 1, lanes], (8, LANES))
                sin_out = jnp.broadcast_to(rows_ref[2, row : row + 1, lanes], (8, LANES))
                index = lane + step.astype(jnp.int32)
                beyond = index >= LANES
                index = index & (LANES - 1)
                for sub in range(group // 8):
                    cut = slice(8 * sub, 8 * sub + 8)
                    moved, cos_in, sin_in = (
                        picked(
                            load(part, lanes)[cut], load(part, beyond_lanes)[cut], index, beyond
                        )
                        for part in range(3)
                    )
                    real = cos_out * cos_in - sin_out * sin_in
                    imag = cos_out * sin_in + sin_out * cos_in
                    moved = moved + step
                    used = min(inner, 8)
                    rows = slice(side * inner + 8 * sub, side * inner + 8 * sub + used)
                    if last:
                        index_ref[rows, lanes] = (lane + moved.astype(jnp.int32))[:used]
                        trig_ref[0, rows, lanes] = real[:used]
                        trig_ref[1, rows, lanes] = imag[:used]
                    else:
                        target[0, rows, lanes] = moved[:used]
                        target[1, rows, lanes] = real[:used]
                        target[2, rows, lanes] = imag[:used]


def steer_kernel(levels, total, offset_ref, phase_ref, left_ref, right_ref, index_ref, trig_ref, rows_ref, even_ref, odd_ref):
    steer(
        levels,
        total,
        offset_ref,
        phase_ref,
        left_ref,
        right_ref,
        rows_ref,
        (even_ref, odd_ref),
        index_ref,
        trig_ref,
    )


def steer_scratch(count, columns):
    rows = max(8, 1 << (count - 1))
    return [VMEM((3, 2 * count, columns), F32)] + [VMEM((3, rows, columns), F32)] * 2


def combination(index_ref, trig_ref, row, lanes, rows):
    def spread(values):
        return jnp.broadcast_to(values, (rows, LANES))

    index = spread(index_ref[row : row + 1, lanes])
    cosine = spread(trig_ref[0, row : row + 1, lanes])
    sine = spread(trig_ref[1, row : row + 1, lanes])
    return index & (LANES - 1), index >= LANES, cosine, sine


def term_of(here, following, steering):
    index, beyond, cosine, sine = steering
    real, imag = (picked(a, b, index, beyond) for a, b in zip(here, following))
    return real * cosine - imag * sine, real * sine + imag * cosine


def sums_and_differences(values):
    values = list(values)
    distance = 1
    while distance < len(values):
        for at in range(len(values)):
            if not at & distance:
                low, high = values[at], values[at + distance]
                values[at], values[at + distance] = low + high, low - high
        distance *= 2
    return values


def first_merges_kernel(
    levels,
    total,
    raw_ref,
    left_ref,
    right_ref,
    table_ref,
    offset_ref,
    phase_ref,
    out_ref,
    field_ref,
    term_ref,
    index_ref,
    trig_ref,
    rows_ref,
    even_ref,
    odd_ref,
):
    pulses, width = raw_ref.shape[1], raw_ref.shape[2]
    blocks = out_ref.shape[2] // LANES
    start = lax.axis_index("rg") * width - LEAD
    dims = (((1,), (1,)), ((), ()))
    for block in range(blocks):
        parts = []
        for part in range(2):
            tiles = []
            for tile in (block, block + 1):
                if tile == 0:
                    tiles.append(left_ref[part * pulses : (part + 1) * pulses, :])
                elif tile == blocks:
                    tiles.append(right_ref[part * pulses : (part + 1) * pulses, :])
                else:
                    tiles.append(raw_ref[part, :, (tile - 1) * LANES : tile * LANES])
            parts.append(
                lax.dot_general(
                    jnp.concatenate(tiles, axis=1),
                    table_ref[part],
                    dims,
                    preferred_element_type=F32,
                )
            )
        both = parts[0] + parts[1]
        if block in (0, blocks - 1):
            bins = start + block * LANES + (
                lax.broadcasted_iota(jnp.int32, both.shape, 1) % LANES
            )
            both = jnp.where((bins >= 0) & (bins < total), both, 0.0)
        lanes = slice(block * LANES, (block + 1) * LANES)
        field_ref[0, :, lanes] = both[:, :LANES]
        field_ref[1, :, lanes] = both[:, LANES:]
    steer(
        range(levels),
        total,
        offset_ref,
        phase_ref,
        left_ref,
        right_ref,
        rows_ref,
        (even_ref, odd_ref),
        index_ref,
        trig_ref,
    )
    combinations = 1 << levels
    chunk = pulses // combinations

    def merge_block(block, carry):
        lanes = at_block(block)
        beyond = at_block(jnp.minimum(block + 1, blocks - 1))
        for at in range(combinations):
            steering = combination(index_ref, trig_ref, at, lanes, chunk)
            rows = slice(at * chunk, (at + 1) * chunk)
            here = [field_ref[part, rows, lanes] for part in range(2)]
            following = [field_ref[part, rows, beyond] for part in range(2)]
            term_ref[0, at], term_ref[1, at] = term_of(here, following, steering)
        for tile in range(chunk // 8):
            cut = slice(8 * tile, 8 * tile + 8)
            real, imag = (
                sums_and_differences([term_ref[part, at, cut] for at in range(combinations)])
                for part in range(2)
            )
            for at in range(combinations):
                out_ref[at * (chunk // 8) + tile, :, lanes] = jnp.concatenate(
                    [real[at], imag[at]], axis=0
                ).astype(BF16)
        return carry

    lax.fori_loop(0, blocks, merge_block, 0)


def last_merges_kernel(target_ref, moved_ref, index_ref, trig_ref, out_ref, term_ref):
    holders, _, columns = moved_ref.shape
    per_tile = out_ref.shape[2] // LANES
    out_blocks = out_ref.shape[0] // holders * per_tile
    tiles_across = out_blocks // per_tile

    def merge_block(block, carry):
        lanes = at_block(block)
        beyond = at_block(block + 1)
        for at in range(holders):
            steering = combination(index_ref, trig_ref, at, lanes, 8)
            here = moved_ref[at, :, lanes].astype(F32)
            following = moved_ref[at, :, beyond].astype(F32)
            term_ref[0, at], term_ref[1, at] = term_of(
                (here[:8], here[8:]), (following[:8], following[8:]), steering
            )
        real, imag = (
            sums_and_differences([term_ref[part, at] for at in range(holders)])
            for part in range(2)
        )
        inner = at_block(block % per_tile)
        for at in range(holders):
            to = target_ref[at * tiles_across + block // per_tile]
            out_ref[to, :, inner] = jnp.concatenate([real[at], imag[at]], axis=0).astype(BF16)
        return carry

    lax.fori_loop(0, out_blocks, merge_block, 0)


def place_kernel(source_ref, incoming_ref, out_ref):
    rows = out_ref.shape[1]
    tile_bins = incoming_ref.shape[2]
    across = out_ref.shape[2] // tile_bins
    base = pl.program_id(0) * (rows // 8) * across
    for row in range(rows // 8):
        for column in range(across):
            tile = incoming_ref[source_ref[base + row * across + column]].astype(F32)
            for part in range(2):
                out_ref[
                    part, row * 8 : row * 8 + 8, column * tile_bins : (column + 1) * tile_bins
                ] = tile[8 * part : 8 * part + 8]


def per_device(raw_echoes, chirp, range_offsets, phases, tile_table):
    ap_count, rg_count = lax.axis_size("ap"), lax.axis_size("rg")
    devices = ap_count * rg_count
    _, pulses, width = raw_echoes.shape
    level_count = range_offsets.shape[0]
    total = width * rg_count
    outer_levels = ap_count.bit_length() - 1
    inner_levels = level_count - outer_levels
    columns = width + LANES
    tile_rows = pulses // ap_count
    tile_bins = width // rg_count
    rim_rows = 2 * pulses + 8 * level_count
    shape = jax.ShapeDtypeStruct

    edge = (2, pulses, LANES)
    last_edge = width // LANES - 1
    to_left, to_right = pl.pallas_call(
        rim_kernel,
        grid=(1,),
        out_shape=[shape((rim_rows, LANES), BF16)] * 2,
        in_specs=[
            pl.BlockSpec(edge, lambda i: (0, 0, 0)),
            pl.BlockSpec(edge, lambda i: (0, 0, last_edge)),
        ]
        + whole(2),
        out_specs=whole(2),
    )(raw_echoes, raw_echoes, range_offsets, phases)
    ends = rg_count - 1
    from_left = lax.ppermute(to_right, "rg", [(i, i + 1) for i in range(ends)])
    from_right = lax.ppermute(to_left, "rg", [(i + 1, i) for i in range(ends)])
    table = pl.pallas_call(
        toeplitz_kernel,
        out_shape=shape((2, 2 * LANES, 2 * LANES), BF16),
        in_specs=whole(1),
        out_specs=whole(1)[0],
    )(chirp)
    inner = 1 << inner_levels
    merged = pl.pallas_call(
        functools.partial(first_merges_kernel, inner_levels, total),
        out_shape=shape((ap_count, 2 * tile_rows, columns), BF16),
        in_specs=whole(6),
        out_specs=whole(1)[0],
        scratch_shapes=[
            VMEM((2, pulses, columns), F32),
            VMEM((2, inner, pulses // inner, LANES), F32),
            VMEM((inner, columns), jnp.int32),
            VMEM((2, inner, columns), F32),
        ]
        + steer_scratch(inner_levels, columns),
    )(raw_echoes, from_left, from_right, table, range_offsets, phases)
    moved = lax.all_to_all(merged, "ap", split_axis=0, concat_axis=0, tiled=True)
    index, trig = pl.pallas_call(
        functools.partial(steer_kernel, range(inner_levels, level_count), total),
        out_shape=[shape((ap_count, width), jnp.int32), shape((2, ap_count, width), F32)],
        in_specs=whole(4),
        out_specs=whole(2),
        scratch_shapes=steer_scratch(outer_levels, columns),
    )(range_offsets, phases, from_left, from_right)

    ap_here, rg_here = lax.axis_index("ap"), lax.axis_index("rg")
    slot_row = tile_table // (rg_count * rg_count)
    slot_col = tile_table % (rg_count * rg_count)
    target = slot_row // ap_count * rg_count + slot_col // rg_count
    shaped = (ap_count, ap_count, rg_count, rg_count)
    target = target.reshape(shaped)
    local_slot = (slot_row % ap_count * rg_count + slot_col % rg_count).reshape(shaped)
    mine = target == ap_here * rg_count + rg_here
    slot_from = jnp.sum(jnp.where(mine, local_slot, 0), axis=(0, 3)).reshape(devices)
    ids = jnp.arange(devices, dtype=jnp.int32)
    source = jnp.sum(
        jnp.where(slot_from[None, :] == ids[:, None], ids[None, :], 0), axis=1
    )
    send_to = lax.dynamic_slice(
        target, (0, ap_here, rg_here, 0), (ap_count, 1, 1, rg_count)
    ).reshape(devices)

    outgoing = pl.pallas_call(
        last_merges_kernel,
        out_shape=shape((devices, 2 * tile_rows, tile_bins), BF16),
        grid_spec=pltpu.PrefetchScalarGridSpec(
            num_scalar_prefetch=1,
            in_specs=whole(3),
            out_specs=whole(1)[0],
            scratch_shapes=[VMEM((2, ap_count, tile_rows, LANES), F32)],
        ),
    )(send_to, moved, index, trig)
    incoming = lax.all_to_all(outgoing, ("ap", "rg"), split_axis=0, concat_axis=0, tiled=True)
    steps = 8
    return pl.pallas_call(
        place_kernel,
        out_shape=shape((2, pulses, width), F32),
        grid_spec=pltpu.PrefetchScalarGridSpec(
            num_scalar_prefetch=1,
            grid=(steps,),
            in_specs=whole(1),
            out_specs=pl.BlockSpec((2, pulses // steps, width), lambda i, s: (0, i, 0)),
        ),
    )(source, incoming)


def solution(mesh):
    placed = (P(None, "ap", "rg"), P(), P(None, None, "rg"), P(None, None, "rg"), P())
    return jax.shard_map(
        per_device, mesh=mesh, in_specs=placed, out_specs=P(None, "ap", "rg"), check_vma=False
    )
```

time: 149 us -> 82.8 us (0.56)
  Pallas kernels: 82.2 us -> 22 us
  waiting for transfers between devices: 37.2 us -> 34.1 us
  local copies, waits for them, and re-layouts: 7.14 us -> 4.14 us
    pallas_call x3, Pallas kernels: 57.6 us -> 10 us  [the longest x1 5.19 us: per_device(): pl.pallas_call(last_merges_kernel, out_shape=shape((devices, 2 * tile_row...]
    pallas_call x1, Pallas kernels: 18.2 us -> 5.6 us  [per_device(): pl.pallas_call(functools.partial(first_merges_kernel, inner_levels, total...]
    all_to_all x1, waiting for transfers between devices: 15.7 us -> 12.5 us  [per_device(): lax.all_to_all(merged, 'ap', split_axis=0, concat_axis=0, tiled=True)]
    reshape x2 -> x0, local copies, waits for them, and re-layouts: 3.01 us -> none  [the longest x1 1.51 us: per_device(): offset_rows = range_offsets.reshape(2 * level_count, width)]
  transfers between devices with their start and end apart: 4 -> 4, of which waited for: 3 -> 3; matrix products, arithmetic and copies ran while one was open for 2% -> 3% of each run, Pallas kernels for 1% -> 6%
where the time goes in v1:
time: 82.8 us; the launch traced here: 82.3 us
  waiting for transfers between devices  34.1 us (41%)
  Pallas kernels  22 us (27%)
  starting transfers between devices  21.1 us (25%)
  local copies, waits for them, and re-layouts  4.14 us (5%)
  other arithmetic  0.89 us (1%)
    all_to_all x1, waiting for transfers between devices, per_device(): lax.all_to_all(outgoing, ('ap', 'rg'), split_axis=0, concat_axis=0, tiled...  18.3 us
    all_to_all x1, waiting for transfers between devices, per_device(): lax.all_to_all(merged, 'ap', split_axis=0, concat_axis=0, tiled=True)  12.5 us
    all_to_all x1, starting transfers between devices, per_device(): lax.all_to_all(merged, 'ap', split_axis=0, concat_axis=0, tiled=True)  10.4 us
    pallas_call x1, Pallas kernels, per_device(): pl.pallas_call(functools.partial(first_merges_kernel, inner_levels, total...  5.6 us
    pallas_call x1, Pallas kernels, per_device(): pl.pallas_call(last_merges_kernel, out_shape=shape((devices, 2 * tile_row...  5.19 us
    pallas_call x1, Pallas kernels, per_device(): pl.pallas_call(place_kernel, out_shape=shape((2, pulses, width), F32), gr...  4.88 us
    ppermute x1, starting transfers between devices, per_device(): from_left = lax.ppermute(to_right, 'rg', [(i, i + 1) for i in range(ends)])  4.49 us
    all_to_all x1, starting transfers between devices, per_device(): lax.all_to_all(outgoing, ('ap', 'rg'), split_axis=0, concat_axis=0, tiled...  4.3 us
  transfers between devices with their start and end apart: 4, of which 3 were waited for; matrix products, arithmetic and copies ran while one was open for 3% of the time, Pallas kernels for 6%

profile of v1, /device:TPU:1, one launch (start us, length us, event | category | flops | bytes accessed | tf_op | source)
XLA Modules:
  0.0 82.3 jit_solution(15355181172279763770)
XLA Ops:
  0.0 1.7 %shard_map.55 = (bf16[576,128]{1,0:T(8,128)(2,1)}, bf16[576,128]{1,0:T(8,128)(2,1)}) custom-call(bf16[2,256,1024]{2,1,0:T(8,128)(2,1)} %raw_ref.1, bf16[2,256,1024]{2,1,0:T(8,128)(2,1)} %raw_ref.1, s32[8,2,1024]{2,1,0:T(2,128)} %offset_ref.5, f32[8,2,1024]{2,1,0:T(2,128)} %phase_ref.5), custom_call_target="tpu_custom_call" | custom-call | tf_op jit(solution)/shard_map/pallas_call | solution.py:355
  1.7 4.5 %collective-permute-start = (bf16[576,128]{1,0:T(8,128)(2,1)}, bf16[576,128]{1,0:T(8,128)(2,1)S(1)}, u32[]{:S(2)}, u32[]{:S(2)}) collective-permute-start(bf16[576,128]{1,0:T(8,128)(2,1)} %get-tuple-element.9), channel_id=1, source_target_pairs={{0,1},{1,2},{2,3},{4,5},{5,6},{6,7},{8,9},{9,10},{10,11},{12,13},{... | collective-permute-start | bytes 442376 | tf_op jit(solution)/shard_map/ppermute | solution.py:367
  6.2 1.9 %collective-permute-start.1 = (bf16[576,128]{1,0:T(8,128)(2,1)}, bf16[576,128]{1,0:T(8,128)(2,1)S(1)}, u32[]{:S(2)}, u32[]{:S(2)}) collective-permute-start(bf16[576,128]{1,0:T(8,128)(2,1)} %get-tuple-element.10), channel_id=1, source_target_pairs={{1,0},{2,1},{3,2},{5,4},{6,5},{7,6},{9,8},{10,9},{11,10},{13,12},{... | collective-permute-start | bytes 442376 | tf_op jit(solution)/shard_map/ppermute | solution.py:368
  8.1 1.5 %shard_map.56.table_ref = bf16[2,256,256]{2,1,0:T(8,128)(2,1)} custom-call(f32[2,128]{1,0:T(2,128)} %chirp_ref.1), custom_call_target="tpu_custom_call" | custom-call | tf_op jit(solution)/shard_map/pallas_call | solution.py:369
  9.6 0.0 collective-permute-done.left_ref
  9.6 0.0 copy-start.2
  9.7 3.2 %collective-permute-done.1.right_ref = bf16[576,128]{1,0:T(8,128)(2,1)S(1)} collective-permute-done((bf16[576,128]{1,0:T(8,128)(2,1)}, bf16[576,128]{1,0:T(8,128)(2,1)S(1)}, u32[]{:S(2)}, u32[]{:S(2)}) %collective-permute-start.1) | collective-permute-done | bytes 147488 | tf_op jit(solution)/shard_map/ppermute | solution.py:368
  12.9 0.0 copy-done.2
  12.9 0.0 copy-start.3
  12.9 0.7 copy-done.3
  13.5 5.6 %shard_map.57 = bf16[32,16,1152]{2,1,0:T(8,128)(2,1)} custom-call(bf16[2,256,1024]{2,1,0:T(8,128)(2,1)} %raw_ref.1, bf16[576,128]{1,0:T(8,128)(2,1)} %copy-done.2, bf16[576,128]{1,0:T(8,128)(2,1)} %copy-done.3, bf16[2,256,256]{2,1,0:T(8,128)(2,1)} %shard_map.56.table_ref, s32[8,2,1024]{2,1,0:T(2,128)} %offset_ref.5, f32[8,2,1024]{2,1,0:T(2,128)} %phase_ref.5), custom_call_target="tpu_custom_call" | custom-call | tf_op jit(solution)/shard_map/pallas_call | solution.py:376
  19.1 0.0 copy-start.4
  19.2 10.4 %all-to-all-start = ((bf16[32,16,1152]{2,1,0:T(8,128)(2,1)}), bf16[32,16,1152]{2,1,0:T(8,128)(2,1)S(1)}, u32[]{:S(2)}, u32[]{:S(2)}) async-start(bf16[32,16,1152]{2,1,0:T(8,128)(2,1)} %shard_map.57), calls=%async_computation | async-start | bytes 2359296 | tf_op jit(solution)/shard_map/all_to_all | solution.py:389
  29.5 0.0 copy-done.4
  29.5 0.2 fusion.1
  29.7 0.1 reshape.10
  29.8 0.1 constant_dynamic-slice_fusion
  29.9 0.3 copy.12
  30.2 0.7 reshape.12.target_ref
  30.9 3.1 %shard_map.58 = (s32[32,1024]{1,0:T(8,128)}, f32[2,32,1024]{2,1,0:T(8,128)}) custom-call(s32[8,2,1024]{2,1,0:T(2,128)} %offset_ref.5, f32[8,2,1024]{2,1,0:T(2,128)} %phase_ref.5, bf16[576,128]{1,0:T(8,128)(2,1)} %copy-done.2, bf16[576,128]{1,0:T(8,128)(2,1)} %copy-done.3), custom_call_target="tpu_custom_call" | custom-call | tf_op jit(solution)/shard_map/pallas_call | solution.py:390
  34.0 12.5 %all-to-all-done.moved_ref = bf16[32,16,1152]{2,1,0:T(8,128)(2,1)S(1)} async-done(((bf16[32,16,1152]{2,1,0:T(8,128)(2,1)}), bf16[32,16,1152]{2,1,0:T(8,128)(2,1)S(1)}, u32[]{:S(2)}, u32[]{:S(2)}) %all-to-all-start) | async-done | bytes 1179680 | tf_op jit(solution)/shard_map/all_to_all | solution.py:389
  46.6 0.0 copy-start
  46.6 1.0 %copy-done = bf16[32,16,1152]{2,1,0:T(8,128)(2,1)} copy-done((bf16[32,16,1152]{2,1,0:T(8,128)(2,1)}, bf16[32,16,1152]{2,1,0:T(8,128)(2,1)S(1)}, u32[]{:S(2)}) %copy-start) | copy-done | bytes 1179672
  47.6 5.2 %shard_map.59 = bf16[128,16,256]{2,1,0:T(8,128)(2,1)} custom-call(s32[128]{0:T(128)} %reshape.12.target_ref, bf16[32,16,1152]{2,1,0:T(8,128)(2,1)} %copy-done, s32[32,1024]{1,0:T(8,128)} %get-tuple-element.11.index_ref, f32[2,32,1024]{2,1,0:T(8,128)} %get-tuple-element.12.trig_ref), custom_call_target="tpu_custom_call" | custom-call | tf_op jit(solution)/shard_map/pallas_call | solution.py:415
  52.8 4.3 %all-to-all-start.1 = ((bf16[128,16,256]{2,1,0:T(8,128)(2,1)}), bf16[128,16,256]{2,1,0:T(8,128)(2,1)S(1)}, u32[]{:S(2)}, u32[]{:S(2)}) async-start(bf16[128,16,256]{2,1,0:T(8,128)(2,1)} %shard_map.59), calls=%async_computation.1 | async-start | bytes 2097152 | tf_op jit(solution)/shard_map/all_to_all | solution.py:425
  57.1 0.1 reshape.11
  57.2 0.1 select_reduce_fusion
  57.3 0.1 copy.10
  57.4 0.1 eq.27
  57.5 0.6 select_reduce_fusion.1.source_ref
  58.1 18.3 %all-to-all-done.1.incoming_ref = bf16[128,16,256]{2,1,0:T(8,128)(2,1)S(1)} async-done(((bf16[128,16,256]{2,1,0:T(8,128)(2,1)}), bf16[128,16,256]{2,1,0:T(8,128)(2,1)S(1)}, u32[]{:S(2)}, u32[]{:S(2)}) %all-to-all-start.1) | async-done | bytes 1048608 | tf_op jit(solution)/shard_map/all_to_all | solution.py:425
  76.4 0.0 copy-start.1
  76.4 1.0 %copy-done.1 = bf16[128,16,256]{2,1,0:T(8,128)(2,1)} copy-done((bf16[128,16,256]{2,1,0:T(8,128)(2,1)}, bf16[128,16,256]{2,1,0:T(8,128)(2,1)S(1)}, u32[]{:S(2)}) %copy-start.1) | copy-done | bytes 1048600
  77.4 4.9 %shard_map.60 = f32[2,256,1024]{2,1,0:T(8,128)} custom-call(s32[128]{0:T(128)} %select_reduce_fusion.1.source_ref, bf16[128,16,256]{2,1,0:T(8,128)(2,1)} %copy-done.1), custom_call_target="tpu_custom_call" | custom-call | tf_op jit(solution)/shard_map/pallas_call | solution.py:427
Async XLA Ops:
  1.7 7.9 %collective-permute-start = (bf16[576,128]{1,0:T(8,128)(2,1)}, bf16[576,128]{1,0:T(8,128)(2,1)S(1)}, u32[]{:S(2)}, u32[]{:S(2)}) collective-permute-start(bf16[576,128]{1,0:T(8,128)(2,1)} %get-tuple-element.9), channel_id=1, source_target_pairs={{0,1},{1,2},{2,3},{4,5},{5,6},{6,7},{8,9},{9,10},{10,11},{12,13},{... | collective-permute-start | bytes 442376 | tf_op jit(solution)/shard_map/ppermute | solution.py:367
  6.2 6.7 %collective-permute-start.1 = (bf16[576,128]{1,0:T(8,128)(2,1)}, bf16[576,128]{1,0:T(8,128)(2,1)S(1)}, u32[]{:S(2)}, u32[]{:S(2)}) collective-permute-start(bf16[576,128]{1,0:T(8,128)(2,1)} %get-tuple-element.10), channel_id=1, source_target_pairs={{1,0},{2,1},{3,2},{5,4},{6,5},{7,6},{9,8},{10,9},{11,10},{13,12},{... | collective-permute-start | bytes 442376 | tf_op jit(solution)/shard_map/ppermute | solution.py:368
  9.6 3.2 %copy-start.2 = (bf16[576,128]{1,0:T(8,128)(2,1)}, bf16[576,128]{1,0:T(8,128)(2,1)S(1)}, u32[]{:S(2)}) copy-start(bf16[576,128]{1,0:T(8,128)(2,1)S(1)} %collective-permute-done.left_ref) | copy-start | bytes 442372
  12.9 0.7 copy-start.3
  19.1 10.4 %copy-start.4 = (s32[1024,16]{0,1:T(8,128)S(1)}, s32[1024,16]{0,1:T(8,128)}, u32[]{:S(2)}) copy-start(s32[1024,16]{0,1:T(8,128)} %param.9) | copy-start | bytes 196612
  19.2 27.4 %all-to-all-start = ((bf16[32,16,1152]{2,1,0:T(8,128)(2,1)}), bf16[32,16,1152]{2,1,0:T(8,128)(2,1)S(1)}, u32[]{:S(2)}, u32[]{:S(2)}) async-start(bf16[32,16,1152]{2,1,0:T(8,128)(2,1)} %shard_map.57), calls=%async_computation | async-start | bytes 2359296 | tf_op jit(solution)/shard_map/all_to_all | solution.py:389
  46.6 1.0 %copy-start = (bf16[32,16,1152]{2,1,0:T(8,128)(2,1)}, bf16[32,16,1152]{2,1,0:T(8,128)(2,1)S(1)}, u32[]{:S(2)}) copy-start(bf16[32,16,1152]{2,1,0:T(8,128)(2,1)S(1)} %all-to-all-done.moved_ref) | copy-start | bytes 3538948
  52.8 23.7 %all-to-all-start.1 = ((bf16[128,16,256]{2,1,0:T(8,128)(2,1)}), bf16[128,16,256]{2,1,0:T(8,128)(2,1)S(1)}, u32[]{:S(2)}, u32[]{:S(2)}) async-start(bf16[128,16,256]{2,1,0:T(8,128)(2,1)} %shard_map.59), calls=%async_computation.1 | async-start | bytes 2097152 | tf_op jit(solution)/shard_map/all_to_all | solution.py:425
  76.4 1.0 %copy-start.1 = (bf16[128,16,256]{2,1,0:T(8,128)(2,1)}, bf16[128,16,256]{2,1,0:T(8,128)(2,1)S(1)}, u32[]{:S(2)}) copy-start(bf16[128,16,256]{2,1,0:T(8,128)(2,1)S(1)} %all-to-all-done.1.incoming_ref) | copy-start | bytes 3145732

commit v2 on v1

--- a/solution.py
+++ b/solution.py
@@ -19,6 +19,14 @@
 
 def whole(count):
     return [pl.BlockSpec(memory_space=VMEM)] * count
+
+
+def near(value):
+    return pltpu.with_memory_space_constraint(value, VMEM)
+
+
+def params():
+    return pltpu.CompilerParams(vmem_limit_bytes=24 * 2**20)
 
 
 def at_block(block):
@@ -355,27 +363,30 @@
     to_left, to_right = pl.pallas_call(
         rim_kernel,
         grid=(1,),
-        out_shape=[shape((rim_rows, LANES), BF16)] * 2,
+        out_shape=[VMEM((rim_rows, LANES), BF16)] * 2,
+        compiler_params=params(),
         in_specs=[
             pl.BlockSpec(edge, lambda i: (0, 0, 0)),
             pl.BlockSpec(edge, lambda i: (0, 0, last_edge)),
         ]
         + whole(2),
         out_specs=whole(2),
-    )(raw_echoes, raw_echoes, range_offsets, phases)
+    )(raw_echoes, raw_echoes, *map(near, (range_offsets, phases)))
     ends = rg_count - 1
     from_left = lax.ppermute(to_right, "rg", [(i, i + 1) for i in range(ends)])
     from_right = lax.ppermute(to_left, "rg", [(i + 1, i) for i in range(ends)])
     table = pl.pallas_call(
         toeplitz_kernel,
-        out_shape=shape((2, 2 * LANES, 2 * LANES), BF16),
+        out_shape=VMEM((2, 2 * LANES, 2 * LANES), BF16),
+        compiler_params=params(),
         in_specs=whole(1),
         out_specs=whole(1)[0],
     )(chirp)
     inner = 1 << inner_levels
     merged = pl.pallas_call(
         functools.partial(first_merges_kernel, inner_levels, total),
-        out_shape=shape((ap_count, 2 * tile_rows, columns), BF16),
+        out_shape=VMEM((ap_count, 2 * tile_rows, columns), BF16),
+        compiler_params=params(),
         in_specs=whole(6),
         out_specs=whole(1)[0],
         scratch_shapes=[
@@ -385,15 +396,16 @@
             VMEM((2, inner, columns), F32),
         ]
         + steer_scratch(inner_levels, columns),
-    )(raw_echoes, from_left, from_right, table, range_offsets, phases)
+    )(*map(near, (raw_echoes, from_left, from_right, table, range_offsets, phases)))
     moved = lax.all_to_all(merged, "ap", split_axis=0, concat_axis=0, tiled=True)
     index, trig = pl.pallas_call(
         functools.partial(steer_kernel, range(inner_levels, level_count), total),
-        out_shape=[shape((ap_count, width), jnp.int32), shape((2, ap_count, width), F32)],
+        out_shape=[VMEM((ap_count, width), jnp.int32), VMEM((2, ap_count, width), F32)],
+        compiler_params=params(),
         in_specs=whole(4),
         out_specs=whole(2),
         scratch_shapes=steer_scratch(outer_levels, columns),
-    )(range_offsets, phases, from_left, from_right)
+    )(*map(near, (range_offsets, phases, from_left, from_right)))
 
     ap_here, rg_here = lax.axis_index("ap"), lax.axis_index("rg")
     slot_row = tile_table // (rg_count * rg_count)
@@ -414,26 +426,28 @@
 
     outgoing = pl.pallas_call(
         last_merges_kernel,
-        out_shape=shape((devices, 2 * tile_rows, tile_bins), BF16),
+        out_shape=VMEM((devices, 2 * tile_rows, tile_bins), BF16),
+        compiler_params=params(),
         grid_spec=pltpu.PrefetchScalarGridSpec(
             num_scalar_prefetch=1,
             in_specs=whole(3),
             out_specs=whole(1)[0],
             scratch_shapes=[VMEM((2, ap_count, tile_rows, LANES), F32)],
         ),
-    )(send_to, moved, index, trig)
+    )(send_to, *map(near, (moved, index, trig)))
     incoming = lax.all_to_all(outgoing, ("ap", "rg"), split_axis=0, concat_axis=0, tiled=True)
     steps = 8
     return pl.pallas_call(
         place_kernel,
         out_shape=shape((2, pulses, width), F32),
+        compiler_params=params(),
         grid_spec=pltpu.PrefetchScalarGridSpec(
             num_scalar_prefetch=1,
             grid=(steps,),
             in_specs=whole(1),
             out_specs=pl.BlockSpec((2, pulses // steps, width), lambda i, s: (0, i, 0)),
         ),
-    )(source, incoming)
+    )(source, near(incoming))
 
 
 def solution(mesh):

time: 82.8 us -> 77.1 us (0.931)
  Pallas kernels: 22 us -> 12.9 us
  waiting for transfers between devices: 34.1 us -> 38.2 us
    pallas_call x4, Pallas kernels: 13.3 us -> 7.46 us  [the longest x1 3.72 us: per_device(): pl.pallas_call(last_merges_kernel, out_shape=VMEM((devices, 2 * tile_rows...]
    all_to_all x1, waiting for transfers between devices: 12.5 us -> 14.9 us  [per_device(): lax.all_to_all(merged, 'ap', split_axis=0, concat_axis=0, tiled=True)]
    pallas_call x1, Pallas kernels: 3.11 us -> 1.28 us  [per_device(): pl.pallas_call(functools.partial(steer_kernel, range(inner_levels, level_...]
    pallas_call x1, Pallas kernels: 5.6 us -> 4.2 us  [per_device(): pl.pallas_call(functools.partial(first_merges_kernel, inner_levels, total...]
    ppermute x1, waiting for transfers between devices: 3.24 us -> 4.38 us  [per_device(): from_right = lax.ppermute(to_left, 'rg', [(i + 1, i) for i in range(ends)])]
    unnamed x11 -> x17, local copies, waits for them, and re-layouts: 2.94 us -> 3.22 us
  transfers between devices with their start and end apart: 4 -> 4, of which waited for: 3 -> 3; matrix products, arithmetic and copies ran while one was open for 3% -> 2% of each run, Pallas kernels for 6% -> 2%
where the time goes in v2:
time: 77.1 us; the launch traced here: 76.7 us
  waiting for transfers between devices  38.2 us (50%)
  starting transfers between devices  21.2 us (27%)
  Pallas kernels  12.9 us (17%)
  local copies, waits for them, and re-layouts  3.84 us (5%)
    all_to_all x1, waiting for transfers between devices, per_device(): lax.all_to_all(outgoing, ('ap', 'rg'), split_axis=0, concat_axis=0, tiled...  18.9 us
    all_to_all x1, waiting for transfers between devices, per_device(): lax.all_to_all(merged, 'ap', split_axis=0, concat_axis=0, tiled=True)  14.9 us
    all_to_all x1, starting transfers between devices, per_device(): lax.all_to_all(merged, 'ap', split_axis=0, concat_axis=0, tiled=True)  10.4 us
    ppermute x1, starting transfers between devices, per_device(): from_left = lax.ppermute(to_right, 'rg', [(i, i + 1) for i in range(ends)])  4.63 us
    ppermute x1, waiting for transfers between devices, per_device(): from_right = lax.ppermute(to_left, 'rg', [(i + 1, i) for i in range(ends)])  4.38 us
    all_to_all x1, starting transfers between devices, per_device(): lax.all_to_all(outgoing, ('ap', 'rg'), split_axis=0, concat_axis=0, tiled...  4.3 us
    pallas_call x1, Pallas kernels, per_device(): pl.pallas_call(functools.partial(first_merges_kernel, inner_levels, total...  4.2 us
    pallas_call x1, Pallas kernels, per_device(): pl.pallas_call(last_merges_kernel, out_shape=VMEM((devices, 2 * tile_rows...  3.72 us
  transfers between devices with their start and end apart: 4, of which 3 were waited for; matrix products, arithmetic and copies ran while one was open for 2% of the time, Pallas kernels for 2%

profile of v2, /device:TPU:1, one launch (start us, length us, event | category | flops | bytes accessed | tf_op | source)
XLA Modules:
  0.0 76.7 jit_solution(7146654835137986823)
XLA Ops:
  0.0 0.0 copy-start
  0.0 1.2 %copy-done = bf16[2,256,1024]{2,1,0:T(8,128)(2,1)S(1)} copy-done((bf16[2,256,1024]{2,1,0:T(8,128)(2,1)S(1)}, bf16[2,256,1024]{2,1,0:T(8,128)(2,1)}, u32[]{:S(2)}) %copy-start) | copy-done | bytes 1048600
  1.2 0.0 copy-start.2
  1.2 0.8 %copy-done.2 = s32[8,2,1024]{2,1,0:T(2,128)S(1)} copy-done((s32[8,2,1024]{2,1,0:T(2,128)S(1)}, s32[8,2,1024]{2,1,0:T(2,128)}, u32[]{:S(2)}) %copy-start.2) | copy-done | bytes 65560
  2.1 0.0 copy-start.4
  2.1 0.8 %copy-done.4 = f32[8,2,1024]{2,1,0:T(2,128)S(1)} copy-done((f32[8,2,1024]{2,1,0:T(2,128)S(1)}, f32[8,2,1024]{2,1,0:T(2,128)}, u32[]{:S(2)}) %copy-start.4) | copy-done | bytes 65560
  2.9 0.0 copy-start.6
  2.9 0.0 copy-start.1
  2.9 0.1 shard_map.55
  3.0 4.6 %collective-permute-start = (bf16[576,128]{1,0:T(8,128)(2,1)S(1)}, bf16[576,128]{1,0:T(8,128)(2,1)S(1)}, u32[]{:S(2)}, u32[]{:S(2)}) collective-permute-start(bf16[576,128]{1,0:T(8,128)(2,1)S(1)} %get-tuple-element.9), channel_id=1, source_target_pairs={{0,1},{1,2},{2,3},{4,5},{5,6},{6,7},{8,9},{9,10},{10,11},{12,13},{... | collective-permute-start | bytes 442376 | tf_op jit(solution)/shard_map/ppermute | solution.py:376
  7.6 1.9 %collective-permute-start.1 = (bf16[576,128]{1,0:T(8,128)(2,1)S(1)}, bf16[576,128]{1,0:T(8,128)(2,1)S(1)}, u32[]{:S(2)}, u32[]{:S(2)}) collective-permute-start(bf16[576,128]{1,0:T(8,128)(2,1)S(1)} %get-tuple-element.10), channel_id=1, source_target_pairs={{1,0},{2,1},{3,2},{5,4},{6,5},{7,6},{9,8},{10,9},{11,10},{13,12},{... | collective-permute-start | bytes 442376 | tf_op jit(solution)/shard_map/ppermute | solution.py:377
  9.6 0.0 copy-done.6
  9.6 0.1 shard_map.56.table_ref
  9.7 0.0 collective-permute-done.left_ref
  9.7 4.4 %collective-permute-done.1.right_ref = bf16[576,128]{1,0:T(8,128)(2,1)S(1)} collective-permute-done((bf16[576,128]{1,0:T(8,128)(2,1)S(1)}, bf16[576,128]{1,0:T(8,128)(2,1)S(1)}, u32[]{:S(2)}, u32[]{:S(2)}) %collective-permute-start.1) | collective-permute-done | bytes 147488 | tf_op jit(solution)/shard_map/ppermute | solution.py:377
  14.1 0.0 copy-done.1
  14.1 4.2 %shard_map.57 = bf16[32,16,1152]{2,1,0:T(8,128)(2,1)} custom-call(bf16[2,256,1024]{2,1,0:T(8,128)(2,1)S(1)} %copy-done.1, bf16[576,128]{1,0:T(8,128)(2,1)S(1)} %collective-permute-done.left_ref, bf16[576,128]{1,0:T(8,128)(2,1)S(1)} %collective-permute-done.1.right_ref, bf16[2,256,256]{2,1,0:T(8,128)(2,1)S(1)} %shard_map.56.table_ref, ...), custom_call_target="tpu_custom_call" | custom-call | tf_op jit(solution)/shard_map/pallas_call | solution.py:386
  18.3 0.0 copy-start.7
  18.3 0.0 copy-start.3
  18.3 0.0 copy-start.5
  18.3 10.4 %all-to-all-start = ((bf16[32,16,1152]{2,1,0:T(8,128)(2,1)}), bf16[32,16,1152]{2,1,0:T(8,128)(2,1)S(1)}, u32[]{:S(2)}, u32[]{:S(2)}) async-start(bf16[32,16,1152]{2,1,0:T(8,128)(2,1)} %shard_map.57), calls=%async_computation | async-start | bytes 2359296 | tf_op jit(solution)/shard_map/all_to_all | solution.py:400
  28.7 0.0 copy-done.7
  28.7 0.2 fusion.1
  28.9 0.1 reshape.10
  29.0 0.1 constant_dynamic-slice_fusion
  29.1 0.3 copy.12
  29.4 0.1 reshape.12.target_ref
  29.5 0.0 copy-done.3
  29.5 0.0 copy-done.5
  29.5 1.3 %shard_map.58 = (s32[32,1024]{1,0:T(8,128)S(1)}, f32[2,32,1024]{2,1,0:T(8,128)S(1)}) custom-call(s32[8,2,1024]{2,1,0:T(2,128)S(1)} %copy-done.3, f32[8,2,1024]{2,1,0:T(2,128)S(1)} %copy-done.5, bf16[576,128]{1,0:T(8,128)(2,1)S(1)} %collective-permute-done.left_ref, bf16[576,128]{1,0:T(8,128)(2,1)S(1)} %collective-permute-done.1.right_ref), custom_call_target="tpu_custom_call" | custom-call | tf_op jit(solution)/shard_map/pallas_call | solution.py:401
  30.8 14.9 %all-to-all-done.moved_ref = bf16[32,16,1152]{2,1,0:T(8,128)(2,1)S(1)} async-done(((bf16[32,16,1152]{2,1,0:T(8,128)(2,1)}), bf16[32,16,1152]{2,1,0:T(8,128)(2,1)S(1)}, u32[]{:S(2)}, u32[]{:S(2)}) %all-to-all-start) | async-done | bytes 1179680 | tf_op jit(solution)/shard_map/all_to_all | solution.py:400
  45.7 3.7 %shard_map.59 = bf16[128,16,256]{2,1,0:T(8,128)(2,1)} custom-call(s32[128]{0:T(128)S(1)} %reshape.12.target_ref, bf16[32,16,1152]{2,1,0:T(8,128)(2,1)S(1)} %all-to-all-done.moved_ref, s32[32,1024]{1,0:T(8,128)S(1)} %get-tuple-element.11.index_ref, f32[2,32,1024]{2,1,0:T(8,128)S(1)} %get-tuple-element.12.trig_ref), custom_call_target="tpu_custom_call" | custom-call | tf_op jit(solution)/shard_map/pallas_call | solution.py:427
  49.5 4.3 %all-to-all-start.1 = ((bf16[128,16,256]{2,1,0:T(8,128)(2,1)}), bf16[128,16,256]{2,1,0:T(8,128)(2,1)S(1)}, u32[]{:S(2)}, u32[]{:S(2)}) async-start(bf16[128,16,256]{2,1,0:T(8,128)(2,1)} %shard_map.59), calls=%async_computation.1 | async-start | bytes 2097152 | tf_op jit(solution)/shard_map/all_to_all | solution.py:438
  53.8 0.1 reshape.11
  53.9 0.1 select_reduce_fusion
  54.0 0.1 copy.10
  54.0 0.1 eq.27
  54.2 0.1 select_reduce_fusion.1.source_ref
  54.3 18.9 %all-to-all-done.1.incoming_ref = bf16[128,16,256]{2,1,0:T(8,128)(2,1)S(1)} async-done(((bf16[128,16,256]{2,1,0:T(8,128)(2,1)}), bf16[128,16,256]{2,1,0:T(8,128)(2,1)S(1)}, u32[]{:S(2)}, u32[]{:S(2)}) %all-to-all-start.1) | async-done | bytes 1048608 | tf_op jit(solution)/shard_map/all_to_all | solution.py:438
  73.1 3.5 %shard_map.60 = f32[2,256,1024]{2,1,0:T(8,128)} custom-call(s32[128]{0:T(128)S(1)} %select_reduce_fusion.1.source_ref, bf16[128,16,256]{2,1,0:T(8,128)(2,1)S(1)} %all-to-all-done.1.incoming_ref), custom_call_target="tpu_custom_call" | custom-call | tf_op jit(solution)/shard_map/pallas_call | solution.py:440
Async XLA Ops:
  0.0 1.2 %copy-start = (bf16[2,256,1024]{2,1,0:T(8,128)(2,1)S(1)}, bf16[2,256,1024]{2,1,0:T(8,128)(2,1)}, u32[]{:S(2)}) copy-start(bf16[2,256,1024]{2,1,0:T(8,128)(2,1)} %raw_ref.1) | copy-start | bytes 3145732
  1.2 0.8 %copy-start.2 = (s32[8,2,1024]{2,1,0:T(2,128)S(1)}, s32[8,2,1024]{2,1,0:T(2,128)}, u32[]{:S(2)}) copy-start(s32[8,2,1024]{2,1,0:T(2,128)} %offset_ref.5) | copy-start | bytes 196612
  2.1 0.8 %copy-start.4 = (f32[8,2,1024]{2,1,0:T(2,128)S(1)}, f32[8,2,1024]{2,1,0:T(2,128)}, u32[]{:S(2)}) copy-start(f32[8,2,1024]{2,1,0:T(2,128)} %phase_ref.5) | copy-start | bytes 196612
  2.9 6.7 %copy-start.6 = (f32[2,128]{1,0:T(2,128)S(1)}, f32[2,128]{1,0:T(2,128)}, u32[]{:S(2)}) copy-start(f32[2,128]{1,0:T(2,128)} %chirp_ref.1) | copy-start | bytes 3076
  2.9 11.2 %copy-start.1 = (bf16[2,256,1024]{2,1,0:T(8,128)(2,1)S(1)}, bf16[2,256,1024]{2,1,0:T(8,128)(2,1)}, u32[]{:S(2)}) copy-start(bf16[2,256,1024]{2,1,0:T(8,128)(2,1)} %raw_ref.1) | copy-start | bytes 3145732
  3.0 6.7 %collective-permute-start = (bf16[576,128]{1,0:T(8,128)(2,1)S(1)}, bf16[576,128]{1,0:T(8,128)(2,1)S(1)}, u32[]{:S(2)}, u32[]{:S(2)}) collective-permute-start(bf16[576,128]{1,0:T(8,128)(2,1)S(1)} %get-tuple-element.9), channel_id=1, source_target_pairs={{0,1},{1,2},{2,3},{4,5},{5,6},{6,7},{8,9},{9,10},{10,11},{12,13},{... | collective-permute-start | bytes 442376 | tf_op jit(solution)/shard_map/ppermute | solution.py:376
  7.6 6.5 %collective-permute-start.1 = (bf16[576,128]{1,0:T(8,128)(2,1)S(1)}, bf16[576,128]{1,0:T(8,128)(2,1)S(1)}, u32[]{:S(2)}, u32[]{:S(2)}) collective-permute-start(bf16[576,128]{1,0:T(8,128)(2,1)S(1)} %get-tuple-element.10), channel_id=1, source_target_pairs={{1,0},{2,1},{3,2},{5,4},{6,5},{7,6},{9,8},{10,9},{11,10},{13,12},{... | collective-permute-start | bytes 442376 | tf_op jit(solution)/shard_map/ppermute | solution.py:377
  18.3 10.4 %copy-start.7 = (s32[1024,16]{0,1:T(8,128)S(1)}, s32[1024,16]{0,1:T(8,128)}, u32[]{:S(2)}) copy-start(s32[1024,16]{0,1:T(8,128)} %param.9) | copy-start | bytes 196612
  18.3 11.2 %copy-start.3 = (s32[8,2,1024]{2,1,0:T(2,128)S(1)}, s32[8,2,1024]{2,1,0:T(2,128)}, u32[]{:S(2)}) copy-start(s32[8,2,1024]{2,1,0:T(2,128)} %offset_ref.5) | copy-start | bytes 196612
  18.3 11.2 %copy-start.5 = (f32[8,2,1024]{2,1,0:T(2,128)S(1)}, f32[8,2,1024]{2,1,0:T(2,128)}, u32[]{:S(2)}) copy-start(f32[8,2,1024]{2,1,0:T(2,128)} %phase_ref.5) | copy-start | bytes 196612
  18.3 27.4 %all-to-all-start = ((bf16[32,16,1152]{2,1,0:T(8,128)(2,1)}), bf16[32,16,1152]{2,1,0:T(8,128)(2,1)S(1)}, u32[]{:S(2)}, u32[]{:S(2)}) async-start(bf16[32,16,1152]{2,1,0:T(8,128)(2,1)} %shard_map.57), calls=%async_computation | async-start | bytes 2359296 | tf_op jit(solution)/shard_map/all_to_all | solution.py:400
  49.5 23.7 %all-to-all-start.1 = ((bf16[128,16,256]{2,1,0:T(8,128)(2,1)}), bf16[128,16,256]{2,1,0:T(8,128)(2,1)S(1)}, u32[]{:S(2)}, u32[]{:S(2)}) async-start(bf16[128,16,256]{2,1,0:T(8,128)(2,1)} %shard_map.59), calls=%async_computation.1 | async-start | bytes 2097152 | tf_op jit(solution)/shard_map/all_to_all | solution.py:438

commit v3 on v2

--- a/solution.py
+++ b/solution.py
@@ -25,6 +25,10 @@
     return pltpu.with_memory_space_constraint(value, VMEM)
 
 
+def far(value):
+    return pltpu.with_memory_space_constraint(value, pltpu.HBM)
+
+
 def params():
     return pltpu.CompilerParams(vmem_limit_bytes=24 * 2**20)
 
@@ -41,17 +45,28 @@
     return high, middle, low
 
 
-def rim_kernel(head_ref, tail_ref, offset_ref, phase_ref, left_ref, right_ref):
-    pulses = head_ref.shape[1]
-    levels, _, width = offset_ref.shape
+def rim_kernel(raw_ref, offset_ref, phase_ref, left_ref, right_ref, offset_rim, phase_rim, semaphore):
+    _, pulses, width = raw_ref.shape
+    levels = offset_ref.shape[0]
     rows = 2 * levels
-    for edge_ref, out_ref, start in ((head_ref, left_ref, 0), (tail_ref, right_ref, width - LANES)):
-        cut = slice(start, start + LANES)
-        out_ref[:pulses] = edge_ref[0]
-        out_ref[pulses : 2 * pulses] = edge_ref[1]
+    copies = []
+    for side, (out_ref, start) in enumerate(((left_ref, 0), (right_ref, width - LANES))):
+        cut = pl.ds(start, LANES)
+        for source, target in (
+            (raw_ref.at[0, :, cut], out_ref.at[:pulses]),
+            (raw_ref.at[1, :, cut], out_ref.at[pulses : 2 * pulses]),
+            (offset_ref.at[:, :, cut], offset_rim.at[side]),
+            (phase_ref.at[:, :, cut], phase_rim.at[side]),
+        ):
+            copy = pltpu.make_async_copy(source, target, semaphore.at[len(copies)])
+            copy.start()
+            copies.append(copy)
+    for copy in copies:
+        copy.wait()
+    for side, out_ref in enumerate((left_ref, right_ref)):
         at = 2 * pulses
-        offsets = jnp.concatenate([offset_ref[l, :, cut] for l in range(levels)], axis=0)
-        angles = jnp.concatenate([phase_ref[l, :, cut] for l in range(levels)], axis=0)
+        offsets = jnp.concatenate([offset_rim[side, l] for l in range(levels)], axis=0)
+        angles = jnp.concatenate([phase_rim[side, l] for l in range(levels)], axis=0)
         out_ref[at : at + rows] = offsets.astype(F32).astype(BF16)
         for part in split_three(angles):
             at += rows
@@ -79,16 +94,31 @@
     return jnp.where(beyond, gathered(following, index), gathered(here, index))
 
 
-def steer(levels, total, offset_ref, phase_ref, left_ref, right_ref, rows_ref, pair_refs, index_ref, trig_ref):
+def steer(
+    levels,
+    total,
+    inner_blocks,
+    out_blocks,
+    offset_ref,
+    phase_ref,
+    rims,
+    rows_ref,
+    pair_refs,
+    index_ref,
+    trig_ref,
+):
     all_levels, _, width = offset_ref.shape
     columns = rows_ref.shape[2]
     blocks = columns // LANES
     rim_rows = 2 * all_levels
-    base = left_ref.shape[0] - 4 * rim_rows
     first, count = levels[0], 2 * len(levels)
     start = lax.axis_index("rg") * width - LANES
 
     def rim(ref):
+        if ref is None:
+            blank = jnp.zeros((count, LANES), F32)
+            return blank, blank
+        base = ref.shape[0] - 4 * rim_rows
         aligned = first * 2 // 16 * 16
         parts = [
             ref[base + k * rim_rows + aligned : base + (k + 1) * rim_rows, :].astype(F32)[
@@ -98,8 +128,7 @@
         ]
         return parts[0], parts[1] + parts[2] + parts[3]
 
-    left_offset, left_phase = rim(left_ref)
-    right_offset, right_phase = rim(right_ref)
+    (left_offset, left_phase), (right_offset, right_phase) = map(rim, rims)
     middle_offset = jnp.concatenate([offset_ref[l] for l in levels], axis=0).astype(F32)
     middle_phase = jnp.concatenate([phase_ref[l] for l in levels], axis=0)
     offsets = jnp.concatenate([left_offset, middle_offset, right_offset], axis=1)
@@ -121,7 +150,7 @@
         group = max(inner, 8)
         source, target = pair_refs[(at + 1) % 2], pair_refs[at % 2]
         last = at == len(levels) - 1
-        for block in range(index_ref.shape[1] // LANES if last else blocks):
+        for block in out_blocks if last else inner_blocks:
             lanes = slice(block * LANES, (block + 1) * LANES)
             ahead = min(block + 1, blocks - 1)
             beyond_lanes = slice(ahead * LANES, (ahead + 1) * LANES)
@@ -164,14 +193,27 @@
                         target[2, rows, lanes] = imag[:used]
 
 
-def steer_kernel(levels, total, offset_ref, phase_ref, left_ref, right_ref, index_ref, trig_ref, rows_ref, even_ref, odd_ref):
+def steer_kernel(
+    levels,
+    total,
+    offset_ref,
+    phase_ref,
+    left_ref,
+    right_ref,
+    index_ref,
+    trig_ref,
+    rows_ref,
+    even_ref,
+    odd_ref,
+):
     steer(
         levels,
         total,
+        range(rows_ref.shape[2] // LANES),
+        range(index_ref.shape[1] // LANES),
         offset_ref,
         phase_ref,
-        left_ref,
-        right_ref,
+        (left_ref, right_ref),
         rows_ref,
         (even_ref, odd_ref),
         index_ref,
@@ -212,9 +254,99 @@
     return values
 
 
-def first_merges_kernel(
+def filter_block(tiles, table_ref):
+    parts = [
+        lax.dot_general(
+            jnp.concatenate(tiles[part], axis=1),
+            table_ref[part],
+            (((1,), (1,)), ((), ())),
+            preferred_element_type=F32,
+        )
+        for part in range(2)
+    ]
+    return parts[0] + parts[1]
+
+
+def merge_first(levels, field_ref, here_lanes, next_lanes, lanes, index_ref, trig_ref, term_ref, out_ref):
+    pulses = field_ref.shape[1]
+    combinations = 1 << levels
+    chunk = pulses // combinations
+    for at in range(combinations):
+        steering = combination(index_ref, trig_ref, at, lanes, chunk)
+        rows = slice(at * chunk, (at + 1) * chunk)
+        here = [field_ref[part, rows, here_lanes] for part in range(2)]
+        following = [field_ref[part, rows, next_lanes] for part in range(2)]
+        term_ref[0, at], term_ref[1, at] = term_of(here, following, steering)
+    for tile in range(chunk // 8):
+        cut = slice(8 * tile, 8 * tile + 8)
+        real, imag = (
+            sums_and_differences([term_ref[part, at, cut] for at in range(combinations)])
+            for part in range(2)
+        )
+        for at in range(combinations):
+            out_ref[at * (chunk // 8) + tile, :, lanes] = jnp.concatenate(
+                [real[at], imag[at]], axis=0
+            ).astype(BF16)
+
+
+def inner_merges_kernel(
     levels,
     total,
+    raw_ref,
+    table_ref,
+    offset_ref,
+    phase_ref,
+    out_ref,
+    ends_ref,
+    field_ref,
+    term_ref,
+    index_ref,
+    trig_ref,
+    rows_ref,
+    even_ref,
+    odd_ref,
+):
+    tiles = raw_ref.shape[2] // LANES
+    for block in range(1, tiles):
+        cut = slice((block - 1) * LANES, (block + 1) * LANES)
+        both = filter_block([[raw_ref[part, :, cut]] for part in range(2)], table_ref)
+        lanes = slice(block * LANES, (block + 1) * LANES)
+        for part in range(2):
+            values = both[:, part * LANES : (part + 1) * LANES]
+            field_ref[part, :, lanes] = values
+            if block == 1:
+                ends_ref[part, :, :LANES] = values
+            if block == tiles - 1:
+                ends_ref[part, :, LANES:] = values
+    steer(
+        range(levels),
+        total,
+        range(1, tiles),
+        range(1, tiles - 1),
+        offset_ref,
+        phase_ref,
+        (None, None),
+        rows_ref,
+        (even_ref, odd_ref),
+        index_ref,
+        trig_ref,
+    )
+
+    def merge_block(block, carry):
+        lanes, beyond = at_block(block), at_block(block + 1)
+        merge_first(
+            levels, field_ref, lanes, beyond, lanes, index_ref, trig_ref, term_ref, out_ref
+        )
+        return carry
+
+    lax.fori_loop(1, tiles - 1, merge_block, 0)
+
+
+def outer_merges_kernel(
+    levels,
+    total,
+    partial_ref,
+    ends_ref,
     raw_ref,
     left_ref,
     right_ref,
@@ -231,74 +363,54 @@
     odd_ref,
 ):
     pulses, width = raw_ref.shape[1], raw_ref.shape[2]
-    blocks = out_ref.shape[2] // LANES
+    tiles = width // LANES
     start = lax.axis_index("rg") * width - LEAD
-    dims = (((1,), (1,)), ((), ()))
-    for block in range(blocks):
-        parts = []
+
+    def held(position):
+        return slice(position * LANES, (position + 1) * LANES)
+
+    for position, block in ((0, 0), (3, tiles)):
+        pair = []
         for part in range(2):
-            tiles = []
-            for tile in (block, block + 1):
-                if tile == 0:
-                    tiles.append(left_ref[part * pulses : (part + 1) * pulses, :])
-                elif tile == blocks:
-                    tiles.append(right_ref[part * pulses : (part + 1) * pulses, :])
-                else:
-                    tiles.append(raw_ref[part, :, (tile - 1) * LANES : tile * LANES])
-            parts.append(
-                lax.dot_general(
-                    jnp.concatenate(tiles, axis=1),
-                    table_ref[part],
-                    dims,
-                    preferred_element_type=F32,
-                )
-            )
-        both = parts[0] + parts[1]
-        if block in (0, blocks - 1):
-            bins = start + block * LANES + (
-                lax.broadcasted_iota(jnp.int32, both.shape, 1) % LANES
-            )
-            both = jnp.where((bins >= 0) & (bins < total), both, 0.0)
-        lanes = slice(block * LANES, (block + 1) * LANES)
-        field_ref[0, :, lanes] = both[:, :LANES]
-        field_ref[1, :, lanes] = both[:, LANES:]
+            rows = slice(part * pulses, (part + 1) * pulses)
+            if block == 0:
+                pair.append([left_ref[rows, :], raw_ref[part, :, :LANES]])
+            else:
+                pair.append([raw_ref[part, :, width - LANES :], right_ref[rows, :]])
+        both = filter_block(pair, table_ref)
+        bins = start + block * LANES + (lax.broadcasted_iota(jnp.int32, both.shape, 1) % LANES)
+        both = jnp.where((bins >= 0) & (bins < total), both, 0.0)
+        for part in range(2):
+            field_ref[part, :, held(position)] = both[:, part * LANES : (part + 1) * LANES]
+    for part in range(2):
+        field_ref[part, :, LANES : 3 * LANES] = ends_ref[part]
+    middle = slice(LANES, (tiles - 1) * LANES)
+    out_ref[:, :, middle] = partial_ref[:, :, middle]
     steer(
         range(levels),
         total,
+        (0, 1, tiles - 1, tiles),
+        (0, tiles - 1, tiles),
         offset_ref,
         phase_ref,
-        left_ref,
-        right_ref,
+        (left_ref, right_ref),
         rows_ref,
         (even_ref, odd_ref),
         index_ref,
         trig_ref,
     )
-    combinations = 1 << levels
-    chunk = pulses // combinations
-
-    def merge_block(block, carry):
-        lanes = at_block(block)
-        beyond = at_block(jnp.minimum(block + 1, blocks - 1))
-        for at in range(combinations):
-            steering = combination(index_ref, trig_ref, at, lanes, chunk)
-            rows = slice(at * chunk, (at + 1) * chunk)
-            here = [field_ref[part, rows, lanes] for part in range(2)]
-            following = [field_ref[part, rows, beyond] for part in range(2)]
-            term_ref[0, at], term_ref[1, at] = term_of(here, following, steering)
-        for tile in range(chunk // 8):
-            cut = slice(8 * tile, 8 * tile + 8)
-            real, imag = (
-                sums_and_differences([term_ref[part, at, cut] for at in range(combinations)])
-                for part in range(2)
-            )
-            for at in range(combinations):
-                out_ref[at * (chunk // 8) + tile, :, lanes] = jnp.concatenate(
-                    [real[at], imag[at]], axis=0
-                ).astype(BF16)
-        return carry
-
-    lax.fori_loop(0, blocks, merge_block, 0)
+    for here, following, block in ((0, 1, 0), (2, 3, tiles - 1), (3, 3, tiles)):
+        merge_first(
+            levels,
+            field_ref,
+            held(here),
+            held(following),
+            slice(block * LANES, (block + 1) * LANES),
+            index_ref,
+            trig_ref,
+            term_ref,
+            out_ref,
+        )
 
 
 def last_merges_kernel(target_ref, moved_ref, index_ref, trig_ref, out_ref, term_ref):
@@ -330,18 +442,28 @@
     lax.fori_loop(0, out_blocks, merge_block, 0)
 
 
-def place_kernel(source_ref, incoming_ref, out_ref):
-    rows = out_ref.shape[1]
+def place_kernel(steps, source_ref, incoming_ref, out_ref, image_ref, semaphore):
+    _, rows, width = out_ref.shape
     tile_bins = incoming_ref.shape[2]
-    across = out_ref.shape[2] // tile_bins
-    base = pl.program_id(0) * (rows // 8) * across
-    for row in range(rows // 8):
-        for column in range(across):
-            tile = incoming_ref[source_ref[base + row * across + column]].astype(F32)
-            for part in range(2):
-                out_ref[
-                    part, row * 8 : row * 8 + 8, column * tile_bins : (column + 1) * tile_bins
-                ] = tile[8 * part : 8 * part + 8]
+    across = width // tile_bins
+    share = rows // steps
+    copies = []
+    for step in range(steps):
+        for row in range(step * share // 8, (step + 1) * share // 8):
+            for column in range(across):
+                tile = incoming_ref[source_ref[row * across + column]].astype(F32)
+                for part in range(2):
+                    image_ref[
+                        part, row * 8 : row * 8 + 8, column * tile_bins : (column + 1) * tile_bins
+                    ] = tile[8 * part : 8 * part + 8]
+        cut = pl.ds(step * share, share)
+        copy = pltpu.make_async_copy(
+            image_ref.at[:, cut, :], out_ref.at[:, cut, :], semaphore.at[step]
+        )
+        copy.start()
+        copies.append(copy)
+    for copy in copies:
+        copy.wait()
 
 
 def per_device(raw_echoes, chirp, range_offsets, phases, tile_table):
@@ -358,20 +480,19 @@
     rim_rows = 2 * pulses + 8 * level_count
     shape = jax.ShapeDtypeStruct
 
-    edge = (2, pulses, LANES)
-    last_edge = width // LANES - 1
+    anywhere = pl.BlockSpec(memory_space=pl.ANY)
     to_left, to_right = pl.pallas_call(
         rim_kernel,
-        grid=(1,),
         out_shape=[VMEM((rim_rows, LANES), BF16)] * 2,
         compiler_params=params(),
-        in_specs=[
-            pl.BlockSpec(edge, lambda i: (0, 0, 0)),
-            pl.BlockSpec(edge, lambda i: (0, 0, last_edge)),
-        ]
-        + whole(2),
+        in_specs=[pl.BlockSpec(memory_space=pltpu.HBM)] * 3,
         out_specs=whole(2),
-    )(raw_echoes, raw_echoes, *map(near, (range_offsets, phases)))
+        scratch_shapes=[
+            VMEM((2, level_count, 2, LANES), jnp.int32),
+            VMEM((2, level_count, 2, LANES), F32),
+            pltpu.SemaphoreType.DMA((8,)),
+        ],
+    )(*map(far, (raw_echoes, range_offsets, phases)))
     ends = rg_count - 1
     from_left = lax.ppermute(to_right, "rg", [(i, i + 1) for i in range(ends)])
     from_right = lax.ppermute(to_left, "rg", [(i + 1, i) for i in range(ends)])
@@ -383,20 +504,39 @@
         out_specs=whole(1)[0],
     )(chirp)
     inner = 1 << inner_levels
-    merged = pl.pallas_call(
-        functools.partial(first_merges_kernel, inner_levels, total),
-        out_shape=VMEM((ap_count, 2 * tile_rows, columns), BF16),
-        compiler_params=params(),
-        in_specs=whole(6),
-        out_specs=whole(1)[0],
-        scratch_shapes=[
-            VMEM((2, pulses, columns), F32),
+    near_raw, near_offsets, near_phases = map(near, (raw_echoes, range_offsets, phases))
+    merged_shape = VMEM((ap_count, 2 * tile_rows, columns), BF16)
+
+    def first_scratch(held):
+        return [
+            VMEM((2, pulses, held), F32),
             VMEM((2, inner, pulses // inner, LANES), F32),
             VMEM((inner, columns), jnp.int32),
             VMEM((2, inner, columns), F32),
-        ]
-        + steer_scratch(inner_levels, columns),
-    )(*map(near, (raw_echoes, from_left, from_right, table, range_offsets, phases)))
+        ] + steer_scratch(inner_levels, columns)
+
+    partial, field_ends = pl.pallas_call(
+        functools.partial(inner_merges_kernel, inner_levels, total),
+        out_shape=[merged_shape, VMEM((2, pulses, 2 * LANES), F32)],
+        compiler_params=params(),
+        in_specs=whole(4),
+        out_specs=whole(2),
+        scratch_shapes=first_scratch(columns),
+    )(near_raw, near(table), near_offsets, near_phases)
+    merged = pl.pallas_call(
+        functools.partial(outer_merges_kernel, inner_levels, total),
+        out_shape=merged_shape,
+        compiler_params=params(),
+        in_specs=whole(8),
+        out_specs=whole(1)[0],
+        scratch_shapes=first_scratch(4 * LANES),
+    )(
+        *map(near, (partial, field_ends)),
+        near_raw,
+        *map(near, (from_left, from_right, table)),
+        near_offsets,
+        near_phases,
+    )
     moved = lax.all_to_all(merged, "ap", split_axis=0, concat_axis=0, tiled=True)
     index, trig = pl.pallas_call(
         functools.partial(steer_kernel, range(inner_levels, level_count), total),
@@ -405,7 +545,7 @@
         in_specs=whole(4),
         out_specs=whole(2),
         scratch_shapes=steer_scratch(outer_levels, columns),
-    )(*map(near, (range_offsets, phases, from_left, from_right)))
+    )(near_offsets, near_phases, *map(near, (from_left, from_right)))
 
     ap_here, rg_here = lax.axis_index("ap"), lax.axis_index("rg")
     slot_row = tile_table // (rg_count * rg_count)
@@ -436,16 +576,16 @@
         ),
     )(send_to, *map(near, (moved, index, trig)))
     incoming = lax.all_to_all(outgoing, ("ap", "rg"), split_axis=0, concat_axis=0, tiled=True)
-    steps = 8
+    steps = 4
     return pl.pallas_call(
-        place_kernel,
+        functools.partial(place_kernel, steps),
         out_shape=shape((2, pulses, width), F32),
         compiler_params=params(),
         grid_spec=pltpu.PrefetchScalarGridSpec(
             num_scalar_prefetch=1,
-            grid=(steps,),
             in_specs=whole(1),
-            out_specs=pl.BlockSpec((2, pulses // steps, width), lambda i, s: (0, i, 0)),
+            out_specs=anywhere,
+            scratch_shapes=[VMEM((2, pulses, width), F32), pltpu.SemaphoreType.DMA((steps,))],
         ),
     )(source, near(incoming))
 

time: 77.1 us -> 71.5 us (0.927)
  local copies, waits for them, and re-layouts: 3.84 us -> 0.93 us
  waiting for transfers between devices: 38.2 us -> 35.9 us
    unnamed x17 -> x11, local copies, waits for them, and re-layouts: 3.22 us -> 0.32 us
    ppermute x1, waiting for transfers between devices: 4.38 us -> 2.07 us  [per_device(): from_right = lax.ppermute(to_left, 'rg', [(i + 1, i) for i in range(ends)])]
    pallas_call x3 -> x4, Pallas kernels: 7.82 us -> 7.4 us  [the longest x1 2.28 us: per_device(): pl.pallas_call(functools.partial(inner_merges_kernel, inner_levels, total...]
  transfers between devices with their start and end apart: 4 -> 4, of which waited for: 3 -> 3; matrix products, arithmetic and copies ran while one was open for 2% -> 2% of each run, Pallas kernels for 2% -> 5%
where the time goes in v3:
time: 71.5 us; the launch traced here: 71.1 us
  waiting for transfers between devices  35.9 us (50%)
  starting transfers between devices  21.3 us (30%)
  Pallas kernels  12.5 us (17%)
  local copies, waits for them, and re-layouts  0.93 us (1%)
    all_to_all x1, waiting for transfers between devices, per_device(): lax.all_to_all(outgoing, ('ap', 'rg'), split_axis=0, concat_axis=0, tiled...  18.9 us
    all_to_all x1, waiting for transfers between devices, per_device(): lax.all_to_all(merged, 'ap', split_axis=0, concat_axis=0, tiled=True)  15 us
    all_to_all x1, starting transfers between devices, per_device(): lax.all_to_all(merged, 'ap', split_axis=0, concat_axis=0, tiled=True)  10.4 us
    ppermute x1, starting transfers between devices, per_device(): from_left = lax.ppermute(to_right, 'rg', [(i, i + 1) for i in range(ends)])  4.5 us
    all_to_all x1, starting transfers between devices, per_device(): lax.all_to_all(outgoing, ('ap', 'rg'), split_axis=0, concat_axis=0, tiled...  4.49 us
    pallas_call x1, Pallas kernels, per_device(): pl.pallas_call(last_merges_kernel, out_shape=VMEM((devices, 2 * tile_rows...  3.72 us
    pallas_call x1, Pallas kernels, per_device(): pl.pallas_call(functools.partial(inner_merges_kernel, inner_levels, total...  2.28 us
    ppermute x1, waiting for transfers between devices, per_device(): from_right = lax.ppermute(to_left, 'rg', [(i + 1, i) for i in range(ends)])  2.07 us
  transfers between devices with their start and end apart: 4, of which 3 were waited for; matrix products, arithmetic and copies ran while one was open for 2% of the time, Pallas kernels for 5%

profile of v3, /device:TPU:1, one launch (start us, length us, event | category | flops | bytes accessed | tf_op | source)
XLA Modules:
  0.0 71.1 jit_solution(10694254123843681696)
XLA Ops:
  0.0 0.0 copy-start
  0.0 0.0 copy-start.1
  0.0 0.0 copy-start.2
  0.0 0.0 copy-start.3
  0.0 1.2 %shard_map.57 = (bf16[576,128]{1,0:T(8,128)(2,1)S(1)}, bf16[576,128]{1,0:T(8,128)(2,1)S(1)}) custom-call(bf16[2,256,1024]{2,1,0:T(8,128)(2,1)} %raw_ref.5, s32[8,2,1024]{2,1,0:T(2,128)} %offset_ref.7, f32[8,2,1024]{2,1,0:T(2,128)} %phase_ref.7), custom_call_target="tpu_custom_call" | custom-call | tf_op jit(solution)/shard_map/pallas_call | solution.py:484
  1.2 4.5 %collective-permute-start = (bf16[576,128]{1,0:T(8,128)(2,1)S(1)}, bf16[576,128]{1,0:T(8,128)(2,1)S(1)}, u32[]{:S(2)}, u32[]{:S(2)}) collective-permute-start(bf16[576,128]{1,0:T(8,128)(2,1)S(1)} %get-tuple-element.13), channel_id=1, source_target_pairs={{0,1},{1,2},{2,3},{4,5},{5,6},{6,7},{8,9},{9,10},{10,11},{12,13},{... | collective-permute-start | bytes 442376 | tf_op jit(solution)/shard_map/ppermute | solution.py:497
  5.7 1.9 %collective-permute-start.1 = (bf16[576,128]{1,0:T(8,128)(2,1)S(1)}, bf16[576,128]{1,0:T(8,128)(2,1)S(1)}, u32[]{:S(2)}, u32[]{:S(2)}) collective-permute-start(bf16[576,128]{1,0:T(8,128)(2,1)S(1)} %get-tuple-element.14), channel_id=1, source_target_pairs={{1,0},{2,1},{3,2},{5,4},{6,5},{7,6},{9,8},{10,9},{11,10},{13,12},{... | collective-permute-start | bytes 442376 | tf_op jit(solution)/shard_map/ppermute | solution.py:498
  7.6 0.0 copy-done.3
  7.6 0.1 shard_map.55.table_ref
  7.8 0.0 copy-done
  7.8 0.0 copy-done.1
  7.8 0.0 copy-done.2
  7.8 2.3 %shard_map.56 = (bf16[32,16,1152]{2,1,0:T(8,128)(2,1)S(1)}, f32[2,256,256]{2,1,0:T(8,128)S(1)}) custom-call(bf16[2,256,1024]{2,1,0:T(8,128)(2,1)S(1)} %copy-done, bf16[2,256,256]{2,1,0:T(8,128)(2,1)S(1)} %shard_map.55.table_ref, s32[8,2,1024]{2,1,0:T(2,128)S(1)} %copy-done.1, f32[8,2,1024]{2,1,0:T(2,128)S(1)} %copy-done.2), custom_call_target="tpu_custom_call" | custom-call | tf_op jit(solution)/shard_map/pallas_call | solution.py:518
  10.1 0.0 collective-permute-done.left_ref
  10.1 2.1 %collective-permute-done.1.right_ref = bf16[576,128]{1,0:T(8,128)(2,1)S(1)} collective-permute-done((bf16[576,128]{1,0:T(8,128)(2,1)S(1)}, bf16[576,128]{1,0:T(8,128)(2,1)S(1)}, u32[]{:S(2)}, u32[]{:S(2)}) %collective-permute-start.1) | collective-permute-done | bytes 147488 | tf_op jit(solution)/shard_map/ppermute | solution.py:498
  12.2 2.0 %shard_map.58 = bf16[32,16,1152]{2,1,0:T(8,128)(2,1)} custom-call(bf16[32,16,1152]{2,1,0:T(8,128)(2,1)S(1)} %get-tuple-element.11.partial_ref, f32[2,256,256]{2,1,0:T(8,128)S(1)} %get-tuple-element.12.ends_ref, bf16[2,256,1024]{2,1,0:T(8,128)(2,1)S(1)} %copy-done, bf16[576,128]{1,0:T(8,128)(2,1)S(1)} %collective-permute-done.left_ref, ...), custom_call_target="tpu_custom_call" | custom-call | tf_op jit(solution)/shard_map/pallas_call | solution.py:526
  14.2 0.0 copy-start.4
  14.2 10.4 %all-to-all-start = ((bf16[32,16,1152]{2,1,0:T(8,128)(2,1)}), bf16[32,16,1152]{2,1,0:T(8,128)(2,1)S(1)}, u32[]{:S(2)}, u32[]{:S(2)}) async-start(bf16[32,16,1152]{2,1,0:T(8,128)(2,1)} %shard_map.58), calls=%async_computation | async-start | bytes 2359296 | tf_op jit(solution)/shard_map/all_to_all | solution.py:540
  24.6 0.0 copy-done.4
  24.6 0.2 fusion.1
  24.8 0.1 reshape.10
  24.9 0.1 constant_dynamic-slice_fusion
  25.0 0.3 copy.12
  25.3 0.1 reshape.12.target_ref
  25.4 1.3 %shard_map.59 = (s32[32,1024]{1,0:T(8,128)S(1)}, f32[2,32,1024]{2,1,0:T(8,128)S(1)}) custom-call(s32[8,2,1024]{2,1,0:T(2,128)S(1)} %copy-done.1, f32[8,2,1024]{2,1,0:T(2,128)S(1)} %copy-done.2, bf16[576,128]{1,0:T(8,128)(2,1)S(1)} %collective-permute-done.left_ref, bf16[576,128]{1,0:T(8,128)(2,1)S(1)} %collective-permute-done.1.right_ref), custom_call_target="tpu_custom_call" | custom-call | tf_op jit(solution)/shard_map/pallas_call | solution.py:541
  26.7 15.0 %all-to-all-done.moved_ref = bf16[32,16,1152]{2,1,0:T(8,128)(2,1)S(1)} async-done(((bf16[32,16,1152]{2,1,0:T(8,128)(2,1)}), bf16[32,16,1152]{2,1,0:T(8,128)(2,1)S(1)}, u32[]{:S(2)}, u32[]{:S(2)}) %all-to-all-start) | async-done | bytes 1179680 | tf_op jit(solution)/shard_map/all_to_all | solution.py:540
  41.6 3.7 %shard_map.60 = bf16[128,16,256]{2,1,0:T(8,128)(2,1)} custom-call(s32[128]{0:T(128)S(1)} %reshape.12.target_ref, bf16[32,16,1152]{2,1,0:T(8,128)(2,1)S(1)} %all-to-all-done.moved_ref, s32[32,1024]{1,0:T(8,128)S(1)} %get-tuple-element.15.index_ref, f32[2,32,1024]{2,1,0:T(8,128)S(1)} %get-tuple-element.16.trig_ref), custom_call_target="tpu_custom_call" | custom-call | tf_op jit(solution)/shard_map/pallas_call | solution.py:567
  45.3 4.5 %all-to-all-start.1 = ((bf16[128,16,256]{2,1,0:T(8,128)(2,1)}), bf16[128,16,256]{2,1,0:T(8,128)(2,1)S(1)}, u32[]{:S(2)}, u32[]{:S(2)}) async-start(bf16[128,16,256]{2,1,0:T(8,128)(2,1)} %shard_map.60), calls=%async_computation.1 | async-start | bytes 2097152 | tf_op jit(solution)/shard_map/all_to_all | solution.py:578
  49.8 0.1 reshape.11
  50.0 0.1 select_reduce_fusion
  50.0 0.1 copy.10
  50.1 0.1 eq.27
  50.2 0.1 select_reduce_fusion.1.source_ref
  50.3 18.9 %all-to-all-done.1.incoming_ref = bf16[128,16,256]{2,1,0:T(8,128)(2,1)S(1)} async-done(((bf16[128,16,256]{2,1,0:T(8,128)(2,1)}), bf16[128,16,256]{2,1,0:T(8,128)(2,1)S(1)}, u32[]{:S(2)}, u32[]{:S(2)}) %all-to-all-start.1) | async-done | bytes 1048608 | tf_op jit(solution)/shard_map/all_to_all | solution.py:578
  69.2 1.9 %shard_map.61 = f32[2,256,1024]{2,1,0:T(8,128)} custom-call(s32[128]{0:T(128)S(1)} %select_reduce_fusion.1.source_ref, bf16[128,16,256]{2,1,0:T(8,128)(2,1)S(1)} %all-to-all-done.1.incoming_ref), custom_call_target="tpu_custom_call" | custom-call | tf_op jit(solution)/shard_map/pallas_call | solution.py:580
Async XLA Ops:
  0.0 7.8 %copy-start = (bf16[2,256,1024]{2,1,0:T(8,128)(2,1)S(1)}, bf16[2,256,1024]{2,1,0:T(8,128)(2,1)}, u32[]{:S(2)}) copy-start(bf16[2,256,1024]{2,1,0:T(8,128)(2,1)} %raw_ref.5) | copy-start | bytes 3145732
  0.0 7.8 %copy-start.1 = (s32[8,2,1024]{2,1,0:T(2,128)S(1)}, s32[8,2,1024]{2,1,0:T(2,128)}, u32[]{:S(2)}) copy-start(s32[8,2,1024]{2,1,0:T(2,128)} %offset_ref.7) | copy-start | bytes 196612
  0.0 7.8 %copy-start.2 = (f32[8,2,1024]{2,1,0:T(2,128)S(1)}, f32[8,2,1024]{2,1,0:T(2,128)}, u32[]{:S(2)}) copy-start(f32[8,2,1024]{2,1,0:T(2,128)} %phase_ref.7) | copy-start | bytes 196612
  0.0 7.6 %copy-start.3 = (f32[2,128]{1,0:T(2,128)S(1)}, f32[2,128]{1,0:T(2,128)}, u32[]{:S(2)}) copy-start(f32[2,128]{1,0:T(2,128)} %chirp_ref.1) | copy-start | bytes 3076
  1.2 8.9 %collective-permute-start = (bf16[576,128]{1,0:T(8,128)(2,1)S(1)}, bf16[576,128]{1,0:T(8,128)(2,1)S(1)}, u32[]{:S(2)}, u32[]{:S(2)}) collective-permute-start(bf16[576,128]{1,0:T(8,128)(2,1)S(1)} %get-tuple-element.13), channel_id=1, source_target_pairs={{0,1},{1,2},{2,3},{4,5},{5,6},{6,7},{8,9},{9,10},{10,11},{12,13},{... | collective-permute-start | bytes 442376 | tf_op jit(solution)/shard_map/ppermute | solution.py:497
  5.7 6.5 %collective-permute-start.1 = (bf16[576,128]{1,0:T(8,128)(2,1)S(1)}, bf16[576,128]{1,0:T(8,128)(2,1)S(1)}, u32[]{:S(2)}, u32[]{:S(2)}) collective-permute-start(bf16[576,128]{1,0:T(8,128)(2,1)S(1)} %get-tuple-element.14), channel_id=1, source_target_pairs={{1,0},{2,1},{3,2},{5,4},{6,5},{7,6},{9,8},{10,9},{11,10},{13,12},{... | collective-permute-start | bytes 442376 | tf_op jit(solution)/shard_map/ppermute | solution.py:498
  14.2 10.4 %copy-start.4 = (s32[1024,16]{0,1:T(8,128)S(1)}, s32[1024,16]{0,1:T(8,128)}, u32[]{:S(2)}) copy-start(s32[1024,16]{0,1:T(8,128)} %param.9) | copy-start | bytes 196612
  14.2 27.4 %all-to-all-start = ((bf16[32,16,1152]{2,1,0:T(8,128)(2,1)}), bf16[32,16,1152]{2,1,0:T(8,128)(2,1)S(1)}, u32[]{:S(2)}, u32[]{:S(2)}) async-start(bf16[32,16,1152]{2,1,0:T(8,128)(2,1)} %shard_map.58), calls=%async_computation | async-start | bytes 2359296 | tf_op jit(solution)/shard_map/all_to_all | solution.py:540
  45.3 23.9 %all-to-all-start.1 = ((bf16[128,16,256]{2,1,0:T(8,128)(2,1)}), bf16[128,16,256]{2,1,0:T(8,128)(2,1)S(1)}, u32[]{:S(2)}, u32[]{:S(2)}) async-start(bf16[128,16,256]{2,1,0:T(8,128)(2,1)} %shard_map.60), calls=%async_computation.1 | async-start | bytes 2097152 | tf_op jit(solution)/shard_map/all_to_all | solution.py:578

commit v4 on v3

v4 whole, which is shorter than its diff:
```python
import functools
import math

import jax
import jax.numpy as jnp
from jax import lax
from jax.experimental import pallas as pl
from jax.experimental.pallas import tpu as pltpu
from jax.sharding import PartitionSpec as P

ROOT_HALF = 0.7071067811865476
LANES = 128
STEP = 8
LEAD = 64
VMEM = pltpu.VMEM
BF16 = jnp.bfloat16
F32 = jnp.float32


def whole(count):
    return [pl.BlockSpec(memory_space=VMEM)] * count


def near(value):
    return pltpu.with_memory_space_constraint(value, VMEM)


def far(value):
    return pltpu.with_memory_space_constraint(value, pltpu.HBM)


def params():
    return pltpu.CompilerParams(vmem_limit_bytes=24 * 2**20)


def at_block(block):
    return pl.ds(pl.multiple_of(block * LANES, LANES), LANES)


def split_three(values):
    high = values.astype(BF16)
    rest = values - high.astype(F32)
    middle = rest.astype(BF16)
    low = (rest - middle.astype(F32)).astype(BF16)
    return high, middle, low


def rim_kernel(
    raw_ref,
    chirp_ref,
    offset_ref,
    phase_ref,
    left_ref,
    right_ref,
    near_chirp,
    near_offset,
    near_phase,
    semaphore,
):
    _, pulses, width = raw_ref.shape
    levels = offset_ref.shape[0]
    rows = 2 * levels
    copies = []
    for source, target in (
        (offset_ref, near_offset),
        (phase_ref, near_phase),
        (raw_ref.at[0, :, pl.ds(0, LANES)], left_ref.at[:pulses]),
        (raw_ref.at[1, :, pl.ds(0, LANES)], left_ref.at[pulses : 2 * pulses]),
        (raw_ref.at[0, :, pl.ds(width - LANES, LANES)], right_ref.at[:pulses]),
        (raw_ref.at[1, :, pl.ds(width - LANES, LANES)], right_ref.at[pulses : 2 * pulses]),
        (chirp_ref, near_chirp),
    ):
        copy = pltpu.make_async_copy(source, target, semaphore.at[len(copies)])
        copy.start()
        copies.append(copy)
    for copy in copies[:2]:
        copy.wait()
    for start, out_ref in ((0, left_ref), (width - LANES, right_ref)):
        cut = slice(start, start + LANES)
        at = 2 * pulses
        offsets = jnp.concatenate([near_offset[l, :, cut] for l in range(levels)], axis=0)
        angles = jnp.concatenate([near_phase[l, :, cut] for l in range(levels)], axis=0)
        out_ref[at : at + rows] = offsets.astype(F32).astype(BF16)
        for part in split_three(angles):
            at += rows
            out_ref[at : at + rows] = part
    for copy in copies[2:]:
        copy.wait()


def fill_toeplitz(chirp_ref, table_ref):
    taps = chirp_ref[...].astype(BF16).astype(F32)
    zeros = jnp.zeros((1, LANES), F32)
    rolled = []
    for part in range(2):
        row = jnp.concatenate([taps[part : part + 1], zeros], axis=1)
        spread = jnp.broadcast_to(row, (LANES, 2 * LANES))
        rolled.append(pltpu.roll(spread, 0, 1, stride=1, stride_axis=0))
    real, imag = rolled
    table_ref[0] = jnp.concatenate([real, -imag], axis=0).astype(BF16)
    table_ref[1] = jnp.concatenate([imag, real], axis=0).astype(BF16)


def gathered(values, index):
    return lax.gather(
        values,
        index[:, :, None],
        lax.GatherDimensionNumbers(
            offset_dims=(),
            collapsed_slice_dims=(1,),
            start_index_map=(1,),
            operand_batching_dims=(0,),
            start_indices_batching_dims=(0,),
        ),
        slice_sizes=(1, 1),
        mode=lax.GatherScatterMode.PROMISE_IN_BOUNDS,
    )


def picked(here, following, index, beyond):
    return jnp.where(beyond, gathered(following, index), gathered(here, index))


def scaled_trig(angles):
    return jnp.cos(angles) * ROOT_HALF, jnp.sin(angles) * ROOT_HALF


def align(values, blocks, sources_of, rows_ref):
    width = values[0].shape[1]
    lanes = slice(blocks[0] * LANES, (blocks[-1] + 1) * LANES)
    count = len(blocks) * LANES
    for level, (slot, side) in enumerate(sources_of):
        shift = (width - (LANES - LEAD + STEP * (level + 1))) % width
        group, row = 2 * level // 8 * 8, 2 * level % 8
        for part in range(3):
            moved = values[part][group : group + 8]
            if shift:
                moved = pltpu.roll(moved, shift, 1)
            pair = moved[row : row + 2, :count]
            if side is None:
                rows_ref[part, slot : slot + 2, lanes] = pair
            else:
                rows_ref[part, slot : slot + 1, lanes] = jnp.where(side == 1, pair[1:2], pair[0:1])


def sources(levels, inner_levels):
    here = lax.axis_index("ap")
    return [
        (2 * level, None)
        if level < inner_levels
        else (inner_levels + level, (here >> (level - inner_levels)) & 1)
        for level in range(levels)
    ]


def compose(outer, inner, inner_beyond, lane):
    step, cos_out, sin_out = outer
    index = lane + step.astype(jnp.int32)
    beyond = index >= LANES
    index = index & (LANES - 1)
    moved, cos_in, sin_in = (
        picked(a, b, index, beyond) for a, b in zip(inner, inner_beyond)
    )
    return (
        step + moved,
        cos_out * cos_in - sin_out * sin_in,
        cos_out * sin_in + sin_out * cos_in,
    )


def steer(levels, inner_levels, blocks, rows_ref, index_ref, trig_ref):
    lane = lax.broadcasted_iota(jnp.int32, (8, LANES), 1)
    last = blocks[-1]

    def row(slot, block):
        lanes = slice(block * LANES, (block + 1) * LANES)
        return tuple(
            jnp.broadcast_to(rows_ref[part, slot : slot + 1, lanes], (8, LANES))
            for part in range(3)
        )

    def chain(outer_of, inner):
        return {
            block: compose(outer_of(block), inner[block], inner[min(block + 1, last)], lane)
            for block in blocks
        }

    own = {block: row(2 * inner_levels, block) for block in blocks}
    for level in range(inner_levels + 1, levels):
        own = chain(lambda block: row(inner_levels + level, block), own)

    sublane = lax.broadcasted_iota(jnp.int32, (8, LANES), 0)
    inner = {}
    for block in blocks:
        low, high = row(0, block), row(1, block)
        inner[block] = tuple(
            jnp.where(sublane % 2 == 0, a, b) for a, b in zip(low, high)
        )
    for level in range(1, inner_levels):
        bit = (sublane >> level) & 1

        def outer_of(block):
            low, high = row(2 * level, block), row(2 * level + 1, block)
            return tuple(jnp.where(bit == 0, a, b) for a, b in zip(low, high))

        inner = chain(outer_of, inner)

    for block in blocks[:-1]:
        moved, cosine, sine = compose(own[block], inner[block], inner[block + 1], lane)
        reach = lane + moved.astype(jnp.int32)
        lanes = slice(block * LANES, (block + 1) * LANES)
        index_ref[0, :, lanes] = reach & (LANES - 1)
        index_ref[1, :, lanes] = reach - LANES
        trig_ref[0, :, lanes] = cosine
        trig_ref[1, :, lanes] = sine


def combination(index_ref, trig_ref, row, lanes, rows):
    def spread(values):
        return jnp.broadcast_to(values, (rows, LANES))

    index = spread(index_ref[0, row : row + 1, lanes])
    beyond = spread(index_ref[1, row : row + 1, lanes]) >= 0
    cosine = spread(trig_ref[0, row : row + 1, lanes])
    sine = spread(trig_ref[1, row : row + 1, lanes])
    return index, beyond, cosine, sine


def term_of(here, following, steering):
    index, beyond, cosine, sine = steering
    real, imag = (picked(a, b, index, beyond) for a, b in zip(here, following))
    return real * cosine - imag * sine, real * sine + imag * cosine


def sums_and_differences(values):
    values = list(values)
    distance = 1
    while distance < len(values):
        for at in range(len(values)):
            if not at & distance:
                low, high = values[at], values[at + distance]
                values[at], values[at + distance] = low + high, low - high
        distance *= 2
    return values


def filter_block(tiles, table_ref):
    parts = [
        lax.dot_general(
            jnp.concatenate(tiles[part], axis=1),
            table_ref[part],
            (((1,), (1,)), ((), ())),
            preferred_element_type=F32,
        )
        for part in range(2)
    ]
    return parts[0] + parts[1]


def merge_first(
    levels,
    field_ref,
    here_lanes,
    next_lanes,
    lanes,
    index_ref,
    trig_ref,
    term_ref,
    out_ref,
    out_lanes,
):
    pulses = field_ref.shape[1]
    combinations = 1 << levels
    chunk = pulses // combinations
    for at in range(combinations):
        steering = combination(index_ref, trig_ref, at, lanes, chunk)
        rows = slice(at * chunk, (at + 1) * chunk)
        here = [field_ref[part, rows, here_lanes] for part in range(2)]
        following = [field_ref[part, rows, next_lanes] for part in range(2)]
        term_ref[0, at], term_ref[1, at] = term_of(here, following, steering)
    for tile in range(chunk // 8):
        cut = slice(8 * tile, 8 * tile + 8)
        real, imag = (
            sums_and_differences([term_ref[part, at, cut] for at in range(combinations)])
            for part in range(2)
        )
        for at in range(combinations):
            out_ref[at * (chunk // 8) + tile, :, out_lanes] = jnp.concatenate(
                [real[at], imag[at]], axis=0
            ).astype(BF16)


def inner_merges_kernel(
    inner_levels,
    far_raw,
    chirp_ref,
    offset_ref,
    phase_ref,
    out_ref,
    ends_ref,
    steering_ref,
    table_ref,
    raw_ref,
    loaded,
    stored,
    merged_ref,
    field_ref,
    term_ref,
    index_ref,
    trig_ref,
    rows_ref,
):
    tiles = raw_ref.shape[2] // LANES
    levels = offset_ref.shape[0]
    loading = pltpu.make_async_copy(far_raw, raw_ref, loaded.at[0])
    loading.start()
    offsets = jnp.concatenate([offset_ref[l] for l in range(levels)], axis=0)
    angles = jnp.concatenate([phase_ref[l] for l in range(levels)], axis=0)
    values = (offsets.astype(F32) + (STEP - 4.0), *scaled_trig(angles))
    for part in range(3):
        steering_ref[part] = values[part]
    blank = jnp.zeros((2 * levels, LANES), F32)
    align(
        [jnp.concatenate([blank, value, blank], axis=1) for value in values],
        range(tiles + 1),
        sources(levels, inner_levels),
        rows_ref,
    )
    steer(levels, inner_levels, range(1, tiles), rows_ref, index_ref, trig_ref)
    fill_toeplitz(chirp_ref, table_ref)
    loading.wait()
    for block in range(1, tiles):
        cut = slice((block - 1) * LANES, (block + 1) * LANES)
        both = filter_block([[raw_ref[part, :, cut]] for part in range(2)], table_ref)
        lanes = slice(block * LANES, (block + 1) * LANES)
        for part in range(2):
            values = both[:, part * LANES : (part + 1) * LANES]
            field_ref[part, :, lanes] = values
            if block == 1:
                ends_ref[part, :, :LANES] = values
            if block == tiles - 1:
                ends_ref[part, :, LANES:] = values

    def stored_block(lanes):
        return pltpu.make_async_copy(
            merged_ref.at[:, :, lanes], out_ref.at[:, :, lanes], stored.at[0]
        )

    def merge_pair(pair, carry):
        for slot in range(2):
            block = 1 + 2 * pair + slot
            lanes, beyond = at_block(block), at_block(block + 1)
            merge_first(
                inner_levels,
                field_ref,
                lanes,
                beyond,
                lanes,
                index_ref,
                trig_ref,
                term_ref.at[slot],
                merged_ref,
                lanes,
            )
        both = pl.multiple_of((1 + 2 * pair) * LANES, LANES)
        stored_block(pl.ds(both, 2 * LANES)).start()
        return carry

    lax.fori_loop(0, (tiles - 2) // 2, merge_pair, 0)
    stored_block(pl.ds(LANES, (tiles - 2) * LANES)).wait()


def outer_merges_kernel(
    inner_levels,
    total,
    partial_ref,
    ends_ref,
    steering_ref,
    raw_ref,
    left_ref,
    right_ref,
    table_ref,
    out_ref,
    semaphore,
    merged_ref,
    field_ref,
    term_ref,
    index_ref,
    trig_ref,
    rows_ref,
):
    pulses, width = raw_ref.shape[1], raw_ref.shape[2]
    tiles = width // LANES
    rim_rows = steering_ref.shape[1]
    levels = rim_rows // 2
    start = lax.axis_index("rg") * width - LEAD
    own_sources = sources(levels, inner_levels)

    def held(position):
        return slice(position * LANES, (position + 1) * LANES)

    for rim_ref, at, near_lanes, blocks in (
        (left_ref, -LANES, slice(0, 2 * LANES), (0, 1)),
        (right_ref, width, slice(width - 2 * LANES, width), (tiles - 1, tiles)),
    ):
        offsets, high, middle, low = (
            rim_ref[2 * pulses + k * rim_rows : 2 * pulses + (k + 1) * rim_rows, :].astype(F32)
            for k in range(4)
        )
        cosine, sine = scaled_trig(high + middle + low)
        bins = lax.axis_index("rg") * width + at + lax.broadcasted_iota(
            jnp.int32, (rim_rows, LANES), 1
        )
        inside = (bins >= 0) & (bins < total)
        rim = (
            offsets + (STEP - 4.0),
            jnp.where(inside, cosine, 0.0),
            jnp.where(inside, sine, 0.0),
        )
        middle = [steering_ref[part, :, near_lanes] for part in range(3)]
        joined = [
            jnp.concatenate((a, b) if at < 0 else (b, a), axis=1) for a, b in zip(rim, middle)
        ]
        align(joined, blocks, own_sources, rows_ref)
        steer(levels, inner_levels, blocks, rows_ref, index_ref, trig_ref)

    for position, block in ((0, 0), (3, tiles)):
        pair = []
        for part in range(2):
            rows = slice(part * pulses, (part + 1) * pulses)
            if block == 0:
                pair.append([left_ref[rows, :], raw_ref[part, :, :LANES]])
            else:
                pair.append([raw_ref[part, :, width - LANES :], right_ref[rows, :]])
        both = filter_block(pair, table_ref)
        bins = start + block * LANES + (lax.broadcasted_iota(jnp.int32, both.shape, 1) % LANES)
        both = jnp.where((bins >= 0) & (bins < total), both, 0.0)
        for part in range(2):
            field_ref[part, :, held(position)] = both[:, part * LANES : (part + 1) * LANES]
    for part in range(2):
        field_ref[part, :, LANES : 3 * LANES] = ends_ref[part]
    copies = []
    for here, following, block in ((0, 1, 0), (2, 3, tiles - 1)):
        merge_first(
            inner_levels,
            field_ref,
            held(here),
            held(following),
            slice(block * LANES, (block + 1) * LANES),
            index_ref,
            trig_ref,
            term_ref.at[len(copies)],
            merged_ref.at[len(copies)],
            slice(0, LANES),
        )
        copy = pltpu.make_async_copy(
            merged_ref.at[len(copies)],
            out_ref.at[:, :, pl.ds(block * LANES, LANES)],
            semaphore.at[len(copies)],
        )
        copy.start()
        copies.append(copy)
    for copy in copies:
        copy.wait()


def last_sums_kernel(target_ref, moved_ref, out_ref, tile_ref, term_ref, semaphore):
    holders, rows, columns = moved_ref.shape
    per_tile = out_ref.shape[2] // LANES
    tiles_across = columns // out_ref.shape[2]
    near_group = min(8, holders)
    for column in range(tiles_across):
        for part in range(per_tile):
            block = column * per_tile + part
            lanes = slice(block * LANES, (block + 1) * LANES)
            inner = slice(part * LANES, (part + 1) * LANES)
            slot = block % 2
            for first in range(0, holders, near_group):
                sums = sums_and_differences(
                    [moved_ref[first + at, :, lanes].astype(F32) for at in range(near_group)]
                )
                for at in range(near_group):
                    term_ref[slot, first + at] = sums[at]
            for first in range(near_group):
                members = range(first, holders, near_group)
                sums = sums_and_differences([term_ref[slot, at] for at in members])
                for at, value in zip(members, sums):
                    tile_ref[column, at, :, inner] = value.astype(BF16)
        for at in range(holders):
            to = target_ref[at * tiles_across + column]
            pltpu.make_async_copy(
                tile_ref.at[column, at], out_ref.at[to], semaphore.at[column]
            ).start()
    for column in range(tiles_across):
        pltpu.make_async_copy(
            tile_ref.at[column], out_ref.at[pl.ds(0, holders)], semaphore.at[column]
        ).wait()


def place_kernel(steps, source_ref, incoming_ref, out_ref, image_ref, semaphore):
    _, rows, width = out_ref.shape
    tile_bins = incoming_ref.shape[2]
    across = width // tile_bins
    share = rows // steps
    copies = []
    for step in range(steps):
        for row in range(step * share // 8, (step + 1) * share // 8):
            for column in range(across):
                tile = incoming_ref[source_ref[row * across + column]].astype(F32)
                for part in range(2):
                    image_ref[
                        part, row * 8 : row * 8 + 8, column * tile_bins : (column + 1) * tile_bins
                    ] = tile[8 * part : 8 * part + 8]
        cut = pl.ds(step * share, share)
        copy = pltpu.make_async_copy(
            image_ref.at[:, cut, :], out_ref.at[:, cut, :], semaphore.at[step]
        )
        copy.start()
        copies.append(copy)
    for copy in copies:
        copy.wait()


def per_device(raw_echoes, chirp, range_offsets, phases, tile_table):
    ap_count, rg_count = lax.axis_size("ap"), lax.axis_size("rg")
    devices = ap_count * rg_count
    _, pulses, width = raw_echoes.shape
    level_count = range_offsets.shape[0]
    total = width * rg_count
    outer_levels = ap_count.bit_length() - 1
    inner_levels = level_count - outer_levels
    tile_rows = pulses // ap_count
    tile_bins = width // rg_count
    rim_rows = 2 * pulses + 8 * level_count
    shape = jax.ShapeDtypeStruct

    anywhere = pl.BlockSpec(memory_space=pl.ANY)
    distant = pl.BlockSpec(memory_space=pltpu.HBM)
    to_left, to_right, near_chirp, near_offsets, near_phases = pl.pallas_call(
        rim_kernel,
        out_shape=[VMEM((rim_rows, LANES), BF16)] * 2
        + [
            VMEM(chirp.shape, F32),
            VMEM(range_offsets.shape, jnp.int32),
            VMEM(phases.shape, F32),
        ],
        compiler_params=params(),
        in_specs=[distant] * 4,
        out_specs=whole(5),
        scratch_shapes=[pltpu.SemaphoreType.DMA((7,))],
    )(*map(far, (raw_echoes, chirp, range_offsets, phases)))
    ends = rg_count - 1
    from_left = lax.ppermute(to_right, "rg", [(i, i + 1) for i in range(ends)])
    from_right = lax.ppermute(to_left, "rg", [(i + 1, i) for i in range(ends)])
    inner = 1 << inner_levels
    merged_shape = pltpu.HBM((ap_count, 2 * tile_rows, width), BF16)

    def first_scratch(held):
        return [
            VMEM((2, pulses, held), F32),
            VMEM((2, 2, inner, pulses // inner, LANES), F32),
            VMEM((2, inner, width), jnp.int32),
            VMEM((2, inner, width), F32),
            VMEM((3, inner_levels + level_count, width + LANES), F32),
        ]

    partial, field_ends, steering, table, near_raw = pl.pallas_call(
        functools.partial(inner_merges_kernel, inner_levels),
        out_shape=[
            merged_shape,
            VMEM((2, pulses, 2 * LANES), F32),
            VMEM((3, 2 * level_count, width), F32),
            VMEM((2, 2 * LANES, 2 * LANES), BF16),
            VMEM(raw_echoes.shape, BF16),
        ],
        compiler_params=params(),
        in_specs=[distant] + whole(3),
        out_specs=[distant] + whole(4),
        scratch_shapes=[
            pltpu.SemaphoreType.DMA((1,)),
            pltpu.SemaphoreType.DMA((1,)),
            VMEM((ap_count, 2 * tile_rows, width), BF16),
        ]
        + first_scratch(width),
    )(far(raw_echoes), *map(near, (near_chirp, near_offsets, near_phases)))
    merged = pl.pallas_call(
        functools.partial(outer_merges_kernel, inner_levels, total),
        out_shape=merged_shape,
        compiler_params=params(),
        in_specs=[distant] + whole(6),
        out_specs=distant,
        input_output_aliases={0: 0},
        scratch_shapes=[
            pltpu.SemaphoreType.DMA((2,)),
            VMEM((2, ap_count, 2 * tile_rows, LANES), BF16),
        ]
        + first_scratch(4 * LANES),
    )(
        far(partial),
        *map(near, (field_ends, steering, near_raw, from_left, from_right, table)),
    )
    moved = lax.all_to_all(merged, "ap", split_axis=0, concat_axis=0, tiled=True)

    ap_here, rg_here = lax.axis_index("ap"), lax.axis_index("rg")
    slot_row = tile_table // (rg_count * rg_count)
    slot_col = tile_table % (rg_count * rg_count)
    target = slot_row // ap_count * rg_count + slot_col // rg_count
    shaped = (ap_count, ap_count, rg_count, rg_count)
    target = target.reshape(shaped)
    local_slot = (slot_row % ap_count * rg_count + slot_col % rg_count).reshape(shaped)
    mine = target == ap_here * rg_count + rg_here
    slot_from = jnp.sum(jnp.where(mine, local_slot, 0), axis=(0, 3)).reshape(devices)
    ids = jnp.arange(devices, dtype=jnp.int32)
    source = jnp.sum(
        jnp.where(slot_from[None, :] == ids[:, None], ids[None, :], 0), axis=1
    )
    send_to = lax.dynamic_slice(
        target, (0, ap_here, rg_here, 0), (ap_count, 1, 1, rg_count)
    ).reshape(devices)

    outgoing = pl.pallas_call(
        last_sums_kernel,
        out_shape=pltpu.HBM((devices, 2 * tile_rows, tile_bins), BF16),
        compiler_params=params(),
        grid_spec=pltpu.PrefetchScalarGridSpec(
            num_scalar_prefetch=1,
            in_specs=whole(1),
            out_specs=distant,
            scratch_shapes=[
                VMEM((rg_count, ap_count, 2 * tile_rows, tile_bins), BF16),
                VMEM((2, ap_count, 2 * tile_rows, LANES), F32),
                pltpu.SemaphoreType.DMA((rg_count,)),
            ],
        ),
    )(send_to, near(moved))
    incoming = lax.all_to_all(outgoing, ("ap", "rg"), split_axis=0, concat_axis=0, tiled=True)
    steps = 4
    return pl.pallas_call(
        functools.partial(place_kernel, steps),
        out_shape=shape((2, pulses, width), F32),
        compiler_params=params(),
        grid_spec=pltpu.PrefetchScalarGridSpec(
            num_scalar_prefetch=1,
            in_specs=whole(1),
            out_specs=anywhere,
            scratch_shapes=[VMEM((2, pulses, width), F32), pltpu.SemaphoreType.DMA((steps,))],
        ),
    )(source, near(incoming))


def solution(mesh):
    placed = (P(None, "ap", "rg"), P(), P(None, None, "rg"), P(None, None, "rg"), P())
    return jax.shard_map(
        per_device, mesh=mesh, in_specs=placed, out_specs=P(None, "ap", "rg"), check_vma=False
    )
```

time: 71.5 us -> 69.5 us (0.972)
  Pallas kernels: 12.5 us -> 10.7 us
    pallas_call x5 -> x3, Pallas kernels: 8.57 us -> 6.96 us  [the longest x1 3.93 us: per_device(): pl.pallas_call(functools.partial(inner_merges_kernel, inner_levels), out_...]
    ppermute x1, waiting for transfers between devices: 2.07 us -> 0.59 us  [per_device(): from_right = lax.ppermute(to_left, 'rg', [(i + 1, i) for i in range(ends)])]
    all_to_all x1, waiting for transfers between devices: 15 us -> 15.9 us  [per_device(): lax.all_to_all(merged, 'ap', split_axis=0, concat_axis=0, tiled=True)]
  transfers between devices with their start and end apart: 4 -> 4, of which waited for: 3 -> 3; matrix products, arithmetic and copies ran while one was open for 2% -> 2% of each run, Pallas kernels for 5% -> 6%
where the time goes in v4:
time: 69.5 us; the launch traced here: 69.1 us
  waiting for transfers between devices  35.3 us (51%)
  starting transfers between devices  21.7 us (31%)
  Pallas kernels  10.7 us (15%)
  local copies, waits for them, and re-layouts  0.92 us (1%)
    all_to_all x1, waiting for transfers between devices, per_device(): lax.all_to_all(outgoing, ('ap', 'rg'), split_axis=0, concat_axis=0, tiled...  18.9 us
    all_to_all x1, waiting for transfers between devices, per_device(): lax.all_to_all(merged, 'ap', split_axis=0, concat_axis=0, tiled=True)  15.9 us
    all_to_all x1, starting transfers between devices, per_device(): lax.all_to_all(merged, 'ap', split_axis=0, concat_axis=0, tiled=True)  10.4 us
    all_to_all x1, starting transfers between devices, per_device(): lax.all_to_all(outgoing, ('ap', 'rg'), split_axis=0, concat_axis=0, tiled...  4.92 us
    ppermute x1, starting transfers between devices, per_device(): from_left = lax.ppermute(to_right, 'rg', [(i, i + 1) for i in range(ends)])  4.5 us
    pallas_call x1, Pallas kernels, per_device(): pl.pallas_call(functools.partial(inner_merges_kernel, inner_levels), out_...  3.93 us
    pallas_call x1, Pallas kernels, per_device(): pl.pallas_call(last_sums_kernel, out_shape=pltpu.HBM((devices, 2 * tile_r...  1.97 us
    pallas_call x1, Pallas kernels, per_device(): pl.pallas_call(functools.partial(place_kernel, steps), out_shape=shape((2...  1.92 us
  transfers between devices with their start and end apart: 4, of which 3 were waited for; matrix products, arithmetic and copies ran while one was open for 2% of the time, Pallas kernels for 6%

profile of v4, /device:TPU:1, one launch (start us, length us, event | category | flops | bytes accessed | tf_op | source)
XLA Modules:
  0.0 69.1 jit_solution(11318477250973825006)
XLA Ops:
  0.0 1.1 %shard_map.55 = (bf16[576,128]{1,0:T(8,128)(2,1)S(1)}, bf16[576,128]{1,0:T(8,128)(2,1)S(1)}, f32[2,128]{1,0:T(2,128)S(1)}, s32[8,2,1024]{2,1,0:T(2,128)S(1)}, f32[8,2,1024]{2,1,0:T(2,128)S(1)}) custom-call(bf16[2,256,1024]{2,1,0:T(8,128)(2,1)} %far_raw.1, f32[2,128]{1,0:T(2,128)} %chirp_ref.1, s32[8,2,1024]{2,1,0:T(2,128)} %offset_ref.1, f32[8,2,1024]{2,1,0:T(2,128)} %phase_ref.1), custom_call_target="tpu_custom_call" | custom-call | tf_op jit(solution)/shard_map/pallas_call | solution.py:539
  1.1 4.5 %collective-permute-start = (bf16[576,128]{1,0:T(8,128)(2,1)S(1)}, bf16[576,128]{1,0:T(8,128)(2,1)S(1)}, u32[]{:S(2)}, u32[]{:S(2)}) collective-permute-start(bf16[576,128]{1,0:T(8,128)(2,1)S(1)} %get-tuple-element.22), channel_id=1, source_target_pairs={{0,1},{1,2},{2,3},{4,5},{5,6},{6,7},{8,9},{9,10},{10,11},{12,13},{... | collective-permute-start | bytes 442376 | tf_op jit(solution)/shard_map/ppermute | solution.py:553
  5.6 1.9 %collective-permute-start.1 = (bf16[576,128]{1,0:T(8,128)(2,1)S(1)}, bf16[576,128]{1,0:T(8,128)(2,1)S(1)}, u32[]{:S(2)}, u32[]{:S(2)}) collective-permute-start(bf16[576,128]{1,0:T(8,128)(2,1)S(1)} %get-tuple-element.23), channel_id=1, source_target_pairs={{1,0},{2,1},{3,2},{5,4},{6,5},{7,6},{9,8},{10,9},{11,10},{13,12},{... | collective-permute-start | bytes 442376 | tf_op jit(solution)/shard_map/ppermute | solution.py:554
  7.5 3.9 %shard_map.56 = (bf16[32,16,1024]{2,1,0:T(8,128)(2,1)}, f32[2,256,256]{2,1,0:T(8,128)S(1)}, f32[3,16,1024]{2,1,0:T(8,128)S(1)}, bf16[2,256,256]{2,1,0:T(8,128)(2,1)S(1)}, bf16[2,256,1024]{2,1,0:T(8,128)(2,1)S(1)}) custom-call(bf16[2,256,1024]{2,1,0:T(8,128)(2,1)} %far_raw.1, f32[2,128]{1,0:T(2,128)S(1)} %get-tuple-element.15.chirp_ref, ...), custom_call_target="tpu_custom_call" | custom-call | tf_op jit(solution)/shard_map/pallas_call | solution.py:567
  11.4 0.0 collective-permute-done.left_ref
  11.5 0.6 collective-permute-done.1.right_ref
  12.0 1.8 %shard_map.57 = bf16[32,16,1024]{2,1,0:T(8,128)(2,1)} custom-call(bf16[32,16,1024]{2,1,0:T(8,128)(2,1)} %get-tuple-element.18.partial_ref, f32[2,256,256]{2,1,0:T(8,128)S(1)} %get-tuple-element.19.ends_ref, f32[3,16,1024]{2,1,0:T(8,128)S(1)} %get-tuple-element.20.steering_ref, ...), custom_call_target="tpu_custom_call", output_to_operand_aliasing={{}: (0, {})} | custom-call | tf_op jit(solution)/shard_map/pallas_call | solution.py:586
  13.8 0.0 copy-start
  13.8 10.4 %all-to-all-start = ((bf16[32,16,1024]{2,1,0:T(8,128)(2,1)}), bf16[32,16,1024]{2,1,0:T(8,128)(2,1)S(1)}, u32[]{:S(2)}, u32[]{:S(2)}) async-start(bf16[32,16,1024]{2,1,0:T(8,128)(2,1)} %shard_map.57), calls=%async_computation | async-start | bytes 2097152 | tf_op jit(solution)/shard_map/all_to_all | solution.py:602
  24.2 0.0 copy-done
  24.2 0.2 fusion.1
  24.4 0.1 reshape.10
  24.5 0.1 constant_dynamic-slice_fusion
  24.6 0.3 copy.13
  24.9 0.1 reshape.12.target_ref
  25.0 15.9 %all-to-all-done.moved_ref = bf16[32,16,1024]{2,1,0:T(8,128)(2,1)S(1)} async-done(((bf16[32,16,1024]{2,1,0:T(8,128)(2,1)}), bf16[32,16,1024]{2,1,0:T(8,128)(2,1)S(1)}, u32[]{:S(2)}, u32[]{:S(2)}) %all-to-all-start) | async-done | bytes 1048608 | tf_op jit(solution)/shard_map/all_to_all | solution.py:602
  40.9 2.0 %shard_map.58 = bf16[128,16,256]{2,1,0:T(8,128)(2,1)} custom-call(s32[128]{0:T(128)S(1)} %reshape.12.target_ref, bf16[32,16,1024]{2,1,0:T(8,128)(2,1)S(1)} %all-to-all-done.moved_ref), custom_call_target="tpu_custom_call" | custom-call | tf_op jit(solution)/shard_map/pallas_call | solution.py:621
  42.9 4.9 %all-to-all-start.1 = ((bf16[128,16,256]{2,1,0:T(8,128)(2,1)}), bf16[128,16,256]{2,1,0:T(8,128)(2,1)S(1)}, u32[]{:S(2)}, u32[]{:S(2)}) async-start(bf16[128,16,256]{2,1,0:T(8,128)(2,1)} %shard_map.58), calls=%async_computation.1 | async-start | bytes 2097152 | tf_op jit(solution)/shard_map/all_to_all | solution.py:636
  47.8 0.1 reshape.11
  47.9 0.1 select_reduce_fusion
  48.0 0.1 copy.11
  48.1 0.1 eq.27
  48.2 0.1 select_reduce_fusion.1.source_ref
  48.3 18.9 %all-to-all-done.1.incoming_ref = bf16[128,16,256]{2,1,0:T(8,128)(2,1)S(1)} async-done(((bf16[128,16,256]{2,1,0:T(8,128)(2,1)}), bf16[128,16,256]{2,1,0:T(8,128)(2,1)S(1)}, u32[]{:S(2)}, u32[]{:S(2)}) %all-to-all-start.1) | async-done | bytes 1048608 | tf_op jit(solution)/shard_map/all_to_all | solution.py:636
  67.1 1.9 %shard_map.59 = f32[2,256,1024]{2,1,0:T(8,128)} custom-call(s32[128]{0:T(128)S(1)} %select_reduce_fusion.1.source_ref, bf16[128,16,256]{2,1,0:T(8,128)(2,1)S(1)} %all-to-all-done.1.incoming_ref), custom_call_target="tpu_custom_call" | custom-call | tf_op jit(solution)/shard_map/pallas_call | solution.py:638
Async XLA Ops:
  1.1 10.4 %collective-permute-start = (bf16[576,128]{1,0:T(8,128)(2,1)S(1)}, bf16[576,128]{1,0:T(8,128)(2,1)S(1)}, u32[]{:S(2)}, u32[]{:S(2)}) collective-permute-start(bf16[576,128]{1,0:T(8,128)(2,1)S(1)} %get-tuple-element.22), channel_id=1, source_target_pairs={{0,1},{1,2},{2,3},{4,5},{5,6},{6,7},{8,9},{9,10},{10,11},{12,13},{... | collective-permute-start | bytes 442376 | tf_op jit(solution)/shard_map/ppermute | solution.py:553
  5.6 6.5 %collective-permute-start.1 = (bf16[576,128]{1,0:T(8,128)(2,1)S(1)}, bf16[576,128]{1,0:T(8,128)(2,1)S(1)}, u32[]{:S(2)}, u32[]{:S(2)}) collective-permute-start(bf16[576,128]{1,0:T(8,128)(2,1)S(1)} %get-tuple-element.23), channel_id=1, source_target_pairs={{1,0},{2,1},{3,2},{5,4},{6,5},{7,6},{9,8},{10,9},{11,10},{13,12},{... | collective-permute-start | bytes 442376 | tf_op jit(solution)/shard_map/ppermute | solution.py:554
  13.8 10.4 %copy-start = (s32[1024,16]{0,1:T(8,128)S(1)}, s32[1024,16]{0,1:T(8,128)}, u32[]{:S(2)}) copy-start(s32[1024,16]{0,1:T(8,128)} %param.9) | copy-start | bytes 196612
  13.8 27.0 %all-to-all-start = ((bf16[32,16,1024]{2,1,0:T(8,128)(2,1)}), bf16[32,16,1024]{2,1,0:T(8,128)(2,1)S(1)}, u32[]{:S(2)}, u32[]{:S(2)}) async-start(bf16[32,16,1024]{2,1,0:T(8,128)(2,1)} %shard_map.57), calls=%async_computation | async-start | bytes 2097152 | tf_op jit(solution)/shard_map/all_to_all | solution.py:602
  42.9 24.3 %all-to-all-start.1 = ((bf16[128,16,256]{2,1,0:T(8,128)(2,1)}), bf16[128,16,256]{2,1,0:T(8,128)(2,1)S(1)}, u32[]{:S(2)}, u32[]{:S(2)}) async-start(bf16[128,16,256]{2,1,0:T(8,128)(2,1)} %shard_map.58), calls=%async_computation.1 | async-start | bytes 2097152 | tf_op jit(solution)/shard_map/all_to_all | solution.py:636

commit v5 on v4

--- a/solution.py
+++ b/solution.py
@@ -50,24 +50,28 @@
     chirp_ref,
     offset_ref,
     phase_ref,
-    left_ref,
-    right_ref,
+    paired_ref,
+    crossed_ref,
     near_chirp,
     near_offset,
     near_phase,
     semaphore,
 ):
     _, pulses, width = raw_ref.shape
+    far_end = width - LANES
+    odd = lax.rem(lax.axis_index("rg"), 2)
+    paired_at = pl.multiple_of((1 - odd) * far_end, LANES)
+    crossed_at = pl.multiple_of(odd * far_end, LANES)
     levels = offset_ref.shape[0]
     rows = 2 * levels
     copies = []
     for source, target in (
         (offset_ref, near_offset),
         (phase_ref, near_phase),
-        (raw_ref.at[0, :, pl.ds(0, LANES)], left_ref.at[:pulses]),
-        (raw_ref.at[1, :, pl.ds(0, LANES)], left_ref.at[pulses : 2 * pulses]),
-        (raw_ref.at[0, :, pl.ds(width - LANES, LANES)], right_ref.at[:pulses]),
-        (raw_ref.at[1, :, pl.ds(width - LANES, LANES)], right_ref.at[pulses : 2 * pulses]),
+        (raw_ref.at[0, :, pl.ds(paired_at, LANES)], paired_ref.at[:pulses]),
+        (raw_ref.at[1, :, pl.ds(paired_at, LANES)], paired_ref.at[pulses : 2 * pulses]),
+        (raw_ref.at[0, :, pl.ds(crossed_at, LANES)], crossed_ref.at[:pulses]),
+        (raw_ref.at[1, :, pl.ds(crossed_at, LANES)], crossed_ref.at[pulses : 2 * pulses]),
         (chirp_ref, near_chirp),
     ):
         copy = pltpu.make_async_copy(source, target, semaphore.at[len(copies)])
@@ -75,8 +79,8 @@
         copies.append(copy)
     for copy in copies[:2]:
         copy.wait()
-    for start, out_ref in ((0, left_ref), (width - LANES, right_ref)):
-        cut = slice(start, start + LANES)
+    for start, out_ref in ((paired_at, paired_ref), (crossed_at, crossed_ref)):
+        cut = pl.ds(start, LANES)
         at = 2 * pulses
         offsets = jnp.concatenate([near_offset[l, :, cut] for l in range(levels)], axis=0)
         angles = jnp.concatenate([near_phase[l, :, cut] for l in range(levels)], axis=0)
@@ -179,34 +183,34 @@
             for part in range(3)
         )
 
-    def chain(outer_of, inner):
+    sublane = lax.broadcasted_iota(jnp.int32, (8, LANES), 0)
+
+    def operator(level):
+        if level >= inner_levels:
+            return {block: row(inner_levels + level, block) for block in blocks}
+        upper = ((sublane >> level) & 1) == 1
         return {
-            block: compose(outer_of(block), inner[block], inner[min(block + 1, last)], lane)
+            block: tuple(
+                jnp.where(upper, b, a)
+                for a, b in zip(row(2 * level, block), row(2 * level + 1, block))
+            )
             for block in blocks
         }
 
-    own = {block: row(2 * inner_levels, block) for block in blocks}
-    for level in range(inner_levels + 1, levels):
-        own = chain(lambda block: row(inner_levels + level, block), own)
-
-    sublane = lax.broadcasted_iota(jnp.int32, (8, LANES), 0)
-    inner = {}
-    for block in blocks:
-        low, high = row(0, block), row(1, block)
-        inner[block] = tuple(
-            jnp.where(sublane % 2 == 0, a, b) for a, b in zip(low, high)
-        )
-    for level in range(1, inner_levels):
-        bit = (sublane >> level) & 1
-
-        def outer_of(block):
-            low, high = row(2 * level, block), row(2 * level + 1, block)
-            return tuple(jnp.where(bit == 0, a, b) for a, b in zip(low, high))
-
-        inner = chain(outer_of, inner)
+    operators = [operator(level) for level in range(levels)]
+    while len(operators) > 1:
+        kept = blocks[:-1] if len(operators) == 2 else blocks
+        joined = [
+            {
+                block: compose(outer[block], inner[block], inner[min(block + 1, last)], lane)
+                for block in kept
+            }
+            for inner, outer in zip(operators[0::2], operators[1::2])
+        ]
+        operators = joined + operators[len(operators) // 2 * 2 :]
 
     for block in blocks[:-1]:
-        moved, cosine, sine = compose(own[block], inner[block], inner[block + 1], lane)
+        moved, cosine, sine = operators[0][block]
         reach = lane + moved.astype(jnp.int32)
         lanes = slice(block * LANES, (block + 1) * LANES)
         index_ref[0, :, lanes] = reach & (LANES - 1)
@@ -377,8 +381,8 @@
     ends_ref,
     steering_ref,
     raw_ref,
-    left_ref,
-    right_ref,
+    paired_ref,
+    crossed_ref,
     table_ref,
     out_ref,
     semaphore,
@@ -395,16 +399,23 @@
     levels = rim_rows // 2
     start = lax.axis_index("rg") * width - LEAD
     own_sources = sources(levels, inner_levels)
+    odd = lax.rem(lax.axis_index("rg"), 2) == 1
+
+    def left_rim(rows):
+        return jnp.where(odd, paired_ref[rows, :], crossed_ref[rows, :])
+
+    def right_rim(rows):
+        return jnp.where(odd, crossed_ref[rows, :], paired_ref[rows, :])
 
     def held(position):
         return slice(position * LANES, (position + 1) * LANES)
 
-    for rim_ref, at, near_lanes, blocks in (
-        (left_ref, -LANES, slice(0, 2 * LANES), (0, 1)),
-        (right_ref, width, slice(width - 2 * LANES, width), (tiles - 1, tiles)),
+    for rim_of, at, near_lanes, blocks in (
+        (left_rim, -LANES, slice(0, 2 * LANES), (0, 1)),
+        (right_rim, width, slice(width - 2 * LANES, width), (tiles - 1, tiles)),
     ):
         offsets, high, middle, low = (
-            rim_ref[2 * pulses + k * rim_rows : 2 * pulses + (k + 1) * rim_rows, :].astype(F32)
+            rim_of(slice(2 * pulses + k * rim_rows, 2 * pulses + (k + 1) * rim_rows)).astype(F32)
             for k in range(4)
         )
         cosine, sine = scaled_trig(high + middle + low)
@@ -429,9 +440,9 @@
         for part in range(2):
             rows = slice(part * pulses, (part + 1) * pulses)
             if block == 0:
-                pair.append([left_ref[rows, :], raw_ref[part, :, :LANES]])
+                pair.append([left_rim(rows), raw_ref[part, :, :LANES]])
             else:
-                pair.append([raw_ref[part, :, width - LANES :], right_ref[rows, :]])
+                pair.append([raw_ref[part, :, width - LANES :], right_rim(rows)])
         both = filter_block(pair, table_ref)
         bins = start + block * LANES + (lax.broadcasted_iota(jnp.int32, both.shape, 1) % LANES)
         both = jnp.where((bins >= 0) & (bins < total), both, 0.0)
@@ -536,7 +547,7 @@
 
     anywhere = pl.BlockSpec(memory_space=pl.ANY)
     distant = pl.BlockSpec(memory_space=pltpu.HBM)
-    to_left, to_right, near_chirp, near_offsets, near_phases = pl.pallas_call(
+    to_paired, to_crossed, near_chirp, near_offsets, near_phases = pl.pallas_call(
         rim_kernel,
         out_shape=[VMEM((rim_rows, LANES), BF16)] * 2
         + [
@@ -549,9 +560,11 @@
         out_specs=whole(5),
         scratch_shapes=[pltpu.SemaphoreType.DMA((7,))],
     )(*map(far, (raw_echoes, chirp, range_offsets, phases)))
-    ends = rg_count - 1
-    from_left = lax.ppermute(to_right, "rg", [(i, i + 1) for i in range(ends)])
-    from_right = lax.ppermute(to_left, "rg", [(i + 1, i) for i in range(ends)])
+    from_paired = lax.ppermute(to_paired, "rg", [(i, i ^ 1) for i in range(rg_count)])
+    crossed_pairs = [(i, i + 1) for i in range(1, rg_count - 1, 2)]
+    from_crossed = lax.ppermute(
+        to_crossed, "rg", crossed_pairs + [(j, i) for i, j in crossed_pairs]
+    )
     inner = 1 << inner_levels
     merged_shape = pltpu.HBM((ap_count, 2 * tile_rows, width), BF16)
 
@@ -597,7 +610,7 @@
         + first_scratch(4 * LANES),
     )(
         far(partial),
-        *map(near, (field_ends, steering, near_raw, from_left, from_right, table)),
+        *map(near, (field_ends, steering, near_raw, from_paired, from_crossed, table)),
     )
     moved = lax.all_to_all(merged, "ap", split_axis=0, concat_axis=0, tiled=True)
 
@@ -634,7 +647,7 @@
         ),
     )(send_to, near(moved))
     incoming = lax.all_to_all(outgoing, ("ap", "rg"), split_axis=0, concat_axis=0, tiled=True)
-    steps = 4
+    steps = 8
     return pl.pallas_call(
         functools.partial(place_kernel, steps),
         out_shape=shape((2, pulses, width), F32),

time: 69.5 us -> 66.7 us (0.960)
  starting transfers between devices: 21.7 us -> 19.2 us
    ppermute x2, starting transfers between devices: 6.42 us -> 4.59 us  [the longest x1 3.13 us: per_device(): lax.ppermute(to_crossed, 'rg', crossed_pairs + [(j, i) for i, j in crosse...]
  transfers between devices with their start and end apart: 4 -> 4, of which waited for: 3 -> 2; matrix products, arithmetic and copies ran while one was open for 2% -> 2% of each run, Pallas kernels for 6% -> 6%
where the time goes in v5:
time: 66.7 us; the launch traced here: 66.3 us
  waiting for transfers between devices  34.8 us (52%)
  starting transfers between devices  19.2 us (29%)
  Pallas kernels  10.8 us (16%)
  local copies, waits for them, and re-layouts  0.92 us (1%)
    all_to_all x1, waiting for transfers between devices, per_device(): lax.all_to_all(outgoing, ('ap', 'rg'), split_axis=0, concat_axis=0, tiled...  18.9 us
    all_to_all x1, waiting for transfers between devices, per_device(): lax.all_to_all(merged, 'ap', split_axis=0, concat_axis=0, tiled=True)  16 us
    all_to_all x1, starting transfers between devices, per_device(): lax.all_to_all(merged, 'ap', split_axis=0, concat_axis=0, tiled=True)  10.4 us
    all_to_all x1, starting transfers between devices, per_device(): lax.all_to_all(outgoing, ('ap', 'rg'), split_axis=0, concat_axis=0, tiled...  4.26 us
    pallas_call x1, Pallas kernels, per_device(): pl.pallas_call(functools.partial(inner_merges_kernel, inner_levels), out_...  4.22 us
    ppermute x1, starting transfers between devices, per_device(): lax.ppermute(to_crossed, 'rg', crossed_pairs + [(j, i) for i, j in crosse...  3.13 us
    pallas_call x1, Pallas kernels, per_device(): pl.pallas_call(last_sums_kernel, out_shape=pltpu.HBM((devices, 2 * tile_r...  1.97 us
    pallas_call x1, Pallas kernels, per_device(): pl.pallas_call(functools.partial(place_kernel, steps), out_shape=shape((2...  1.93 us
  transfers between devices with their start and end apart: 4, of which 2 were waited for; matrix products, arithmetic and copies ran while one was open for 2% of the time, Pallas kernels for 6%

profile of v5, /device:TPU:1, one launch (start us, length us, event | category | flops | bytes accessed | tf_op | source)
XLA Modules:
  0.0 66.3 jit_solution(6299120091103776440)
XLA Ops:
  0.0 1.1 %shard_map.55 = (bf16[576,128]{1,0:T(8,128)(2,1)S(1)}, bf16[576,128]{1,0:T(8,128)(2,1)S(1)}, f32[2,128]{1,0:T(2,128)S(1)}, s32[8,2,1024]{2,1,0:T(2,128)S(1)}, f32[8,2,1024]{2,1,0:T(2,128)S(1)}) custom-call(bf16[2,256,1024]{2,1,0:T(8,128)(2,1)} %far_raw.1, f32[2,128]{1,0:T(2,128)} %chirp_ref.1, s32[8,2,1024]{2,1,0:T(2,128)} %offset_ref.1, f32[8,2,1024]{2,1,0:T(2,128)} %phase_ref.1), custom_call_target="tpu_custom_call" | custom-call | tf_op jit(solution)/shard_map/pallas_call | solution.py:550
  1.1 1.5 %collective-permute-start = (bf16[576,128]{1,0:T(8,128)(2,1)S(1)}, bf16[576,128]{1,0:T(8,128)(2,1)S(1)}, u32[]{:S(2)}, u32[]{:S(2)}) collective-permute-start(bf16[576,128]{1,0:T(8,128)(2,1)S(1)} %get-tuple-element.22), channel_id=1, source_target_pairs={{0,1},{1,0},{2,3},{3,2},{4,5},{5,4},{6,7},{7,6},{8,9},{9,8},{10,11... | collective-permute-start | bytes 442376 | tf_op jit(solution)/shard_map/ppermute | solution.py:563
  2.5 3.1 %collective-permute-start.1 = (bf16[576,128]{1,0:T(8,128)(2,1)S(1)}, bf16[576,128]{1,0:T(8,128)(2,1)S(1)}, u32[]{:S(2)}, u32[]{:S(2)}) collective-permute-start(bf16[576,128]{1,0:T(8,128)(2,1)S(1)} %get-tuple-element.23), channel_id=1, source_target_pairs={{1,2},{2,1},{5,6},{6,5},{9,10},{10,9},{13,14},{14,13},{17,18},{18,... | collective-permute-start | bytes 442376 | tf_op jit(solution)/shard_map/ppermute | solution.py:565
  5.7 4.2 %shard_map.56 = (bf16[32,16,1024]{2,1,0:T(8,128)(2,1)}, f32[2,256,256]{2,1,0:T(8,128)S(1)}, f32[3,16,1024]{2,1,0:T(8,128)S(1)}, bf16[2,256,256]{2,1,0:T(8,128)(2,1)S(1)}, bf16[2,256,1024]{2,1,0:T(8,128)(2,1)S(1)}) custom-call(bf16[2,256,1024]{2,1,0:T(8,128)(2,1)} %far_raw.1, f32[2,128]{1,0:T(2,128)S(1)} %get-tuple-element.15.chirp_ref, ...), custom_call_target="tpu_custom_call" | custom-call | tf_op jit(solution)/shard_map/pallas_call | solution.py:580
  9.9 0.0 collective-permute-done.paired_ref
  9.9 0.0 collective-permute-done.1.crossed_ref
  9.9 1.6 %shard_map.57 = bf16[32,16,1024]{2,1,0:T(8,128)(2,1)} custom-call(bf16[32,16,1024]{2,1,0:T(8,128)(2,1)} %get-tuple-element.18.partial_ref, f32[2,256,256]{2,1,0:T(8,128)S(1)} %get-tuple-element.19.ends_ref, f32[3,16,1024]{2,1,0:T(8,128)S(1)} %get-tuple-element.20.steering_ref, ...), custom_call_target="tpu_custom_call", output_to_operand_aliasing={{}: (0, {})} | custom-call | tf_op jit(solution)/shard_map/pallas_call | solution.py:599
  11.5 0.0 copy-start
  11.6 10.4 %all-to-all-start = ((bf16[32,16,1024]{2,1,0:T(8,128)(2,1)}), bf16[32,16,1024]{2,1,0:T(8,128)(2,1)S(1)}, u32[]{:S(2)}, u32[]{:S(2)}) async-start(bf16[32,16,1024]{2,1,0:T(8,128)(2,1)} %shard_map.57), calls=%async_computation | async-start | bytes 2097152 | tf_op jit(solution)/shard_map/all_to_all | solution.py:615
  21.9 0.0 copy-done
  21.9 0.2 fusion.1
  22.1 0.1 reshape.10
  22.2 0.1 constant_dynamic-slice_fusion
  22.3 0.3 copy.13
  22.6 0.1 reshape.12.target_ref
  22.8 16.0 %all-to-all-done.moved_ref = bf16[32,16,1024]{2,1,0:T(8,128)(2,1)S(1)} async-done(((bf16[32,16,1024]{2,1,0:T(8,128)(2,1)}), bf16[32,16,1024]{2,1,0:T(8,128)(2,1)S(1)}, u32[]{:S(2)}, u32[]{:S(2)}) %all-to-all-start) | async-done | bytes 1048608 | tf_op jit(solution)/shard_map/all_to_all | solution.py:615
  38.7 2.0 %shard_map.58 = bf16[128,16,256]{2,1,0:T(8,128)(2,1)} custom-call(s32[128]{0:T(128)S(1)} %reshape.12.target_ref, bf16[32,16,1024]{2,1,0:T(8,128)(2,1)S(1)} %all-to-all-done.moved_ref), custom_call_target="tpu_custom_call" | custom-call | tf_op jit(solution)/shard_map/pallas_call | solution.py:634
  40.7 4.3 %all-to-all-start.1 = ((bf16[128,16,256]{2,1,0:T(8,128)(2,1)}), bf16[128,16,256]{2,1,0:T(8,128)(2,1)S(1)}, u32[]{:S(2)}, u32[]{:S(2)}) async-start(bf16[128,16,256]{2,1,0:T(8,128)(2,1)} %shard_map.58), calls=%async_computation.1 | async-start | bytes 2097152 | tf_op jit(solution)/shard_map/all_to_all | solution.py:649
  45.0 0.1 reshape.11
  45.1 0.1 select_reduce_fusion
  45.2 0.1 copy.11
  45.2 0.1 eq.27
  45.4 0.1 select_reduce_fusion.1.source_ref
  45.5 18.9 %all-to-all-done.1.incoming_ref = bf16[128,16,256]{2,1,0:T(8,128)(2,1)S(1)} async-done(((bf16[128,16,256]{2,1,0:T(8,128)(2,1)}), bf16[128,16,256]{2,1,0:T(8,128)(2,1)S(1)}, u32[]{:S(2)}, u32[]{:S(2)}) %all-to-all-start.1) | async-done | bytes 1048608 | tf_op jit(solution)/shard_map/all_to_all | solution.py:649
  64.3 1.9 %shard_map.59 = f32[2,256,1024]{2,1,0:T(8,128)} custom-call(s32[128]{0:T(128)S(1)} %select_reduce_fusion.1.source_ref, bf16[128,16,256]{2,1,0:T(8,128)(2,1)S(1)} %all-to-all-done.1.incoming_ref), custom_call_target="tpu_custom_call" | custom-call | tf_op jit(solution)/shard_map/pallas_call | solution.py:651
Async XLA Ops:
  1.1 8.8 %collective-permute-start = (bf16[576,128]{1,0:T(8,128)(2,1)S(1)}, bf16[576,128]{1,0:T(8,128)(2,1)S(1)}, u32[]{:S(2)}, u32[]{:S(2)}) collective-permute-start(bf16[576,128]{1,0:T(8,128)(2,1)S(1)} %get-tuple-element.22), channel_id=1, source_target_pairs={{0,1},{1,0},{2,3},{3,2},{4,5},{5,4},{6,7},{7,6},{8,9},{9,8},{10,11... | collective-permute-start | bytes 442376 | tf_op jit(solution)/shard_map/ppermute | solution.py:563
  2.5 7.4 %collective-permute-start.1 = (bf16[576,128]{1,0:T(8,128)(2,1)S(1)}, bf16[576,128]{1,0:T(8,128)(2,1)S(1)}, u32[]{:S(2)}, u32[]{:S(2)}) collective-permute-start(bf16[576,128]{1,0:T(8,128)(2,1)S(1)} %get-tuple-element.23), channel_id=1, source_target_pairs={{1,2},{2,1},{5,6},{6,5},{9,10},{10,9},{13,14},{14,13},{17,18},{18,... | collective-permute-start | bytes 442376 | tf_op jit(solution)/shard_map/ppermute | solution.py:565
  11.5 10.4 %copy-start = (s32[1024,16]{0,1:T(8,128)S(1)}, s32[1024,16]{0,1:T(8,128)}, u32[]{:S(2)}) copy-start(s32[1024,16]{0,1:T(8,128)} %param.9) | copy-start | bytes 196612
  11.6 27.2 %all-to-all-start = ((bf16[32,16,1024]{2,1,0:T(8,128)(2,1)}), bf16[32,16,1024]{2,1,0:T(8,128)(2,1)S(1)}, u32[]{:S(2)}, u32[]{:S(2)}) async-start(bf16[32,16,1024]{2,1,0:T(8,128)(2,1)} %shard_map.57), calls=%async_computation | async-start | bytes 2097152 | tf_op jit(solution)/shard_map/all_to_all | solution.py:615
  40.7 23.6 %all-to-all-start.1 = ((bf16[128,16,256]{2,1,0:T(8,128)(2,1)}), bf16[128,16,256]{2,1,0:T(8,128)(2,1)S(1)}, u32[]{:S(2)}, u32[]{:S(2)}) async-start(bf16[128,16,256]{2,1,0:T(8,128)(2,1)} %shard_map.58), calls=%async_computation.1 | async-start | bytes 2097152 | tf_op jit(solution)/shard_map/all_to_all | solution.py:649

commit v6 on v5

--- a/solution.py
+++ b/solution.py
@@ -55,6 +55,7 @@
     near_chirp,
     near_offset,
     near_phase,
+    near_raw,
     semaphore,
 ):
     _, pulses, width = raw_ref.shape
@@ -73,6 +74,7 @@
         (raw_ref.at[0, :, pl.ds(crossed_at, LANES)], crossed_ref.at[:pulses]),
         (raw_ref.at[1, :, pl.ds(crossed_at, LANES)], crossed_ref.at[pulses : 2 * pulses]),
         (chirp_ref, near_chirp),
+        (raw_ref, near_raw),
     ):
         copy = pltpu.make_async_copy(source, target, semaphore.at[len(copies)])
         copy.start()
@@ -82,8 +84,7 @@
     for start, out_ref in ((paired_at, paired_ref), (crossed_at, crossed_ref)):
         cut = pl.ds(start, LANES)
         at = 2 * pulses
-        offsets = jnp.concatenate([near_offset[l, :, cut] for l in range(levels)], axis=0)
-        angles = jnp.concatenate([near_phase[l, :, cut] for l in range(levels)], axis=0)
+        offsets, angles = by_side(near_offset, cut), by_side(near_phase, cut)
         out_ref[at : at + rows] = offsets.astype(F32).astype(BF16)
         for part in split_three(angles):
             at += rows
@@ -129,32 +130,35 @@
     return jnp.cos(angles) * ROOT_HALF, jnp.sin(angles) * ROOT_HALF
 
 
-def align(values, blocks, sources_of, rows_ref):
-    width = values[0].shape[1]
+def by_side(ref, lanes):
+    levels = ref.shape[0]
+    return jnp.concatenate(
+        [ref[level, side : side + 1, lanes] for side in range(2) for level in reversed(range(levels))],
+        axis=0,
+    )
+
+
+def align(values, inner_levels, blocks, rows_ref):
+    rows, width = values[0].shape
+    levels = rows // 2
     lanes = slice(blocks[0] * LANES, (blocks[-1] + 1) * LANES)
     count = len(blocks) * LANES
-    for level, (slot, side) in enumerate(sources_of):
-        shift = (width - (LANES - LEAD + STEP * (level + 1))) % width
-        group, row = 2 * level // 8 * 8, 2 * level % 8
-        for part in range(3):
-            moved = values[part][group : group + 8]
-            if shift:
-                moved = pltpu.roll(moved, shift, 1)
-            pair = moved[row : row + 2, :count]
-            if side is None:
-                rows_ref[part, slot : slot + 2, lanes] = pair
-            else:
-                rows_ref[part, slot : slot + 1, lanes] = jnp.where(side == 1, pair[1:2], pair[0:1])
-
-
-def sources(levels, inner_levels):
-    here = lax.axis_index("ap")
-    return [
-        (2 * level, None)
-        if level < inner_levels
-        else (inner_levels + level, (here >> (level - inner_levels)) & 1)
-        for level in range(levels)
-    ]
+    level = levels - 1 - lax.broadcasted_iota(jnp.int32, (levels, count), 0)
+    bit = jnp.left_shift(1, jnp.maximum(level - inner_levels, 0))
+    upper = (lax.axis_index("ap") & bit) != 0
+    for part in range(3):
+        sides = [
+            pltpu.roll(
+                values[part][side * levels : (side + 1) * levels],
+                width - (LEAD + STEP * levels),
+                1,
+                stride=STEP,
+                stride_axis=0,
+            )[:, :count]
+            for side in range(2)
+        ]
+        for at, moved in enumerate(sides + [jnp.where(upper, sides[1], sides[0])]):
+            rows_ref[part, at * levels : (at + 1) * levels, lanes] = moved
 
 
 def compose(outer, inner, inner_beyond, lane):
@@ -186,13 +190,14 @@
     sublane = lax.broadcasted_iota(jnp.int32, (8, LANES), 0)
 
     def operator(level):
+        slot = levels - 1 - level
         if level >= inner_levels:
-            return {block: row(inner_levels + level, block) for block in blocks}
+            return {block: row(2 * levels + slot, block) for block in blocks}
         upper = ((sublane >> level) & 1) == 1
         return {
             block: tuple(
                 jnp.where(upper, b, a)
-                for a, b in zip(row(2 * level, block), row(2 * level + 1, block))
+                for a, b in zip(row(slot, block), row(levels + slot, block))
             )
             for block in blocks
         }
@@ -296,7 +301,7 @@
 
 def inner_merges_kernel(
     inner_levels,
-    far_raw,
+    raw_ref,
     chirp_ref,
     offset_ref,
     phase_ref,
@@ -304,8 +309,6 @@
     ends_ref,
     steering_ref,
     table_ref,
-    raw_ref,
-    loaded,
     stored,
     merged_ref,
     field_ref,
@@ -316,23 +319,19 @@
 ):
     tiles = raw_ref.shape[2] // LANES
     levels = offset_ref.shape[0]
-    loading = pltpu.make_async_copy(far_raw, raw_ref, loaded.at[0])
-    loading.start()
-    offsets = jnp.concatenate([offset_ref[l] for l in range(levels)], axis=0)
-    angles = jnp.concatenate([phase_ref[l] for l in range(levels)], axis=0)
+    offsets, angles = (by_side(ref, slice(None)) for ref in (offset_ref, phase_ref))
     values = (offsets.astype(F32) + (STEP - 4.0), *scaled_trig(angles))
     for part in range(3):
         steering_ref[part] = values[part]
     blank = jnp.zeros((2 * levels, LANES), F32)
     align(
         [jnp.concatenate([blank, value, blank], axis=1) for value in values],
+        inner_levels,
         range(tiles + 1),
-        sources(levels, inner_levels),
         rows_ref,
     )
     steer(levels, inner_levels, range(1, tiles), rows_ref, index_ref, trig_ref)
     fill_toeplitz(chirp_ref, table_ref)
-    loading.wait()
     for block in range(1, tiles):
         cut = slice((block - 1) * LANES, (block + 1) * LANES)
         both = filter_block([[raw_ref[part, :, cut]] for part in range(2)], table_ref)
@@ -398,7 +397,6 @@
     rim_rows = steering_ref.shape[1]
     levels = rim_rows // 2
     start = lax.axis_index("rg") * width - LEAD
-    own_sources = sources(levels, inner_levels)
     odd = lax.rem(lax.axis_index("rg"), 2) == 1
 
     def left_rim(rows):
@@ -432,7 +430,7 @@
         joined = [
             jnp.concatenate((a, b) if at < 0 else (b, a), axis=1) for a, b in zip(rim, middle)
         ]
-        align(joined, blocks, own_sources, rows_ref)
+        align(joined, inner_levels, blocks, rows_ref)
         steer(levels, inner_levels, blocks, rows_ref, index_ref, trig_ref)
 
     for position, block in ((0, 0), (3, tiles)):
@@ -547,18 +545,19 @@
 
     anywhere = pl.BlockSpec(memory_space=pl.ANY)
     distant = pl.BlockSpec(memory_space=pltpu.HBM)
-    to_paired, to_crossed, near_chirp, near_offsets, near_phases = pl.pallas_call(
+    to_paired, to_crossed, near_chirp, near_offsets, near_phases, near_raw = pl.pallas_call(
         rim_kernel,
         out_shape=[VMEM((rim_rows, LANES), BF16)] * 2
         + [
             VMEM(chirp.shape, F32),
             VMEM(range_offsets.shape, jnp.int32),
             VMEM(phases.shape, F32),
+            VMEM(raw_echoes.shape, BF16),
         ],
         compiler_params=params(),
         in_specs=[distant] * 4,
-        out_specs=whole(5),
-        scratch_shapes=[pltpu.SemaphoreType.DMA((7,))],
+        out_specs=whole(6),
+        scratch_shapes=[pltpu.SemaphoreType.DMA((8,))],
     )(*map(far, (raw_echoes, chirp, range_offsets, phases)))
     from_paired = lax.ppermute(to_paired, "rg", [(i, i ^ 1) for i in range(rg_count)])
     crossed_pairs = [(i, i + 1) for i in range(1, rg_count - 1, 2)]
@@ -574,28 +573,26 @@
             VMEM((2, 2, inner, pulses // inner, LANES), F32),
             VMEM((2, inner, width), jnp.int32),
             VMEM((2, inner, width), F32),
-            VMEM((3, inner_levels + level_count, width + LANES), F32),
+            VMEM((3, 3 * level_count, width + LANES), F32),
         ]
 
-    partial, field_ends, steering, table, near_raw = pl.pallas_call(
+    partial, field_ends, steering, table = pl.pallas_call(
         functools.partial(inner_merges_kernel, inner_levels),
         out_shape=[
             merged_shape,
             VMEM((2, pulses, 2 * LANES), F32),
             VMEM((3, 2 * level_count, width), F32),
             VMEM((2, 2 * LANES, 2 * LANES), BF16),
-            VMEM(raw_echoes.shape, BF16),
         ],
         compiler_params=params(),
-        in_specs=[distant] + whole(3),
-        out_specs=[distant] + whole(4),
+        in_specs=whole(4),
+        out_specs=[distant] + whole(3),
         scratch_shapes=[
-            pltpu.SemaphoreType.DMA((1,)),
             pltpu.SemaphoreType.DMA((1,)),
             VMEM((ap_count, 2 * tile_rows, width), BF16),
         ]
         + first_scratch(width),
-    )(far(raw_echoes), *map(near, (near_chirp, near_offsets, near_phases)))
+    )(*map(near, (near_raw, near_chirp, near_offsets, near_phases)))
     merged = pl.pallas_call(
         functools.partial(outer_merges_kernel, inner_levels, total),
         out_shape=merged_shape,

time: 66.7 us -> 65.8 us (0.987)
  Pallas kernels: 10.8 us -> 9.97 us
    pallas_call x1, Pallas kernels: 4.22 us -> 3.02 us  [per_device(): pl.pallas_call(functools.partial(inner_merges_kernel, inner_levels), out_...]
    all_to_all x1, waiting for transfers between devices: 16 us -> 15.3 us  [per_device(): lax.all_to_all(merged, 'ap', split_axis=0, concat_axis=0, tiled=True)]
  transfers between devices with their start and end apart: 4 -> 4, of which waited for: 2 -> 3; matrix products, arithmetic and copies ran while one was open for 2% -> 2% of each run, Pallas kernels for 6% -> 5%
where the time goes in v6:
time: 65.8 us; the launch traced here: 65.4 us
  waiting for transfers between devices  34.4 us (52%)
  starting transfers between devices  19.6 us (30%)
  Pallas kernels  9.97 us (15%)
  local copies, waits for them, and re-layouts  0.92 us (1%)
    all_to_all x1, waiting for transfers between devices, per_device(): lax.all_to_all(outgoing, ('ap', 'rg'), split_axis=0, concat_axis=0, tiled...  18.9 us
    all_to_all x1, waiting for transfers between devices, per_device(): lax.all_to_all(merged, 'ap', split_axis=0, concat_axis=0, tiled=True)  15.3 us
    all_to_all x1, starting transfers between devices, per_device(): lax.all_to_all(merged, 'ap', split_axis=0, concat_axis=0, tiled=True)  10.8 us
    all_to_all x1, starting transfers between devices, per_device(): lax.all_to_all(outgoing, ('ap', 'rg'), split_axis=0, concat_axis=0, tiled...  4.26 us
    ppermute x1, starting transfers between devices, per_device(): lax.ppermute(to_crossed, 'rg', crossed_pairs + [(j, i) for i, j in crosse...  3.13 us
    pallas_call x1, Pallas kernels, per_device(): pl.pallas_call(functools.partial(inner_merges_kernel, inner_levels), out_...  3.02 us
    pallas_call x1, Pallas kernels, per_device(): pl.pallas_call(last_sums_kernel, out_shape=pltpu.HBM((devices, 2 * tile_r...  1.97 us
    pallas_call x1, Pallas kernels, per_device(): pl.pallas_call(functools.partial(place_kernel, steps), out_shape=shape((2...  1.93 us
  transfers between devices with their start and end apart: 4, of which 3 were waited for; matrix products, arithmetic and copies ran while one was open for 2% of the time, Pallas kernels for 5%

profile of v6, /device:TPU:1, one launch (start us, length us, event | category | flops | bytes accessed | tf_op | source)
XLA Modules:
  0.0 65.4 jit_solution(8709362356955768162)
XLA Ops:
  0.0 1.5 %shard_map.55 = (bf16[576,128]{1,0:T(8,128)(2,1)S(1)}, bf16[576,128]{1,0:T(8,128)(2,1)S(1)}, f32[2,128]{1,0:T(2,128)S(1)}, s32[8,2,1024]{2,1,0:T(2,128)S(1)}, f3...) custom-call(bf16[2,256,1024]{2,1,0:T(8,128)(2,1)} %raw_ref.1, f32[2,128]{1,0:T(2,128)} %chirp_ref.1, ...), custom_call_target="tpu_custom_call" | custom-call | tf_op jit(solution)/shard_map/pallas_call | solution.py:548
  1.5 1.5 %collective-permute-start = (bf16[576,128]{1,0:T(8,128)(2,1)S(1)}, bf16[576,128]{1,0:T(8,128)(2,1)S(1)}, u32[]{:S(2)}, u32[]{:S(2)}) collective-permute-start(bf16[576,128]{1,0:T(8,128)(2,1)S(1)} %get-tuple-element.22), channel_id=1, source_target_pairs={{0,1},{1,0},{2,3},{3,2},{4,5},{5,4},{6,7},{7,6},{8,9},{9,8},{10,11... | collective-permute-start | bytes 442376 | tf_op jit(solution)/shard_map/ppermute | solution.py:562
  3.0 3.1 %collective-permute-start.1 = (bf16[576,128]{1,0:T(8,128)(2,1)S(1)}, bf16[576,128]{1,0:T(8,128)(2,1)S(1)}, u32[]{:S(2)}, u32[]{:S(2)}) collective-permute-start(bf16[576,128]{1,0:T(8,128)(2,1)S(1)} %get-tuple-element.23), channel_id=1, source_target_pairs={{1,2},{2,1},{5,6},{6,5},{9,10},{10,9},{13,14},{14,13},{17,18},{18,... | collective-permute-start | bytes 442376 | tf_op jit(solution)/shard_map/ppermute | solution.py:564
  6.1 3.0 %shard_map.56 = (bf16[32,16,1024]{2,1,0:T(8,128)(2,1)}, f32[2,256,256]{2,1,0:T(8,128)S(1)}, f32[3,16,1024]{2,1,0:T(8,128)S(1)}, bf16[2,256,256]{2,1,0:T(8,128)(2,1)S(1)}) custom-call(bf16[2,256,1024]{2,1,0:T(8,128)(2,1)S(1)} %get-tuple-element.15.raw_ref, f32[2,128]{1,0:T(2,128)S(1)} %get-tuple-element.16.chirp_ref, ...), custom_call_target="tpu_custom_call" | custom-call | tf_op jit(solution)/shard_map/pallas_call | solution.py:579
  9.2 0.0 collective-permute-done.paired_ref
  9.2 0.3 collective-permute-done.1.crossed_ref
  9.5 1.5 %shard_map.57 = bf16[32,16,1024]{2,1,0:T(8,128)(2,1)} custom-call(bf16[32,16,1024]{2,1,0:T(8,128)(2,1)} %get-tuple-element.19.partial_ref, f32[2,256,256]{2,1,0:T(8,128)S(1)} %get-tuple-element.20.ends_ref, f32[3,16,1024]{2,1,0:T(8,128)S(1)} %get-tuple-element.21.steering_ref, ...), custom_call_target="tpu_custom_call", output_to_operand_aliasing={{}: (0, {})} | custom-call | tf_op jit(solution)/shard_map/pallas_call | solution.py:596
  11.0 0.0 copy-start
  11.0 10.8 %all-to-all-start = ((bf16[32,16,1024]{2,1,0:T(8,128)(2,1)}), bf16[32,16,1024]{2,1,0:T(8,128)(2,1)S(1)}, u32[]{:S(2)}, u32[]{:S(2)}) async-start(bf16[32,16,1024]{2,1,0:T(8,128)(2,1)} %shard_map.57), calls=%async_computation | async-start | bytes 2097152 | tf_op jit(solution)/shard_map/all_to_all | solution.py:612
  21.8 0.0 copy-done
  21.8 0.2 fusion.1
  22.0 0.1 reshape.10
  22.1 0.1 constant_dynamic-slice_fusion
  22.2 0.3 copy.13
  22.5 0.1 reshape.12.target_ref
  22.6 15.3 %all-to-all-done.moved_ref = bf16[32,16,1024]{2,1,0:T(8,128)(2,1)S(1)} async-done(((bf16[32,16,1024]{2,1,0:T(8,128)(2,1)}), bf16[32,16,1024]{2,1,0:T(8,128)(2,1)S(1)}, u32[]{:S(2)}, u32[]{:S(2)}) %all-to-all-start) | async-done | bytes 1048608 | tf_op jit(solution)/shard_map/all_to_all | solution.py:612
  37.9 2.0 %shard_map.58 = bf16[128,16,256]{2,1,0:T(8,128)(2,1)} custom-call(s32[128]{0:T(128)S(1)} %reshape.12.target_ref, bf16[32,16,1024]{2,1,0:T(8,128)(2,1)S(1)} %all-to-all-done.moved_ref), custom_call_target="tpu_custom_call" | custom-call | tf_op jit(solution)/shard_map/pallas_call | solution.py:631
  39.9 4.3 %all-to-all-start.1 = ((bf16[128,16,256]{2,1,0:T(8,128)(2,1)}), bf16[128,16,256]{2,1,0:T(8,128)(2,1)S(1)}, u32[]{:S(2)}, u32[]{:S(2)}) async-start(bf16[128,16,256]{2,1,0:T(8,128)(2,1)} %shard_map.58), calls=%async_computation.1 | async-start | bytes 2097152 | tf_op jit(solution)/shard_map/all_to_all | solution.py:646
  44.1 0.1 reshape.11
  44.3 0.1 select_reduce_fusion
  44.3 0.1 copy.11
  44.4 0.1 eq.27
  44.5 0.1 select_reduce_fusion.1.source_ref
  44.6 18.9 %all-to-all-done.1.incoming_ref = bf16[128,16,256]{2,1,0:T(8,128)(2,1)S(1)} async-done(((bf16[128,16,256]{2,1,0:T(8,128)(2,1)}), bf16[128,16,256]{2,1,0:T(8,128)(2,1)S(1)}, u32[]{:S(2)}, u32[]{:S(2)}) %all-to-all-start.1) | async-done | bytes 1048608 | tf_op jit(solution)/shard_map/all_to_all | solution.py:646
  63.5 1.9 %shard_map.59 = f32[2,256,1024]{2,1,0:T(8,128)} custom-call(s32[128]{0:T(128)S(1)} %select_reduce_fusion.1.source_ref, bf16[128,16,256]{2,1,0:T(8,128)(2,1)S(1)} %all-to-all-done.1.incoming_ref), custom_call_target="tpu_custom_call" | custom-call | tf_op jit(solution)/shard_map/pallas_call | solution.py:648
Async XLA Ops:
  1.5 7.6 %collective-permute-start = (bf16[576,128]{1,0:T(8,128)(2,1)S(1)}, bf16[576,128]{1,0:T(8,128)(2,1)S(1)}, u32[]{:S(2)}, u32[]{:S(2)}) collective-permute-start(bf16[576,128]{1,0:T(8,128)(2,1)S(1)} %get-tuple-element.22), channel_id=1, source_target_pairs={{0,1},{1,0},{2,3},{3,2},{4,5},{5,4},{6,7},{7,6},{8,9},{9,8},{10,11... | collective-permute-start | bytes 442376 | tf_op jit(solution)/shard_map/ppermute | solution.py:562
  3.0 6.5 %collective-permute-start.1 = (bf16[576,128]{1,0:T(8,128)(2,1)S(1)}, bf16[576,128]{1,0:T(8,128)(2,1)S(1)}, u32[]{:S(2)}, u32[]{:S(2)}) collective-permute-start(bf16[576,128]{1,0:T(8,128)(2,1)S(1)} %get-tuple-element.23), channel_id=1, source_target_pairs={{1,2},{2,1},{5,6},{6,5},{9,10},{10,9},{13,14},{14,13},{17,18},{18,... | collective-permute-start | bytes 442376 | tf_op jit(solution)/shard_map/ppermute | solution.py:564
  11.0 10.8 %copy-start = (s32[1024,16]{0,1:T(8,128)S(1)}, s32[1024,16]{0,1:T(8,128)}, u32[]{:S(2)}) copy-start(s32[1024,16]{0,1:T(8,128)} %param.9) | copy-start | bytes 196612
  11.0 26.9 %all-to-all-start = ((bf16[32,16,1024]{2,1,0:T(8,128)(2,1)}), bf16[32,16,1024]{2,1,0:T(8,128)(2,1)S(1)}, u32[]{:S(2)}, u32[]{:S(2)}) async-start(bf16[32,16,1024]{2,1,0:T(8,128)(2,1)} %shard_map.57), calls=%async_computation | async-start | bytes 2097152 | tf_op jit(solution)/shard_map/all_to_all | solution.py:612
  39.9 23.6 %all-to-all-start.1 = ((bf16[128,16,256]{2,1,0:T(8,128)(2,1)}), bf16[128,16,256]{2,1,0:T(8,128)(2,1)S(1)}, u32[]{:S(2)}, u32[]{:S(2)}) async-start(bf16[128,16,256]{2,1,0:T(8,128)(2,1)} %shard_map.58), calls=%async_computation.1 | async-start | bytes 2097152 | tf_op jit(solution)/shard_map/all_to_all | solution.py:646

commit v7 on v6

--- a/solution.py
+++ b/solution.py
@@ -473,37 +473,28 @@
         copy.wait()
 
 
-def last_sums_kernel(target_ref, moved_ref, out_ref, tile_ref, term_ref, semaphore):
+def last_sums_kernel(target_ref, moved_ref, out_ref, term_ref):
     holders, rows, columns = moved_ref.shape
     per_tile = out_ref.shape[2] // LANES
     tiles_across = columns // out_ref.shape[2]
     near_group = min(8, holders)
     for column in range(tiles_across):
         for part in range(per_tile):
-            block = column * per_tile + part
-            lanes = slice(block * LANES, (block + 1) * LANES)
+            start = (column * per_tile + part) * LANES
+            lanes = slice(start, start + LANES)
             inner = slice(part * LANES, (part + 1) * LANES)
-            slot = block % 2
             for first in range(0, holders, near_group):
                 sums = sums_and_differences(
                     [moved_ref[first + at, :, lanes].astype(F32) for at in range(near_group)]
                 )
                 for at in range(near_group):
-                    term_ref[slot, first + at] = sums[at]
+                    term_ref[part, first + at] = sums[at]
             for first in range(near_group):
                 members = range(first, holders, near_group)
-                sums = sums_and_differences([term_ref[slot, at] for at in members])
+                sums = sums_and_differences([term_ref[part, at] for at in members])
                 for at, value in zip(members, sums):
-                    tile_ref[column, at, :, inner] = value.astype(BF16)
-        for at in range(holders):
-            to = target_ref[at * tiles_across + column]
-            pltpu.make_async_copy(
-                tile_ref.at[column, at], out_ref.at[to], semaphore.at[column]
-            ).start()
-    for column in range(tiles_across):
-        pltpu.make_async_copy(
-            tile_ref.at[column], out_ref.at[pl.ds(0, holders)], semaphore.at[column]
-        ).wait()
+                    to = target_ref[at * tiles_across + column]
+                    out_ref[to, :, inner] = value.astype(BF16)
 
 
 def place_kernel(steps, source_ref, incoming_ref, out_ref, image_ref, semaphore):
@@ -628,19 +619,16 @@
         target, (0, ap_here, rg_here, 0), (ap_count, 1, 1, rg_count)
     ).reshape(devices)
 
+    moved, source = lax.optimization_barrier((moved, source))
     outgoing = pl.pallas_call(
         last_sums_kernel,
-        out_shape=pltpu.HBM((devices, 2 * tile_rows, tile_bins), BF16),
+        out_shape=VMEM((devices, 2 * tile_rows, tile_bins), BF16),
         compiler_params=params(),
         grid_spec=pltpu.PrefetchScalarGridSpec(
             num_scalar_prefetch=1,
             in_specs=whole(1),
-            out_specs=distant,
-            scratch_shapes=[
-                VMEM((rg_count, ap_count, 2 * tile_rows, tile_bins), BF16),
-                VMEM((2, ap_count, 2 * tile_rows, LANES), F32),
-                pltpu.SemaphoreType.DMA((rg_count,)),
-            ],
+            out_specs=whole(1)[0],
+            scratch_shapes=[VMEM((tile_bins // LANES, ap_count, 2 * tile_rows, LANES), F32)],
         ),
     )(send_to, near(moved))
     incoming = lax.all_to_all(outgoing, ("ap", "rg"), split_axis=0, concat_axis=0, tiled=True)

time: 65.8 us -> 64.6 us (0.982)
  blocking collectives: 0 us -> 23.4 us
  waiting for transfers between devices: 34.4 us -> 15.1 us
  starting transfers between devices: 19.6 us -> 15.4 us
  Pallas kernels: 9.97 us -> 9.03 us
    all_to_all x0 -> x1, blocking collectives: none -> 23.4 us  [per_device(): lax.all_to_all(outgoing, ('ap', 'rg'), split_axis=0, concat_axis=0, tiled...]
    all_to_all x1 -> x0, waiting for transfers between devices: 18.9 us -> none  [per_device(): lax.all_to_all(outgoing, ('ap', 'rg'), split_axis=0, concat_axis=0, tiled...]
    all_to_all x1 -> x0, starting transfers between devices: 4.26 us -> none  [per_device(): lax.all_to_all(outgoing, ('ap', 'rg'), split_axis=0, concat_axis=0, tiled...]
    pallas_call x1, Pallas kernels: 1.97 us -> 1.03 us  [per_device(): pl.pallas_call(last_sums_kernel, out_shape=VMEM((devices, 2 * tile_rows,...]
  transfers between devices with their start and end apart: 4 -> 3, of which waited for: 3 -> 2; matrix products, arithmetic and copies ran while one was open for 2% -> 2% of each run, Pallas kernels for 5% -> 5%
where the time goes in v7:
time: 64.6 us; the launch traced here: 64.3 us
  blocking collectives  23.4 us (36%)
  starting transfers between devices  15.4 us (24%)
  waiting for transfers between devices  15.1 us (23%)
  Pallas kernels  9.03 us (14%)
  local copies, waits for them, and re-layouts  0.92 us (1%)
    all_to_all x1, blocking collectives, per_device(): lax.all_to_all(outgoing, ('ap', 'rg'), split_axis=0, concat_axis=0, tiled...  23.4 us
    all_to_all x1, waiting for transfers between devices, per_device(): lax.all_to_all(merged, 'ap', split_axis=0, concat_axis=0, tiled=True)  14.8 us
    all_to_all x1, starting transfers between devices, per_device(): lax.all_to_all(merged, 'ap', split_axis=0, concat_axis=0, tiled=True)  10.8 us
    ppermute x1, starting transfers between devices, per_device(): lax.ppermute(to_crossed, 'rg', crossed_pairs + [(j, i) for i, j in crosse...  3.13 us
    pallas_call x1, Pallas kernels, per_device(): pl.pallas_call(functools.partial(inner_merges_kernel, inner_levels), out_...  3.02 us
    pallas_call x1, Pallas kernels, per_device(): pl.pallas_call(functools.partial(place_kernel, steps), out_shape=shape((2...  1.93 us
    pallas_call x1, Pallas kernels, per_device(): pl.pallas_call(rim_kernel, out_shape=[VMEM((rim_rows, LANES), BF16)] * 2...  1.53 us
    pallas_call x1, Pallas kernels, per_device(): pl.pallas_call(functools.partial(outer_merges_kernel, inner_levels, total...  1.52 us
  transfers between devices with their start and end apart: 3, of which 2 were waited for; matrix products, arithmetic and copies ran while one was open for 2% of the time, Pallas kernels for 5%

profile of v7, /device:TPU:1, one launch (start us, length us, event | category | flops | bytes accessed | tf_op | source)
XLA Modules:
  0.0 64.3 jit_solution(9601653620034915540)
XLA Ops:
  0.0 1.5 %shard_map.55 = (bf16[576,128]{1,0:T(8,128)(2,1)S(1)}, bf16[576,128]{1,0:T(8,128)(2,1)S(1)}, f32[2,128]{1,0:T(2,128)S(1)}, s32[8,2,1024]{2,1,0:T(2,128)S(1)}, f3...) custom-call(bf16[2,256,1024]{2,1,0:T(8,128)(2,1)} %raw_ref.1, f32[2,128]{1,0:T(2,128)} %chirp_ref.1, ...), custom_call_target="tpu_custom_call" | custom-call | tf_op jit(solution)/shard_map/pallas_call | solution.py:539
  1.5 1.5 %collective-permute-start = (bf16[576,128]{1,0:T(8,128)(2,1)S(1)}, bf16[576,128]{1,0:T(8,128)(2,1)S(1)}, u32[]{:S(2)}, u32[]{:S(2)}) collective-permute-start(bf16[576,128]{1,0:T(8,128)(2,1)S(1)} %get-tuple-element.24), channel_id=1, source_target_pairs={{0,1},{1,0},{2,3},{3,2},{4,5},{5,4},{6,7},{7,6},{8,9},{9,8},{10,11... | collective-permute-start | bytes 442376 | tf_op jit(solution)/shard_map/ppermute | solution.py:553
  3.0 3.1 %collective-permute-start.1 = (bf16[576,128]{1,0:T(8,128)(2,1)S(1)}, bf16[576,128]{1,0:T(8,128)(2,1)S(1)}, u32[]{:S(2)}, u32[]{:S(2)}) collective-permute-start(bf16[576,128]{1,0:T(8,128)(2,1)S(1)} %get-tuple-element.25), channel_id=1, source_target_pairs={{1,2},{2,1},{5,6},{6,5},{9,10},{10,9},{13,14},{14,13},{17,18},{18,... | collective-permute-start | bytes 442376 | tf_op jit(solution)/shard_map/ppermute | solution.py:555
  6.1 3.0 %shard_map.56 = (bf16[32,16,1024]{2,1,0:T(8,128)(2,1)}, f32[2,256,256]{2,1,0:T(8,128)S(1)}, f32[3,16,1024]{2,1,0:T(8,128)S(1)}, bf16[2,256,256]{2,1,0:T(8,128)(2,1)S(1)}) custom-call(bf16[2,256,1024]{2,1,0:T(8,128)(2,1)S(1)} %get-tuple-element.17.raw_ref, f32[2,128]{1,0:T(2,128)S(1)} %get-tuple-element.18.chirp_ref, ...), custom_call_target="tpu_custom_call" | custom-call | tf_op jit(solution)/shard_map/pallas_call | solution.py:570
  9.2 0.0 collective-permute-done.paired_ref
  9.2 0.3 collective-permute-done.1.crossed_ref
  9.5 1.5 %shard_map.57 = bf16[32,16,1024]{2,1,0:T(8,128)(2,1)} custom-call(bf16[32,16,1024]{2,1,0:T(8,128)(2,1)} %get-tuple-element.21.partial_ref, f32[2,256,256]{2,1,0:T(8,128)S(1)} %get-tuple-element.22.ends_ref, f32[3,16,1024]{2,1,0:T(8,128)S(1)} %get-tuple-element.23.steering_ref, ...), custom_call_target="tpu_custom_call", output_to_operand_aliasing={{}: (0, {})} | custom-call | tf_op jit(solution)/shard_map/pallas_call | solution.py:587
  11.0 0.0 copy-start
  11.0 10.8 %all-to-all-start = ((bf16[32,16,1024]{2,1,0:T(8,128)(2,1)}), bf16[32,16,1024]{2,1,0:T(8,128)(2,1)S(1)}, u32[]{:S(2)}, u32[]{:S(2)}) async-start(bf16[32,16,1024]{2,1,0:T(8,128)(2,1)} %shard_map.57), calls=%async_computation | async-start | bytes 2097152 | tf_op jit(solution)/shard_map/all_to_all | solution.py:603
  21.8 0.0 copy-done
  21.8 0.2 fusion.1
  22.0 0.1 reshape.10
  22.1 0.1 reshape.11
  22.2 0.1 select_reduce_fusion
  22.3 0.1 copy.11
  22.4 0.1 eq.27
  22.5 0.1 constant_dynamic-slice_fusion
  22.6 0.3 copy.13
  22.9 0.1 reshape.12.target_ref
  23.0 0.1 select_reduce_fusion.1.source_ref
  23.1 14.8 %all-to-all-done.moved_ref = bf16[32,16,1024]{2,1,0:T(8,128)(2,1)S(1)} async-done(((bf16[32,16,1024]{2,1,0:T(8,128)(2,1)}), bf16[32,16,1024]{2,1,0:T(8,128)(2,1)S(1)}, u32[]{:S(2)}, u32[]{:S(2)}) %all-to-all-start) | async-done | bytes 1048608 | tf_op jit(solution)/shard_map/all_to_all | solution.py:603
  37.9 1.0 %shard_map.58 = bf16[128,16,256]{2,1,0:T(8,128)(2,1)S(1)} custom-call(s32[128]{0:T(128)S(1)} %reshape.12.target_ref, bf16[32,16,1024]{2,1,0:T(8,128)(2,1)S(1)} %all-to-all-done.moved_ref), custom_call_target="tpu_custom_call" | custom-call | tf_op jit(solution)/shard_map/pallas_call | solution.py:623
  38.9 23.4 %all_to_all.10.incoming_ref = bf16[128,16,256]{2,1,0:T(8,128)(2,1)S(1)} all-to-all(bf16[128,16,256]{2,1,0:T(8,128)(2,1)S(1)} %shard_map.58), channel_id=1, replica_groups=mesh['ap'=32,'rg'=4] {'ap','rg'}, dimensions={0} | all-to-all | bytes 2097152 | tf_op jit(solution)/shard_map/all_to_all | solution.py:634
  62.3 1.9 %shard_map.59 = f32[2,256,1024]{2,1,0:T(8,128)} custom-call(s32[128]{0:T(128)S(1)} %select_reduce_fusion.1.source_ref, bf16[128,16,256]{2,1,0:T(8,128)(2,1)S(1)} %all_to_all.10.incoming_ref), custom_call_target="tpu_custom_call" | custom-call | tf_op jit(solution)/shard_map/pallas_call | solution.py:636
Async XLA Ops:
  1.5 7.6 %collective-permute-start = (bf16[576,128]{1,0:T(8,128)(2,1)S(1)}, bf16[576,128]{1,0:T(8,128)(2,1)S(1)}, u32[]{:S(2)}, u32[]{:S(2)}) collective-permute-start(bf16[576,128]{1,0:T(8,128)(2,1)S(1)} %get-tuple-element.24), channel_id=1, source_target_pairs={{0,1},{1,0},{2,3},{3,2},{4,5},{5,4},{6,7},{7,6},{8,9},{9,8},{10,11... | collective-permute-start | bytes 442376 | tf_op jit(solution)/shard_map/ppermute | solution.py:553
  3.0 6.5 %collective-permute-start.1 = (bf16[576,128]{1,0:T(8,128)(2,1)S(1)}, bf16[576,128]{1,0:T(8,128)(2,1)S(1)}, u32[]{:S(2)}, u32[]{:S(2)}) collective-permute-start(bf16[576,128]{1,0:T(8,128)(2,1)S(1)} %get-tuple-element.25), channel_id=1, source_target_pairs={{1,2},{2,1},{5,6},{6,5},{9,10},{10,9},{13,14},{14,13},{17,18},{18,... | collective-permute-start | bytes 442376 | tf_op jit(solution)/shard_map/ppermute | solution.py:555
  11.0 10.8 %copy-start = (s32[1024,16]{0,1:T(8,128)S(1)}, s32[1024,16]{0,1:T(8,128)}, u32[]{:S(2)}) copy-start(s32[1024,16]{0,1:T(8,128)} %param.9) | copy-start | bytes 196612
  11.0 26.9 %all-to-all-start = ((bf16[32,16,1024]{2,1,0:T(8,128)(2,1)}), bf16[32,16,1024]{2,1,0:T(8,128)(2,1)S(1)}, u32[]{:S(2)}, u32[]{:S(2)}) async-start(bf16[32,16,1024]{2,1,0:T(8,128)(2,1)} %shard_map.57), calls=%async_computation | async-start | bytes 2097152 | tf_op jit(solution)/shard_map/all_to_all | solution.py:603

commit v8 on v7

--- a/solution.py
+++ b/solution.py
@@ -477,7 +477,7 @@
     holders, rows, columns = moved_ref.shape
     per_tile = out_ref.shape[2] // LANES
     tiles_across = columns // out_ref.shape[2]
-    near_group = min(8, holders)
+    near_group = min(4, holders)
     for column in range(tiles_across):
         for part in range(per_tile):
             start = (column * per_tile + part) * LANES
@@ -632,7 +632,7 @@
         ),
     )(send_to, near(moved))
     incoming = lax.all_to_all(outgoing, ("ap", "rg"), split_axis=0, concat_axis=0, tiled=True)
-    steps = 8
+    steps = 16
     return pl.pallas_call(
         functools.partial(place_kernel, steps),
         out_shape=shape((2, pulses, width), F32),

time: 64.6 us -> 64.6 us (level)
  no operation moved by 1% of the time
where the time goes in v8:
time: 64.6 us; the launch traced here: 64.3 us
  blocking collectives  23.4 us (36%)
  starting transfers between devices  15.4 us (24%)
  waiting for transfers between devices  15.1 us (23%)
  Pallas kernels  9.09 us (14%)
  local copies, waits for them, and re-layouts  0.92 us (1%)
    all_to_all x1, blocking collectives, per_device(): lax.all_to_all(outgoing, ('ap', 'rg'), split_axis=0, concat_axis=0, tiled...  23.4 us
    all_to_all x1, waiting for transfers between devices, per_device(): lax.all_to_all(merged, 'ap', split_axis=0, concat_axis=0, tiled=True)  14.8 us
    all_to_all x1, starting transfers between devices, per_device(): lax.all_to_all(merged, 'ap', split_axis=0, concat_axis=0, tiled=True)  10.8 us
    ppermute x1, starting transfers between devices, per_device(): lax.ppermute(to_crossed, 'rg', crossed_pairs + [(j, i) for i, j in crosse...  3.13 us
    pallas_call x1, Pallas kernels, per_device(): pl.pallas_call(functools.partial(inner_merges_kernel, inner_levels), out_...  3.02 us
    pallas_call x1, Pallas kernels, per_device(): pl.pallas_call(functools.partial(place_kernel, steps), out_shape=shape((2...  1.99 us
    pallas_call x1, Pallas kernels, per_device(): pl.pallas_call(rim_kernel, out_shape=[VMEM((rim_rows, LANES), BF16)] * 2...  1.53 us
    pallas_call x1, Pallas kernels, per_device(): pl.pallas_call(functools.partial(outer_merges_kernel, inner_levels, total...  1.52 us
  transfers between devices with their start and end apart: 3, of which 2 were waited for; matrix products, arithmetic and copies ran while one was open for 2% of the time, Pallas kernels for 5%

profile of v8, /device:TPU:1, one launch (start us, length us, event | category | flops | bytes accessed | tf_op | source)
XLA Modules:
  0.0 64.3 jit_solution(6558536657709758512)
XLA Ops:
  0.0 1.5 %shard_map.55 = (bf16[576,128]{1,0:T(8,128)(2,1)S(1)}, bf16[576,128]{1,0:T(8,128)(2,1)S(1)}, f32[2,128]{1,0:T(2,128)S(1)}, s32[8,2,1024]{2,1,0:T(2,128)S(1)}, f3...) custom-call(bf16[2,256,1024]{2,1,0:T(8,128)(2,1)} %raw_ref.1, f32[2,128]{1,0:T(2,128)} %chirp_ref.1, ...), custom_call_target="tpu_custom_call" | custom-call | tf_op jit(solution)/shard_map/pallas_call | solution.py:539
  1.5 1.5 %collective-permute-start = (bf16[576,128]{1,0:T(8,128)(2,1)S(1)}, bf16[576,128]{1,0:T(8,128)(2,1)S(1)}, u32[]{:S(2)}, u32[]{:S(2)}) collective-permute-start(bf16[576,128]{1,0:T(8,128)(2,1)S(1)} %get-tuple-element.24), channel_id=1, source_target_pairs={{0,1},{1,0},{2,3},{3,2},{4,5},{5,4},{6,7},{7,6},{8,9},{9,8},{10,11... | collective-permute-start | bytes 442376 | tf_op jit(solution)/shard_map/ppermute | solution.py:553
  3.0 3.1 %collective-permute-start.1 = (bf16[576,128]{1,0:T(8,128)(2,1)S(1)}, bf16[576,128]{1,0:T(8,128)(2,1)S(1)}, u32[]{:S(2)}, u32[]{:S(2)}) collective-permute-start(bf16[576,128]{1,0:T(8,128)(2,1)S(1)} %get-tuple-element.25), channel_id=1, source_target_pairs={{1,2},{2,1},{5,6},{6,5},{9,10},{10,9},{13,14},{14,13},{17,18},{18,... | collective-permute-start | bytes 442376 | tf_op jit(solution)/shard_map/ppermute | solution.py:555
  6.1 3.0 %shard_map.56 = (bf16[32,16,1024]{2,1,0:T(8,128)(2,1)}, f32[2,256,256]{2,1,0:T(8,128)S(1)}, f32[3,16,1024]{2,1,0:T(8,128)S(1)}, bf16[2,256,256]{2,1,0:T(8,128)(2,1)S(1)}) custom-call(bf16[2,256,1024]{2,1,0:T(8,128)(2,1)S(1)} %get-tuple-element.17.raw_ref, f32[2,128]{1,0:T(2,128)S(1)} %get-tuple-element.18.chirp_ref, ...), custom_call_target="tpu_custom_call" | custom-call | tf_op jit(solution)/shard_map/pallas_call | solution.py:570
  9.2 0.0 collective-permute-done.paired_ref
  9.2 0.3 collective-permute-done.1.crossed_ref
  9.5 1.5 %shard_map.57 = bf16[32,16,1024]{2,1,0:T(8,128)(2,1)} custom-call(bf16[32,16,1024]{2,1,0:T(8,128)(2,1)} %get-tuple-element.21.partial_ref, f32[2,256,256]{2,1,0:T(8,128)S(1)} %get-tuple-element.22.ends_ref, f32[3,16,1024]{2,1,0:T(8,128)S(1)} %get-tuple-element.23.steering_ref, ...), custom_call_target="tpu_custom_call", output_to_operand_aliasing={{}: (0, {})} | custom-call | tf_op jit(solution)/shard_map/pallas_call | solution.py:587
  11.0 0.0 copy-start
  11.0 10.8 %all-to-all-start = ((bf16[32,16,1024]{2,1,0:T(8,128)(2,1)}), bf16[32,16,1024]{2,1,0:T(8,128)(2,1)S(1)}, u32[]{:S(2)}, u32[]{:S(2)}) async-start(bf16[32,16,1024]{2,1,0:T(8,128)(2,1)} %shard_map.57), calls=%async_computation | async-start | bytes 2097152 | tf_op jit(solution)/shard_map/all_to_all | solution.py:603
  21.8 0.0 copy-done
  21.8 0.2 fusion.1
  22.0 0.1 reshape.10
  22.1 0.1 reshape.11
  22.2 0.1 select_reduce_fusion
  22.3 0.1 copy.11
  22.4 0.1 eq.27
  22.5 0.1 constant_dynamic-slice_fusion
  22.6 0.3 copy.13
  22.9 0.1 reshape.12.target_ref
  23.0 0.1 select_reduce_fusion.1.source_ref
  23.1 14.8 %all-to-all-done.moved_ref = bf16[32,16,1024]{2,1,0:T(8,128)(2,1)S(1)} async-done(((bf16[32,16,1024]{2,1,0:T(8,128)(2,1)}), bf16[32,16,1024]{2,1,0:T(8,128)(2,1)S(1)}, u32[]{:S(2)}, u32[]{:S(2)}) %all-to-all-start) | async-done | bytes 1048608 | tf_op jit(solution)/shard_map/all_to_all | solution.py:603
  37.9 1.0 %shard_map.58 = bf16[128,16,256]{2,1,0:T(8,128)(2,1)S(1)} custom-call(s32[128]{0:T(128)S(1)} %reshape.12.target_ref, bf16[32,16,1024]{2,1,0:T(8,128)(2,1)S(1)} %all-to-all-done.moved_ref), custom_call_target="tpu_custom_call" | custom-call | tf_op jit(solution)/shard_map/pallas_call | solution.py:623
  38.9 23.4 %all_to_all.10.incoming_ref = bf16[128,16,256]{2,1,0:T(8,128)(2,1)S(1)} all-to-all(bf16[128,16,256]{2,1,0:T(8,128)(2,1)S(1)} %shard_map.58), channel_id=1, replica_groups=mesh['ap'=32,'rg'=4] {'ap','rg'}, dimensions={0} | all-to-all | bytes 2097152 | tf_op jit(solution)/shard_map/all_to_all | solution.py:634
  62.4 2.0 %shard_map.59 = f32[2,256,1024]{2,1,0:T(8,128)} custom-call(s32[128]{0:T(128)S(1)} %select_reduce_fusion.1.source_ref, bf16[128,16,256]{2,1,0:T(8,128)(2,1)S(1)} %all_to_all.10.incoming_ref), custom_call_target="tpu_custom_call" | custom-call | tf_op jit(solution)/shard_map/pallas_call | solution.py:636
Async XLA Ops:
  1.5 7.6 %collective-permute-start = (bf16[576,128]{1,0:T(8,128)(2,1)S(1)}, bf16[576,128]{1,0:T(8,128)(2,1)S(1)}, u32[]{:S(2)}, u32[]{:S(2)}) collective-permute-start(bf16[576,128]{1,0:T(8,128)(2,1)S(1)} %get-tuple-element.24), channel_id=1, source_target_pairs={{0,1},{1,0},{2,3},{3,2},{4,5},{5,4},{6,7},{7,6},{8,9},{9,8},{10,11... | collective-permute-start | bytes 442376 | tf_op jit(solution)/shard_map/ppermute | solution.py:553
  3.0 6.5 %collective-permute-start.1 = (bf16[576,128]{1,0:T(8,128)(2,1)S(1)}, bf16[576,128]{1,0:T(8,128)(2,1)S(1)}, u32[]{:S(2)}, u32[]{:S(2)}) collective-permute-start(bf16[576,128]{1,0:T(8,128)(2,1)S(1)} %get-tuple-element.25), channel_id=1, source_target_pairs={{1,2},{2,1},{5,6},{6,5},{9,10},{10,9},{13,14},{14,13},{17,18},{18,... | collective-permute-start | bytes 442376 | tf_op jit(solution)/shard_map/ppermute | solution.py:555
  11.0 10.8 %copy-start = (s32[1024,16]{0,1:T(8,128)S(1)}, s32[1024,16]{0,1:T(8,128)}, u32[]{:S(2)}) copy-start(s32[1024,16]{0,1:T(8,128)} %param.9) | copy-start | bytes 196612
  11.0 26.9 %all-to-all-start = ((bf16[32,16,1024]{2,1,0:T(8,128)(2,1)}), bf16[32,16,1024]{2,1,0:T(8,128)(2,1)S(1)}, u32[]{:S(2)}, u32[]{:S(2)}) async-start(bf16[32,16,1024]{2,1,0:T(8,128)(2,1)} %shard_map.57), calls=%async_computation | async-start | bytes 2097152 | tf_op jit(solution)/shard_map/all_to_all | solution.py:603
